TPU v7x, 512 devices: a whole 4x8x8 slice. The times are simulated.
512 devices in a mesh: blk: 32 (over y_hi, x, core), chan: 16 (over z, y_lo).
Axes of the slice: x: 4, y: 8 (y_hi: 4, y_lo: 2; y = y_hi * 2 + y_lo), z: 8, core: 2. Of those that a mesh axis runs over, the one named last changes fastest.
Arguments:
- pair_repr: bfloat16 [2048, 2048, 128], P('blk', 'chan'), may hold values from -6 to 6
- chain_lengths: int32 [8], replicated, may hold values from 192 to 256
- norm_gain: float32 [128], replicated, may hold values from 0.1 to 1.9
- norm_bias: float32 [128], replicated, may hold values from -3 to 3
- left_gate: bfloat16 [128, 128], replicated, may hold values from -0.5 to 0.5
- left_value: bfloat16 [128, 128], replicated, may hold values from -0.5 to 0.5
- right_gate: bfloat16 [128, 128], replicated, may hold values from -0.5 to 0.5
- right_value: bfloat16 [128, 128], replicated, may hold values from -0.5 to 0.5
- out_gain: float32 [128], replicated, may hold values from 0.1 to 1.9
- out_bias: float32 [128], replicated, may hold values from -3 to 3
- out_weight: bfloat16 [128, 128], replicated, may hold values from -0.5 to 0.5
- gate_weight: bfloat16 [128, 128], replicated, may hold values from -0.5 to 0.5
Outputs:
- pair_update: bfloat16 [2048, 416, 128], P('blk', 'chan')
Inputs may be any that keep to these rules, and one draw needn't show every extreme that they name: Chain slot s covers residues s * 256 to (s + 1) * 256 - 1, of which the first chain_lengths[s] are real and the rest padding.
All inputs are finite; a program needn't handle non-finite values.
Results may differ from a plain program's by a relative error of at most 0.0058.
Values may be sent and summed in bfloat16 or wider, within the bound.
No kernel may reach another device: no remote copies, remote signals or barrier semaphores. Data moves between devices by JAX's collectives and lax.ppermute only.
A program may use at most 64 MiB of HBM per device.

v0:
```python
import jax
import jax.numpy as jnp
from jax import lax
from jax.sharding import PartitionSpec as P

JD = 13


epsilon = 1e-05


def normalize(values, gain_vec, bias_vec):
    centre = jnp.mean(values, axis=-1, keepdims=True)
    centred = values - centre
    spread_sq = jnp.mean(centred * centred, axis=-1, keepdims=True)
    return centred * lax.rsqrt(spread_sq + epsilon) * gain_vec + bias_vec


def residue_mask(position, lengths, slot_size):
    chain_id = position // slot_size
    chain_table = jnp.arange(lengths.shape[0], dtype=jnp.int32)
    chain_len = jnp.sum(
        jnp.where(chain_id[:, None] == chain_table[None, :], lengths[None, :], 0), axis=1
    )
    return (position % slot_size < chain_len).astype(jnp.float32)


def on_device(
    pair_repr,
    chain_lengths,
    norm_gain,
    norm_bias,
    left_gate,
    left_value,
    right_gate,
    right_value,
    out_gain,
    out_bias,
    out_weight,
    gate_weight,
):
    row_count = pair_repr.shape[0]
    col_count = pair_repr.shape[1]
    hidden = left_gate.shape[1]
    cycle_size = lax.axis_size("blk")
    cycle_index = lax.axis_index("blk")
    residues = row_count * cycle_size
    slot_size = residues // chain_lengths.shape[0]
    row_start = cycle_index * row_count
    col_start = lax.axis_index("chan") * col_count
    row_real = residue_mask(
        row_start + jnp.arange(row_count, dtype=jnp.int32), chain_lengths, slot_size
    )
    col_real = residue_mask(
        col_start + jnp.arange(col_count, dtype=jnp.int32), chain_lengths, slot_size
    )
    normed = normalize(pair_repr.astype(jnp.float32), norm_gain, norm_bias).astype(jnp.bfloat16)
    left_stack = jnp.concatenate([left_gate, left_value], axis=1)
    left_mix = jnp.einsum("ikd,de->eik", normed, left_stack, preferred_element_type=jnp.float32)
    left_proj = (
        jax.nn.sigmoid(left_mix[:hidden])
        * left_mix[hidden:]
        * (row_real[:, None] * col_real[None, :])
    ).astype(jnp.bfloat16)
    right_stack = jnp.concatenate([right_gate, right_value], axis=1)
    right_mix = jnp.einsum(
        "jkd,de->ejk", normed[:JD], right_stack, preferred_element_type=jnp.float32
    )
    right_proj = (
        jax.nn.sigmoid(right_mix[:hidden])
        * right_mix[hidden:]
        * (row_real[:JD, None] * col_real[None, :])
    ).astype(jnp.bfloat16)
    left_all, right_all = (
        lax.all_to_all(left_proj, "chan", split_axis=0, concat_axis=2, tiled=True),
        lax.all_to_all(right_proj, "chan", split_axis=0, concat_axis=2, tiled=True),
    )
    window = right_all.shape[1]
    product = jnp.einsum(
        "cik,cjk->cij",
        left_all,
        lax.all_gather(right_all, "blk", axis=1, tiled=True),
        preferred_element_type=jnp.float32,
    )
    column_slab = lax.all_to_all(
        product.astype(jnp.bfloat16), "chan", split_axis=2, concat_axis=0, tiled=True
    )
    values = column_slab.astype(jnp.float32)
    centre = jnp.mean(values, axis=0, keepdims=True)
    centred = values - centre
    spread_sq = jnp.mean(centred * centred, axis=0, keepdims=True)
    normed_product = (
        centred * lax.rsqrt(spread_sq + epsilon) * out_gain[:, None, None] + out_bias[:, None, None]
    ).astype(jnp.bfloat16)
    update = jnp.einsum(
        "cij,cd->ijd", normed_product, out_weight, preferred_element_type=jnp.float32
    )
    gate_rows = jnp.concatenate(
        [normed[:, :window], normed[:, row_count : row_count + window]], axis=1
    )
    gate_value = jax.nn.sigmoid(
        jnp.einsum("ijd,de->ije", gate_rows, gate_weight, preferred_element_type=jnp.float32)
    )
    return (gate_value * update).astype(jnp.bfloat16)


def solution(mesh):
    in_specs = (P("blk", "chan", None), P(), P(), P(), P(), P(), P(), P(), P(), P(), P(), P())
    out_specs = P("blk", "chan", None)
    return jax.shard_map(
        on_device, mesh=mesh, in_specs=in_specs, out_specs=out_specs, check_vma=False
    )
```

profile of v0, /device:TPU:1, one launch (start us, length us, event | category | flops | bytes accessed | tf_op | source)
XLA Modules:
  0.0 218.7 jit_solution(9868945080669055126)
XLA Ops:
  6.5 0.0 copy-start
  6.5 0.0 copy-start.1
  6.5 0.0 all-gather.2.cloned.1.call-start
  6.5 0.0 copy-start.8
  6.6 0.0 copy-start.9
  6.6 3.6 %convert_reduce_fusion = f32[64,128]{0,1:T(8,128)S(1)} fusion(bf16[64,128,128]{2,1,0:T(8,128)(2,1)} %param.12), kind=kLoop, calls=%fused_computation.3 | loop fusion | flops 2088960 | bytes 2129920 | tf_op jit(solution)/shard_map/reduce_sum | solution.py:13
  10.2 0.0 copy-done.1
  10.2 7.1 %fusion.4 = f32[64,128]{0,1:T(8,128)S(1)} fusion(f32[64,128]{0,1:T(8,128)S(1)} %broadcast_multiply_fusion, bf16[64,128,128]{2,1,0:T(8,128)(2,1)S(1)} %copy-done.1), kind=kLoop, calls=%fused_computation.6 | loop fusion | flops 4186112 | bytes 2162688 | tf_op jit(solution)/shard_map/reduce_sum | solution.py:15
  17.4 0.0 copy-done.11
  17.4 0.1 select_reduce_fusion
  17.5 0.1 select_reduce_fusion.1
  17.6 0.0 copy-done.8
  17.6 0.0 copy-done.9
  17.6 0.0 copy-start.4
  17.6 0.0 copy-start.5
  17.6 5.4 %fusion.7 = bf16[64,128,128]{2,0,1:T(8,128)(2,1)S(1)} fusion(f32[128]{0:T(128)S(1)} %copy-done.8, f32[128]{0:T(128)S(1)} %copy-done.9, f32[64,128]{0,1:T(8,128)S(1)} %add_rsqrt_fusion, f32[64,128]{0,1:T(8,128)S(1)} %broadcast_multiply_fusion, bf16[64,128,128]{2,1,0:T(8,128)(2,1)S(1)} %copy-done.1), kind=kLoop, calls=%fused_computation.9 | loop fusion | flops 6291456 | bytes 4260864 | tf_op jit(solution)/shard_map/convert_element_type | solution.py:57
  23.0 0.0 copy-start.2
  23.0 1.3 copy-done.2
  24.3 0.1 slice.36
  24.4 0.0 copy-done.4
  24.4 0.1 copy.59
  24.5 0.0 copy-done.5
  24.5 0.1 copy.58
  24.6 0.1 broadcast_multiply_fusion.3
  24.7 0.4 fusion.40
  25.1 0.2 fusion.29
  25.4 0.0 copy-start.6
  25.4 0.0 copy-start.7
  25.4 0.0 copy-start.3
  25.4 0.3 copy.61
  25.7 26.8 %all_to_all.45 = bf16[128,13,128]{2,1,0:T(8,128)(2,1)S(1)} all-to-all(bf16[128,13,128]{2,1,0:T(8,128)(2,1)S(1)} %copy.61), channel_id=1, replica_groups=mesh['blk'=32,'chan'=16] {'chan'}, dimensions={0} | all-to-all | bytes 851968 | tf_op jit(solution)/shard_map/all_to_all | solution.py:76
  52.5 0.3 copy.84
  52.8 0.9 all_to_all.40
  53.8 0.0 all-gather.2.cloned.1.call-update
  53.8 0.0 copy-done.6
  53.8 0.1 copy.54
  53.9 0.0 copy-done.7
  53.9 0.1 copy.53
  54.1 0.1 broadcast_multiply_fusion.1
  54.1 0.0 copy-done.3
  54.1 1.9 fusion.13
  56.0 1.2 fusion.9
  57.2 1.4 copy.56
  58.6 53.9 %all_to_all.46 = bf16[128,64,128]{2,1,0:T(8,128)(2,1)S(1)} all-to-all(bf16[128,64,128]{2,1,0:T(8,128)(2,1)S(1)} %copy.56), channel_id=1, replica_groups=mesh['blk'=32,'chan'=16] {'chan'}, dimensions={0} | all-to-all | bytes 4194304 | tf_op jit(solution)/shard_map/all_to_all | solution.py:75
  112.5 2.7 %copy.83 = bf16[16,8,64,128]{3,0,2,1:T(8,128)(2,1)} copy(bf16[16,8,64,128]{3,2,1,0:T(8,128)(2,1)S(1)} %bitcast.51) | data formatting | bytes 4194304 | tf_op jit(solution)/shard_map/all_to_all | solution.py:75
  115.2 4.2 %all_to_all.36 = bf16[8,64,2048]{2,1,0:T(8,128)(2,1)} reshape(bf16[8,64,16,128]{3,2,1,0:T(8,128)(2,1)} %bitcast.52) | data formatting | bytes 4194304 | tf_op jit(solution)/shard_map/all_to_all | solution.py:75
  119.4 46.3 %all-gather.2.cloned.1.call-done = bf16[8,416,2048]{2,0,1:T(8,128)(2,1)} async-done(((bf16[8,13,2048]{2,0,1:T(8,128)(2,1)}), bf16[8,416,2048]{2,0,1:T(8,128)(2,1)}) %all-gather.2.cloned.1.call-update) | async-done | bytes 13631504 | tf_op jit(solution)/shard_map/all_gather | solution.py:82
  165.6 20.5 %fusion.22 = bf16[8,64,416]{2,1,0:T(8,128)(2,1)S(1)} fusion(bf16[8,64,2048]{2,1,0:T(8,128)(2,1)} %all_to_all.36, bf16[8,416,2048]{2,0,1:T(8,128)(2,1)} %all-gather.2.cloned.1.call-done), kind=kOutput, calls=%fused_computation.32 | convolution fusion | flops 872628224 | bytes 16154624 | tf_op jit(solution)/shard_map/cik,cjk->cij/dot_general | solution.py:79
  186.1 0.5 copy.64
  186.6 1.3 reshape.169
  187.9 8.2 %all-to-all-start.2 = ((bf16[16,2,6656]{2,1,0:T(2,128)(2,1)}), bf16[16,2,6656]{2,1,0:T(2,128)(2,1)S(1)}, u32[]{:S(2)}, u32[]{:S(2)}) async-start(bf16[16,2,6656]{2,1,0:T(2,128)(2,1)} %reshape.169), calls=%async_computation.2 | async-start | bytes 851968 | tf_op jit(solution)/shard_map/all_to_all | solution.py:85
  196.2 0.0 copy-done
  196.2 0.4 fusion.21
  196.6 0.0 copy-start.10
  196.6 0.0 copy-start.12
  196.6 0.0 copy-start.13
  196.6 12.9 %all-to-all-done.2 = bf16[16,2,6656]{2,1,0:T(2,128)(2,1)S(1)} async-done(((bf16[16,2,6656]{2,1,0:T(2,128)(2,1)}), bf16[16,2,6656]{2,1,0:T(2,128)(2,1)S(1)}, u32[]{:S(2)}, u32[]{:S(2)}) %all-to-all-start.2) | async-done | bytes 426016 | tf_op jit(solution)/shard_map/all_to_all | solution.py:85
  209.5 0.5 reshape.170
  210.0 0.2 fusion.27
  210.3 0.3 multiply_reduce_fusion
  210.6 0.0 copy-done.10
  210.6 0.0 copy-done.12
  210.6 0.0 copy-done.13
  210.6 1.3 fusion.25
  (10 shorter events, 0.1 us)
Async XLA Ops:
  6.5 189.6 %copy-start = (bf16[128,128]{1,0:T(8,128)(2,1)S(1)}, bf16[128,128]{1,0:T(8,128)(2,1)}, u32[]{:S(2)}) copy-start(bf16[128,128]{1,0:T(8,128)(2,1)} %param.23) | copy-start | bytes 98308
  6.5 3.7 %copy-start.1 = (bf16[64,128,128]{2,1,0:T(8,128)(2,1)S(1)}, bf16[64,128,128]{2,1,0:T(8,128)(2,1)}, u32[]{:S(2)}) copy-start(bf16[64,128,128]{2,1,0:T(8,128)(2,1)} %param.12) | copy-start | bytes 6291460
  6.5 159.1 %all-gather.2.cloned.1.call-start = ((), (), s32[]{:S(2)}) async-start(), calls=%async_computation.3 | async-start | bytes 14057472 | tf_op jit(solution)/shard_map/all_gather | solution.py:82
  6.5 10.8 %copy-start.11 = (s32[8]{0:T(128)S(1)}, s32[8]{0:T(128)}, u32[]{:S(2)}) copy-start(s32[8]{0:T(128)} %param.13) | copy-start | bytes 100
  6.5 11.0 %copy-start.8 = (f32[128]{0:T(128)S(1)}, f32[128]{0:T(128)}, u32[]{:S(2)}) copy-start(f32[128]{0:T(128)} %param.15) | copy-start | bytes 1540
  6.6 11.0 %copy-start.9 = (f32[128]{0:T(128)S(1)}, f32[128]{0:T(128)}, u32[]{:S(2)}) copy-start(f32[128]{0:T(128)} %param.14) | copy-start | bytes 1540
  17.6 6.8 %copy-start.4 = (bf16[128,128]{1,0:T(8,128)(2,1)S(1)}, bf16[128,128]{1,0:T(8,128)(2,1)}, u32[]{:S(2)}) copy-start(bf16[128,128]{1,0:T(8,128)(2,1)} %param.19) | copy-start | bytes 98308
  17.6 6.9 %copy-start.5 = (bf16[128,128]{1,0:T(8,128)(2,1)S(1)}, bf16[128,128]{1,0:T(8,128)(2,1)}, u32[]{:S(2)}) copy-start(bf16[128,128]{1,0:T(8,128)(2,1)} %param.18) | copy-start | bytes 98308
  23.0 1.3 copy-start.2
  25.4 28.4 %copy-start.6 = (bf16[128,128]{1,0:T(8,128)(2,1)S(1)}, bf16[128,128]{1,0:T(8,128)(2,1)}, u32[]{:S(2)}) copy-start(bf16[128,128]{1,0:T(8,128)(2,1)} %param.17) | copy-start | bytes 98308
  25.4 28.6 %copy-start.7 = (bf16[128,128]{1,0:T(8,128)(2,1)S(1)}, bf16[128,128]{1,0:T(8,128)(2,1)}, u32[]{:S(2)}) copy-start(bf16[128,128]{1,0:T(8,128)(2,1)} %param.16) | copy-start | bytes 98308
  25.4 28.7 %copy-start.3 = (bf16[64,128,128]{2,0,1:T(8,128)(2,1)S(1)}, bf16[64,128,128]{2,0,1:T(8,128)(2,1)}, u32[]{:S(2)}) copy-start(bf16[64,128,128]{2,0,1:T(8,128)(2,1)} %copy-done.2) | copy-start | bytes 6291460
  187.9 21.6 %all-to-all-start.2 = ((bf16[16,2,6656]{2,1,0:T(2,128)(2,1)}), bf16[16,2,6656]{2,1,0:T(2,128)(2,1)S(1)}, u32[]{:S(2)}, u32[]{:S(2)}) async-start(bf16[16,2,6656]{2,1,0:T(2,128)(2,1)} %reshape.169), calls=%async_computation.2 | async-start | bytes 851968 | tf_op jit(solution)/shard_map/all_to_all | solution.py:85
  196.6 14.0 %copy-start.10 = (bf16[128,128]{1,0:T(8,128)(2,1)S(1)}, bf16[128,128]{1,0:T(8,128)(2,1)}, u32[]{:S(2)}) copy-start(bf16[128,128]{1,0:T(8,128)(2,1)} %param.22) | copy-start | bytes 98308
  196.6 14.0 %copy-start.12 = (f32[128]{0:T(128)S(1)}, f32[128]{0:T(128)}, u32[]{:S(2)}) copy-start(f32[128]{0:T(128)} %param.21) | copy-start | bytes 1540
  196.6 14.0 %copy-start.13 = (f32[128]{0:T(128)S(1)}, f32[128]{0:T(128)}, u32[]{:S(2)}) copy-start(f32[128]{0:T(128)} %param.20) | copy-start | bytes 1540
Sparse Core Ops, SparseCore 0:
  53.9 111.6 all-gather.1
where the time goes:
time: 220 us; the launch traced here: 219 us
  blocking collectives  80.7 us (37%)
  waiting for transfers between devices  59.2 us (27%)
  matrix products  24.4 us (11%)
  other arithmetic  18.5 us (8%)
  local copies, waits for them, and re-layouts  14 us (6%)
  between operations  13.8 us (6%)
  starting transfers between devices  8.22 us (4%)
    all_to_all x1, blocking collectives, on_device(): lax.all_to_all(left_proj, 'chan', split_axis=0, concat_axis=2, tiled=True)  53.9 us
    all_gather x1, waiting for transfers between devices, on_device(): lax.all_gather(right_all, 'blk', axis=1, tiled=True)  46.3 us
    all_to_all x1, blocking collectives, on_device(): lax.all_to_all(right_proj, 'chan', split_axis=0, concat_axis=2, tiled=True)  26.8 us
    dot_general x1, matrix products, on_device(): jnp.einsum('cik,cjk->cij', left_all, lax.all_gather(right_all, 'blk', axi...  20.5 us
    all_to_all x1, waiting for transfers between devices, on_device(): lax.all_to_all(product.astype(jnp.bfloat16), 'chan', split_axis=2, concat...  12.9 us
    all_to_all x1, starting transfers between devices, on_device(): lax.all_to_all(product.astype(jnp.bfloat16), 'chan', split_axis=2, concat...  8.22 us
    reduce_sum x1, other arithmetic, normalize(): spread_sq = jnp.mean(centred * centred, axis=-1, keepdims=True)  7.09 us
    all_to_all x2, local copies, waits for them, and re-layouts, on_device(): lax.all_to_all(left_proj, 'chan', split_axis=0, concat_axis=2, tiled=True)  6.9 us
  transfers between devices with their start and end apart: 2, of which 2 were waited for; matrix products, arithmetic and copies ran while one was open for 4% of the time, Pallas kernels for 0%

commit v1 on v0

v1 whole, which is shorter than its diff:
```python
import functools

import jax
import jax.numpy as jnp
from jax import lax
from jax.experimental import pallas as pl
from jax.experimental.pallas import tpu as pltpu
from jax.sharding import Mesh
from jax.sharding import PartitionSpec as P

JD = 13
PAD = 16
AXES = (("yh", 4), ("x", 4), ("core", 2), ("z", 8), ("yl", 2))
SPREAD = ("x", "core", "z", "yl")

epsilon = 1e-05

dot = functools.partial(lax.dot_general, preferred_element_type=jnp.float32)


def normalize(values, gain_vec, bias_vec):
    centre = jnp.mean(values, axis=-1, keepdims=True)
    centred = values - centre
    spread_sq = jnp.mean(centred * centred, axis=-1, keepdims=True)
    return centred * lax.rsqrt(spread_sq + epsilon) * gain_vec + bias_vec


def place():
    blk = (lax.axis_index("yh") * 4 + lax.axis_index("x")) * 2 + lax.axis_index("core")
    chan = lax.axis_index("z") * 2 + lax.axis_index("yl")
    return blk, chan


def real_left(lengths, start, slot_size):
    return lengths[start // slot_size] - start % slot_size


def project_kernel(
    limit, slot_size, where, lengths, pair, gain, bias, gate_w, value_w, out, stack, planes
):
    rows, cols, _ = pair.shape
    hidden = gate_w.shape[1]
    step = pl.program_id(0)
    blk, chan = where()

    @pl.when(step == 0)
    def _():
        stack[:hidden] = (gate_w[...].astype(jnp.float32) * 0.5).T.astype(jnp.bfloat16)
        stack[hidden:] = value_w[...].astype(jnp.float32).T.astype(jnp.bfloat16)

    row_count = real_left(lengths, blk * limit, slot_size) - step * rows
    col_count = real_left(lengths, chan * cols, slot_size)
    col_ids = lax.broadcasted_iota(jnp.int32, (1, cols), 1)

    def body(i, carry):
        normed = normalize(pair[i].astype(jnp.float32), gain[...], bias[...])
        mix = dot(stack[...], normed.astype(jnp.bfloat16), (((1,), (1,)), ((), ())))
        kept = jnp.where(i < row_count, col_count, 0)
        mask = jnp.where(col_ids < kept, 0.5, 0.0)
        gated = (jnp.tanh(mix[:hidden]) + 1.0) * (mix[hidden:] * mask)
        planes[pl.ds(i, hidden, stride=rows), :] = gated
        return carry

    lax.fori_loop(0, rows, body, 0, unroll=2)
    out[...] = planes[...].reshape(hidden, rows, cols).astype(jnp.bfloat16)


def project(pair, lengths, gain, bias, gate_w, value_w, row_blocks, slot_size, where=place):
    rows, cols, width = pair.shape
    hidden = gate_w.shape[1]
    whole = pl.BlockSpec((width, hidden), lambda b: (0, 0))
    vec = pl.BlockSpec((1, width), lambda b: (0, 0))
    return pl.pallas_call(
        functools.partial(project_kernel, rows, slot_size, where),
        grid=(row_blocks,),
        in_specs=[
            pl.BlockSpec(memory_space=pltpu.SMEM),
            pl.BlockSpec((PAD, cols, width), lambda b: (b, 0, 0)),
            vec,
            vec,
            whole,
            whole,
        ],
        out_specs=pl.BlockSpec((hidden, PAD, cols), lambda b: (0, b, 0)),
        out_shape=jax.ShapeDtypeStruct((hidden, PAD * row_blocks, cols), jnp.bfloat16),
        scratch_shapes=[
            pltpu.VMEM((2 * hidden, width), jnp.bfloat16),
            pltpu.VMEM((hidden * PAD, cols), jnp.float32),
        ],
        compiler_params=pltpu.CompilerParams(vmem_limit_bytes=32 << 20),
    )(lengths, pair, gain, bias, gate_w, value_w)


def product_kernel(left, right, out, left_mat, right_mat):
    groups, chans, rows, cols = left.shape
    blks = right.shape[0]
    for c in range(chans):
        span = pl.ds(c * cols, cols)
        left_mat[:, span] = left[:, c].reshape(groups * rows, cols)
        right_mat[:, span] = right[:, c].reshape(blks * PAD, cols)
    low = lax.broadcasted_iota(jnp.int32, (PAD, 2 * rows), 1) < rows
    pieces = 4
    part = blks // pieces
    for p in range(pieces):
        prod = dot(
            right_mat[p * part * PAD : (p + 1) * part * PAD],
            left_mat[...],
            (((1,), (1,)), ((), ())),
        )
        for q in range(part // 2):
            c = p * part // 2 + q
            for g in range(0, groups, 2):
                span = slice(g * rows, (g + 2) * rows)
                first = prod[2 * q * PAD : (2 * q + 1) * PAD, span]
                second = prod[(2 * q + 1) * PAD : (2 * q + 2) * PAD, span]
                out[g, c] = jnp.where(low, first, pltpu.roll(second, rows, 1)).astype(
                    jnp.bfloat16
                )
                out[g + 1, c] = jnp.where(low, pltpu.roll(first, rows, 1), second).astype(
                    jnp.bfloat16
                )


def product_of(left, right):
    groups, chans, rows, cols = left.shape
    blks = right.shape[0]
    return pl.pallas_call(
        product_kernel,
        out_shape=jax.ShapeDtypeStruct((groups, chans, PAD, 2 * rows), jnp.bfloat16),
        scratch_shapes=[
            pltpu.VMEM((groups * rows, chans * cols), jnp.bfloat16),
            pltpu.VMEM((blks * PAD, chans * cols), jnp.bfloat16),
        ],
        compiler_params=pltpu.CompilerParams(vmem_limit_bytes=48 << 20),
    )(left, right)


def update_kernel(
    out_gain,
    out_bias,
    slab,
    pair_a,
    pair_b,
    gain,
    bias,
    gate_w,
    out_w,
    out,
    normed_s,
    gate_s,
    out_s,
):
    hidden = slab.shape[0]
    rows, _, width = pair_a.shape
    for h, pair in enumerate((pair_a, pair_b)):
        flat = pair[...].reshape(rows * PAD, width).astype(jnp.float32)
        normed = normalize(flat, gain[...], bias[...]).astype(jnp.bfloat16)
        gate_s[h] = jax.nn.sigmoid(dot(normed, gate_w[...], (((1,), (0,)), ((), ()))))

    total = lax.fori_loop(
        0,
        hidden,
        lambda c, acc: acc + slab[c].astype(jnp.float32),
        jnp.zeros(slab.shape[1:], jnp.float32),
        unroll=8,
    )
    centre = total * (1.0 / hidden)

    def square(c, acc):
        centred = slab[c].astype(jnp.float32) - centre
        return acc + centred * centred

    squares = lax.fori_loop(0, hidden, square, jnp.zeros_like(centre), unroll=8)
    inv = lax.rsqrt(squares * (1.0 / hidden) + epsilon)

    def finish(c, carry):
        centred = slab[c].astype(jnp.float32) - centre
        normed_s[pl.ds(pl.multiple_of(c * PAD, PAD), PAD), :] = (
            centred * inv * out_gain[c] + out_bias[c]
        )
        return carry

    lax.fori_loop(0, hidden, finish, 0, unroll=8)
    span = 2 * PAD
    for r in range(JD):
        normed = normed_s[pl.ds(r, hidden, stride=PAD), :].astype(jnp.bfloat16)
        update = dot(normed, out_w[...], (((0,), (0,)), ((), ())))
        for h in range(2):
            gate = gate_s[h, pl.ds(r, rows, stride=PAD), :]
            out_s[pl.ds(h * JD + r, rows, stride=span), :] = (
                gate * update[h * rows : (h + 1) * rows]
            )
    whole = out_s[...].reshape(rows, span, width)
    out[...] = whole[:, : 2 * JD].astype(jnp.bfloat16)


def update_of(slab, pair, gain, bias, gate_w, out_gain, out_bias, out_w):
    rows, cols, width = pair.shape
    hidden = slab.shape[0]
    smem = pl.BlockSpec(memory_space=pltpu.SMEM)
    half = cols // 2 // PAD
    vec = pl.BlockSpec((1, width), lambda b: (0, 0))
    mat = pl.BlockSpec((width, width), lambda b: (0, 0))
    return pl.pallas_call(
        update_kernel,
        grid=(1,),
        in_specs=[
            smem,
            smem,
            pl.BlockSpec(slab.shape, lambda b: (0, 0, 0)),
            pl.BlockSpec((rows, PAD, width), lambda b: (0, 0, 0)),
            pl.BlockSpec((rows, PAD, width), lambda b: (0, half, 0)),
            vec,
            vec,
            mat,
            mat,
        ],
        out_specs=pl.BlockSpec((rows, 2 * JD, width), lambda b: (0, 0, 0)),
        out_shape=jax.ShapeDtypeStruct((rows, 2 * JD, width), jnp.bfloat16),
        scratch_shapes=[
            pltpu.VMEM((hidden * PAD, slab.shape[2]), jnp.float32),
            pltpu.VMEM((2, rows * PAD, width), jnp.float32),
            pltpu.VMEM((rows * 2 * PAD, width), jnp.float32),
        ],
        compiler_params=pltpu.CompilerParams(vmem_limit_bytes=32 << 20),
    )(out_gain, out_bias, slab, pair, pair, gain, bias, gate_w, out_w)


def on_device(
    pair_repr,
    chain_lengths,
    norm_gain,
    norm_bias,
    left_gate,
    left_value,
    right_gate,
    right_value,
    out_gain,
    out_bias,
    out_weight,
    gate_weight,
):
    rows, cols, width = pair_repr.shape
    groups = lax.axis_size("x") * lax.axis_size("core")
    chans = lax.axis_size("z") * lax.axis_size("yl")
    residues = rows * groups * lax.axis_size("yh")
    slot_size = residues // chain_lengths.shape[0]
    gain = norm_gain.reshape(1, width)
    bias = norm_bias.reshape(1, width)
    right = project(
        pair_repr, chain_lengths, gain, bias, right_gate, right_value, 1, slot_size
    )
    right = lax.all_to_all(right, SPREAD, 0, 0, tiled=True)
    pair_repr, right = lax.optimization_barrier((pair_repr, right))
    right = lax.all_gather(right, "yh", axis=0, tiled=True)
    left = project(
        pair_repr, chain_lengths, gain, bias, left_gate, left_value, rows // PAD, slot_size
    )
    left = lax.all_to_all(left, SPREAD, 0, 0, tiled=True)
    product = product_of(
        left.reshape(groups, chans, rows, cols), right.reshape(-1, chans, PAD, cols)
    )
    slab = lax.all_to_all(
        product.reshape(groups * chans, PAD, 2 * rows), SPREAD, 0, 0, tiled=True
    )
    return update_of(
        slab, pair_repr, gain, bias, gate_weight, out_gain, out_bias, out_weight
    )


def solution(mesh):
    names = tuple(name for name, _ in AXES)
    sizes = tuple(size for _, size in AXES)
    fine = Mesh(mesh.devices.reshape(sizes), names)
    split = P(names[:3], names[3:], None)
    return jax.shard_map(
        on_device,
        mesh=fine,
        in_specs=(split,) + (P(),) * 11,
        out_specs=split,
        check_vma=False,
    )
```

time: 220 us -> 183 us (0.83)
  Pallas kernels: 0 us -> 26.2 us
  matrix products: 24.4 us -> 0 us
  other arithmetic: 18.5 us -> 0 us
  blocking collectives: 80.7 us -> 66 us
  local copies, waits for them, and re-layouts: 14 us -> 8.96 us
    pallas_call x0 -> x4, Pallas kernels: none -> 26.2 us  [the longest x2 18.3 us: project(): pl.pallas_call(functools.partial(project_kernel, rows, slot_size, where),...]
    dot_general x5 -> x0, matrix products: 24.4 us -> none  [the longest x1 20.5 us: on_device(): jnp.einsum('cik,cjk->cij', left_all, lax.all_gather(right_all, 'blk', axi...]
    all_to_all x2, blocking collectives: 80.7 us -> 66 us  [the longest x1 35.3 us: on_device(): right = lax.all_to_all(right, SPREAD, 0, 0, tiled=True)]
    all_gather x1, waiting for transfers between devices: 46.3 us -> 60.6 us  [on_device(): right = lax.all_gather(right, 'yh', axis=0, tiled=True)]
    all_to_all x1, waiting for transfers between devices: 12.9 us -> 0.01 us  [on_device(): left = lax.all_to_all(left, SPREAD, 0, 0, tiled=True)]
    reduce_sum x6 -> x0, other arithmetic: 11.4 us -> none  [the longest x1 7.09 us: normalize(): spread_sq = jnp.mean(centred * centred, axis=-1, keepdims=True)]
    all_to_all x4 -> x0, local copies, waits for them, and re-layouts: 8.14 us -> none  [the longest x2 6.9 us: on_device(): lax.all_to_all(left_proj, 'chan', split_axis=0, concat_axis=2, tiled=True)]
    convert_element_type x5 -> x0, other arithmetic: 6.88 us -> none  [the longest x1 5.38 us: on_device(): normalize(pair_repr.astype(jnp.float32), norm_gain, norm_bias)]
  transfers between devices with their start and end apart: 2 -> 2, of which waited for: 2 -> 1; matrix products, arithmetic and copies ran while one was open for 4% -> 0% of each run, Pallas kernels for 0% -> 0%
where the time goes in v1:
time: 183 us
  blocking collectives  66 us (36%)
  waiting for transfers between devices  61.3 us (33%)
  Pallas kernels  26.2 us (14%)
  between operations  13.5 us (7%)
  local copies, waits for them, and re-layouts  8.96 us (5%)
  starting transfers between devices  6.96 us (4%)
    all_gather x1, waiting for transfers between devices, on_device(): right = lax.all_gather(right, 'yh', axis=0, tiled=True)  60.6 us
    all_to_all x1, blocking collectives, on_device(): right = lax.all_to_all(right, SPREAD, 0, 0, tiled=True)  35.3 us
    all_to_all x1, blocking collectives, on_device(): lax.all_to_all(product.reshape(groups * chans, PAD, 2 * rows), SPREAD, 0,...  30.7 us
    pallas_call x2, Pallas kernels, project(): pl.pallas_call(functools.partial(project_kernel, rows, slot_size, where),...  18.3 us
    unnamed x36, local copies, waits for them, and re-layouts  8.03 us
    all_to_all x1, starting transfers between devices, on_device(): left = lax.all_to_all(left, SPREAD, 0, 0, tiled=True)  6.92 us
    pallas_call x1, Pallas kernels, product_of(): pl.pallas_call(product_kernel, out_shape=jax.ShapeDtypeStruct((groups, ch...  4.71 us
  transfers between devices with their start and end apart: 2, of which 1 were waited for; matrix products, arithmetic and copies ran while one was open for 0% of the time, Pallas kernels for 0%

profile of v1, /device:TPU:1, one launch (start us, length us, event | category | flops | bytes accessed | tf_op | source)
XLA Modules:
  0.0 182.9 jit_solution(15579675852653654840)
XLA Ops:
  6.5 0.0 copy-start.11
  6.5 0.0 copy-start.13
  6.5 0.0 copy-start.15
  6.5 0.0 copy-start
  6.5 1.6 copy-done
  8.2 0.0 copy-start.4
  8.2 0.8 copy-done.4
  8.9 0.0 copy-start.5
  8.9 0.8 copy-done.5
  9.7 0.0 copy-start.10
  9.7 0.7 copy-done.10
  10.3 0.0 copy-start.12
  10.3 0.7 copy-done.12
  11.0 0.0 copy-start.14
  11.0 0.7 copy-done.14
  11.7 0.0 copy-start.1
  11.7 0.0 copy-start.6
  11.7 0.0 copy-start.7
  11.7 3.9 %shard_map.118 = bf16[128,16,128]{2,1,0:T(8,128)(2,1)S(1)} custom-call(s32[8]{0:T(128)S(1)} %copy-done.14, bf16[64,128,128]{2,1,0:T(8,128)(2,1)S(1)} %copy-done, f32[1,128]{1,0:T(1,128)S(1)} %bitcast.7, f32[1,128]{1,0:T(1,128)S(1)} %bitcast.10, bf16[128,128]{1,0:T(8,128)(2,1)S(1)} %copy-done.4, bf16[128,128]{1,0:T(8,128)(2,1)S(1)} %copy-done.5), custom_call_target="tpu_custom_call" | custom-call | tf_op jit(solution)/shard_map/pallas_call | solution.py:73
  15.6 35.3 %all_to_all.15 = bf16[128,16,128]{2,1,0:T(8,128)(2,1)} all-to-all(bf16[128,16,128]{2,1,0:T(8,128)(2,1)S(1)} %shard_map.118), channel_id=1, replica_groups=mesh['yh'=4,'x'=4,'core'=2,'z'=8,'yl'=2] {'x','core','z','yl'}, dimensions={0} | all-to-all | bytes 1048576 | tf_op jit(solution)/shard_map/all_to_all | solution.py:253
  50.9 0.0 copy-done.11
  50.9 0.0 copy-done.13
  50.9 0.0 copy-done.15
  50.9 0.0 copy-done.1
  50.9 0.0 copy-done.6
  50.9 0.0 copy-done.7
  51.0 14.3 %shard_map.119 = bf16[128,64,128]{2,1,0:T(8,128)(2,1)S(1)} custom-call(s32[8]{0:T(128)S(1)} %copy-done.15, bf16[64,128,128]{2,1,0:T(8,128)(2,1)S(1)} %copy-done.1, f32[1,128]{1,0:T(1,128)S(1)} %bitcast.8, f32[1,128]{1,0:T(1,128)S(1)} %bitcast.11, bf16[128,128]{1,0:T(8,128)(2,1)S(1)} %copy-done.6, bf16[128,128]{1,0:T(8,128)(2,1)S(1)} %copy-done.7), custom_call_target="tpu_custom_call" | custom-call | tf_op jit(solution)/shard_map/pallas_call | solution.py:73
  65.3 0.0 copy-start.2
  65.3 1.3 copy-done.2
  66.6 6.9 %all-to-all-start.1 = ((bf16[128,64,128]{2,1,0:T(8,128)(2,1)}), bf16[128,64,128]{2,1,0:T(8,128)(2,1)}, u32[]{:S(2)}, u32[]{:S(2)}) async-start(bf16[128,64,128]{2,1,0:T(8,128)(2,1)} %copy-done.2), calls=%async_computation.1 | async-start | bytes 4194304 | tf_op jit(solution)/shard_map/all_to_all | solution.py:259
  73.5 0.0 all-gather.2.cloned.1.call-start
  73.6 0.7 all-gather.2.cloned.1.call-update
  74.2 60.6 %all-gather.2.cloned.1.call-done = bf16[512,16,128]{2,1,0:T(8,128)(2,1)} async-done(((bf16[128,16,128]{2,1,0:T(8,128)(2,1)}), bf16[512,16,128]{2,1,0:T(8,128)(2,1)}) %all-gather.2.cloned.1.call-update) | async-done | bytes 2097168 | tf_op jit(solution)/shard_map/all_gather | solution.py:255
  134.8 0.0 all-to-all-done.1
  134.9 0.0 copy-start.3
  134.9 1.6 copy-done.3
  136.4 0.0 copy-start.8
  136.4 0.0 copy-start.9
  136.4 0.0 copy-start.16
  136.5 0.0 copy-start.17
  136.5 4.7 %shard_map.120 = bf16[8,16,16,128]{3,2,1,0:T(8,128)(2,1)S(1)} custom-call(bf16[8,16,64,128]{3,2,1,0:T(8,128)(2,1)} %bitcast.2.left, bf16[32,16,16,128]{3,2,1,0:T(8,128)(2,1)S(1)} %bitcast.6), custom_call_target="tpu_custom_call" | custom-call | tf_op jit(solution)/shard_map/pallas_call | solution.py:127
  141.2 30.7 %all_to_all.16.slab = bf16[128,16,128]{2,1,0:T(8,128)(2,1)S(1)} all-to-all(bf16[128,16,128]{2,1,0:T(8,128)(2,1)S(1)} %bitcast.5), channel_id=1, replica_groups=mesh['yh'=4,'x'=4,'core'=2,'z'=8,'yl'=2] {'x','core','z','yl'}, dimensions={0} | all-to-all | bytes 1048576 | tf_op jit(solution)/shard_map/all_to_all | solution.py:263
  171.9 0.0 copy-done.8
  171.9 0.0 copy-done.9
  171.9 0.0 copy-done.16
  171.9 0.0 copy-done.17
  171.9 3.3 %shard_map.121 = bf16[64,26,128]{2,1,0:T(8,128)(2,1)S(1)} custom-call(f32[128]{0:T(128)S(1)} %copy-done.16, f32[128]{0:T(128)S(1)} %copy-done.17, bf16[128,16,128]{2,1,0:T(8,128)(2,1)S(1)} %all_to_all.16.slab, bf16[64,128,128]{2,1,0:T(8,128)(2,1)S(1)} %copy-done.1, bf16[64,128,128]{2,1,0:T(8,128)(2,1)S(1)} %copy-done.1, f32[1,128]{1,0:T(1,128)S(1)} %bitcast.9, ...), custom_call_target="tpu_custom_call" | custom-call | tf_op jit(solution)/shard_map/pallas_call | solution.py:204
  175.2 0.9 copy.14
Async XLA Ops:
  6.5 44.4 %copy-start.11 = (f32[128]{0:T(128)S(1)}, f32[128]{0:T(128)}, u32[]{:S(2)}) copy-start(f32[128]{0:T(128)} %param.14) | copy-start | bytes 1540
  6.5 44.4 %copy-start.13 = (f32[128]{0:T(128)S(1)}, f32[128]{0:T(128)}, u32[]{:S(2)}) copy-start(f32[128]{0:T(128)} %param.15) | copy-start | bytes 1540
  6.5 44.4 %copy-start.15 = (s32[8]{0:T(128)S(1)}, s32[8]{0:T(128)}, u32[]{:S(2)}) copy-start(s32[8]{0:T(128)} %lengths.3) | copy-start | bytes 100
  6.5 1.6 copy-start
  8.2 0.8 copy-start.4
  8.9 0.8 copy-start.5
  9.7 0.7 copy-start.10
  10.3 0.7 copy-start.12
  11.0 0.7 copy-start.14
  11.7 39.3 %copy-start.1 = (bf16[64,128,128]{2,1,0:T(8,128)(2,1)S(1)}, bf16[64,128,128]{2,1,0:T(8,128)(2,1)}, u32[]{:S(2)}) copy-start(bf16[64,128,128]{2,1,0:T(8,128)(2,1)} %pair_b) | copy-start | bytes 6291460
  11.7 39.3 %copy-start.6 = (bf16[128,128]{1,0:T(8,128)(2,1)S(1)}, bf16[128,128]{1,0:T(8,128)(2,1)}, u32[]{:S(2)}) copy-start(bf16[128,128]{1,0:T(8,128)(2,1)} %gate_w.4) | copy-start | bytes 98308
  11.7 39.3 %copy-start.7 = (bf16[128,128]{1,0:T(8,128)(2,1)S(1)}, bf16[128,128]{1,0:T(8,128)(2,1)}, u32[]{:S(2)}) copy-start(bf16[128,128]{1,0:T(8,128)(2,1)} %value_w.3) | copy-start | bytes 98308
  65.3 1.3 copy-start.2
  66.6 68.3 %all-to-all-start.1 = ((bf16[128,64,128]{2,1,0:T(8,128)(2,1)}), bf16[128,64,128]{2,1,0:T(8,128)(2,1)}, u32[]{:S(2)}, u32[]{:S(2)}) async-start(bf16[128,64,128]{2,1,0:T(8,128)(2,1)} %copy-done.2), calls=%async_computation.1 | async-start | bytes 4194304 | tf_op jit(solution)/shard_map/all_to_all | solution.py:259
  73.5 61.3 %all-gather.2.cloned.1.call-start = ((), (), s32[]{:S(2)}) async-start(), calls=%async_computation.3 | async-start | bytes 2621440 | tf_op jit(solution)/shard_map/all_gather | solution.py:255
  134.9 1.6 copy-start.3
  136.4 35.4 %copy-start.8 = (bf16[128,128]{1,0:T(8,128)(2,1)S(1)}, bf16[128,128]{1,0:T(8,128)(2,1)}, u32[]{:S(2)}) copy-start(bf16[128,128]{1,0:T(8,128)(2,1)} %gate_w.5) | copy-start | bytes 98308
  136.4 35.4 %copy-start.9 = (bf16[128,128]{1,0:T(8,128)(2,1)S(1)}, bf16[128,128]{1,0:T(8,128)(2,1)}, u32[]{:S(2)}) copy-start(bf16[128,128]{1,0:T(8,128)(2,1)} %out_w.1) | copy-start | bytes 98308
  136.4 35.4 %copy-start.16 = (f32[128]{0:T(128)S(1)}, f32[128]{0:T(128)}, u32[]{:S(2)}) copy-start(f32[128]{0:T(128)} %out_gain.1) | copy-start | bytes 1540
  136.5 35.4 %copy-start.17 = (f32[128]{0:T(128)S(1)}, f32[128]{0:T(128)}, u32[]{:S(2)}) copy-start(f32[128]{0:T(128)} %out_bias.1) | copy-start | bytes 1540
Sparse Core Ops, SparseCore 0:
  76.4 58.3 all-gather.1

commit v2 on v1

v2 whole, which is shorter than its diff:
```python
import functools

import jax
import jax.numpy as jnp
from jax import lax
from jax.experimental import pallas as pl
from jax.experimental.pallas import tpu as pltpu
from jax.sharding import Mesh
from jax.sharding import PartitionSpec as P

JD = 13
PAD = 16
BATCH = 4
AXES = (("yh", 4), ("x", 4), ("core", 2), ("z", 8), ("yl", 2))
SPREAD = ("x", "core", "z", "yl")

epsilon = 1e-05

dot = functools.partial(lax.dot_general, preferred_element_type=jnp.float32)


def normalize(values, gain_vec, bias_vec):
    centre = jnp.mean(values, axis=-1, keepdims=True)
    centred = values - centre
    spread_sq = jnp.mean(centred * centred, axis=-1, keepdims=True)
    return centred * lax.rsqrt(spread_sq + epsilon) * gain_vec + bias_vec


def place():
    blk = (lax.axis_index("yh") * 4 + lax.axis_index("x")) * 2 + lax.axis_index("core")
    chan = lax.axis_index("z") * 2 + lax.axis_index("yl")
    return blk, chan


def real_left(lengths, start, slot_size):
    return lengths[start // slot_size] - start % slot_size


def prepare(gain, bias, gate_w, value_w, stack, scale, shift):
    width, hidden = gate_w.shape
    stack[:hidden] = (gate_w[...].astype(jnp.float32) * 0.5).T.astype(jnp.bfloat16)
    stack[hidden:] = value_w[...].astype(jnp.float32).T.astype(jnp.bfloat16)
    scale[...] = jnp.broadcast_to(gain[...], scale.shape).T
    shift[...] = jnp.broadcast_to(bias[...], shift.shape).T


def project_rows(pair, row_count, col_count, stack, scale, shift, planes, out):
    rows, cols, width = pair.shape
    hidden = stack.shape[0] // 2
    col_ids = lax.broadcasted_iota(jnp.int32, (1, cols), 1)
    scale_all = jnp.concatenate([scale[...]] * BATCH, axis=1)
    shift_all = jnp.concatenate([shift[...]] * BATCH, axis=1)
    for start in range(0, rows, BATCH):
        flat = pair[start : start + BATCH].reshape(BATCH * cols, width)
        values = flat.T.astype(jnp.float32)
        centre = jnp.mean(values, axis=0, keepdims=True)
        centred = values - centre
        spread_sq = jnp.mean(centred * centred, axis=0, keepdims=True)
        normed = centred * lax.rsqrt(spread_sq + epsilon) * scale_all + shift_all
        mix = dot(stack[...], normed.astype(jnp.bfloat16), (((1,), (0,)), ((), ())))
        gated = (jnp.tanh(mix[:hidden]) + 1.0) * mix[hidden:]
        for j in range(BATCH):
            i = start + j
            kept = jnp.where(i < row_count, col_count, 0)
            mask = jnp.where(col_ids < kept, 0.5, 0.0)
            planes[pl.ds(i, hidden, stride=rows), :] = gated[:, j * cols : (j + 1) * cols] * mask
    out[...] = planes[...].reshape(hidden, rows, cols).astype(jnp.bfloat16)


def in_hbm(*arrays):
    return [pltpu.with_memory_space_constraint(array, pltpu.HBM) for array in arrays]


def fetch(sems, *copies):
    started = [pltpu.make_async_copy(a, b, sems.at[n]) for n, (a, b) in enumerate(copies)]
    for copy in started:
        copy.start()
    return started


def right_kernel(
    limit,
    slot_size,
    where,
    lengths_h,
    pair_h,
    gain_h,
    bias_h,
    gate_h,
    value_h,
    out,
    lengths,
    pair,
    gain,
    bias,
    gate_w,
    value_w,
    stack,
    scale,
    shift,
    planes,
    sems,
):
    copies = fetch(
        sems,
        (gate_h, gate_w),
        (value_h, value_w),
        (gain_h, gain),
        (bias_h, bias),
        (lengths_h, lengths),
        (pair_h.at[pl.ds(0, PAD)], pair),
    )
    for copy in copies:
        copy.wait()
    blk, chan = where()
    prepare(gain, bias, gate_w, value_w, stack, scale, shift)
    row_count = real_left(lengths, blk * limit, slot_size)
    col_count = real_left(lengths, chan * pair.shape[1], slot_size)
    project_rows(pair, row_count, col_count, stack, scale, shift, planes, out)


def shared_scratch(width, hidden, cols):
    return [
        pltpu.VMEM((2 * hidden, width), jnp.bfloat16),
        pltpu.VMEM((width, cols), jnp.float32),
        pltpu.VMEM((width, cols), jnp.float32),
        pltpu.VMEM((hidden * PAD, cols), jnp.float32),
    ]


def project_right(pair, lengths, gain, bias, gate_w, value_w, slot_size, where=place):
    rows, cols, width = pair.shape
    hidden = gate_w.shape[1]
    return pl.pallas_call(
        functools.partial(right_kernel, rows, slot_size, where),
        in_specs=[pl.BlockSpec(memory_space=pltpu.HBM)] * 6,
        out_specs=pl.BlockSpec((hidden, PAD, cols), lambda: (0, 0, 0)),
        out_shape=jax.ShapeDtypeStruct((hidden, PAD, cols), jnp.bfloat16),
        scratch_shapes=[
            pltpu.SMEM(lengths.shape, jnp.int32),
            pltpu.VMEM((PAD, cols, width), jnp.bfloat16),
            pltpu.VMEM((1, width), jnp.float32),
            pltpu.VMEM((1, width), jnp.float32),
            pltpu.VMEM((width, hidden), jnp.bfloat16),
            pltpu.VMEM((width, hidden), jnp.bfloat16),
            *shared_scratch(width, hidden, cols),
            pltpu.SemaphoreType.DMA((6,)),
        ],
        compiler_params=pltpu.CompilerParams(vmem_limit_bytes=32 << 20),
    )(*in_hbm(lengths, pair, gain, bias, gate_w, value_w))


def left_kernel(
    limit, slot_size, where, lengths, pair, gain, bias, gate_w, value_w, out, stack, scale, shift, planes
):
    step = pl.program_id(0)
    blk, chan = where()

    @pl.when(step == 0)
    def _():
        prepare(gain, bias, gate_w, value_w, stack, scale, shift)

    row_count = real_left(lengths, blk * limit, slot_size) - step * PAD
    col_count = real_left(lengths, chan * pair.shape[1], slot_size)
    project_rows(pair, row_count, col_count, stack, scale, shift, planes, out)


def project_left(pair, lengths, gain, bias, gate_w, value_w, slot_size, where=place):
    rows, cols, width = pair.shape
    hidden = gate_w.shape[1]
    whole = pl.BlockSpec((width, hidden), lambda b: (0, 0))
    vec = pl.BlockSpec((1, width), lambda b: (0, 0))
    return pl.pallas_call(
        functools.partial(left_kernel, rows, slot_size, where),
        grid=(rows // PAD,),
        in_specs=[
            pl.BlockSpec(memory_space=pltpu.SMEM),
            pl.BlockSpec((PAD, cols, width), lambda b: (b, 0, 0)),
            vec,
            vec,
            whole,
            whole,
        ],
        out_specs=pl.BlockSpec((hidden, PAD, cols), lambda b: (0, b, 0)),
        out_shape=pltpu.HBM((hidden, rows, cols), jnp.bfloat16),
        scratch_shapes=shared_scratch(width, hidden, cols),
        cost_estimate=pl.CostEstimate(
            flops=4 * rows * cols * width * hidden,
            bytes_accessed=4 * rows * cols * width,
            transcendentals=rows * cols * hidden,
        ),
        compiler_params=pltpu.CompilerParams(vmem_limit_bytes=32 << 20),
    )(lengths, pair, gain, bias, gate_w, value_w)


def product_kernel(ring, where, *refs):
    left_h, rights_h = refs[0], refs[1 : 1 + ring]
    out, left_mat, right_mat, acc, sems = refs[1 + ring :]
    groups, chans, rows, cols = left_h.shape
    me = where()
    copies = []
    for c in range(chans):
        span = pl.ds(c * cols, cols)
        pairs = [(left_h.at[:, c], left_mat.at[:, :, span])]
        pairs += [
            (right.at[:, c], right_mat.at[pl.ds(d * groups, groups), :, span])
            for d, right in enumerate(rights_h)
        ]
        copies.append(fetch(sems.at[c], *pairs))
    size = 4
    for first in range(0, chans, size):
        for c in range(first, first + size):
            for copy in copies[c]:
                copy.wait()
        span = slice(first * cols, (first + size) * cols)
        part = dot(
            right_mat[:, :, span].reshape(ring * groups * PAD, size * cols),
            left_mat[:, :, span].reshape(groups * rows, size * cols),
            (((1,), (1,)), ((), ())),
        )
        if first == 0:
            acc[...] = part
        else:
            acc[...] += part
    low = lax.broadcasted_iota(jnp.int32, (PAD, 2 * rows), 1) < rows
    half = groups // 2
    for d in range(ring):
        base = lax.rem(me + ring - d, ring) * half
        for q in range(half):
            top = (d * groups + 2 * q) * PAD
            for g in range(0, groups, 2):
                span = slice(g * rows, (g + 2) * rows)
                first = acc[top : top + PAD, span]
                second = acc[top + PAD : top + 2 * PAD, span]
                out[g, base + q] = jnp.where(low, first, pltpu.roll(second, rows, 1)).astype(
                    jnp.bfloat16
                )
                out[g + 1, base + q] = jnp.where(
                    low, pltpu.roll(first, rows, 1), second
                ).astype(jnp.bfloat16)


def product_of(left, rights, where=lambda: lax.axis_index("yh")):
    groups, chans, rows, cols = left.shape
    ring = len(rights)
    hbm = pl.BlockSpec(memory_space=pltpu.HBM)
    return pl.pallas_call(
        functools.partial(product_kernel, ring, where),
        in_specs=[hbm] * (1 + ring),
        out_shape=jax.ShapeDtypeStruct((groups, chans, PAD, 2 * rows), jnp.bfloat16),
        scratch_shapes=[
            pltpu.VMEM((groups, rows, chans * cols), jnp.bfloat16),
            pltpu.VMEM((ring * groups, PAD, chans * cols), jnp.bfloat16),
            pltpu.VMEM((ring * groups * PAD, groups * rows), jnp.float32),
            pltpu.SemaphoreType.DMA((chans, 1 + ring)),
        ],
        compiler_params=pltpu.CompilerParams(vmem_limit_bytes=48 << 20),
    )(*in_hbm(left, *rights))


def gate_kernel(pair_a, pair_b, gain, bias, gate_w, out, gate_s):
    rows, _, width = pair_a.shape
    for h, pair in enumerate((pair_a, pair_b)):
        flat = pair[...].reshape(rows * PAD, width).astype(jnp.float32)
        normed = normalize(flat, gain[...], bias[...]).astype(jnp.bfloat16)
        gate_s[h] = jax.nn.sigmoid(dot(normed, gate_w[...], (((1,), (0,)), ((), ()))))
        for r in range(JD):
            out[h * JD + r] = gate_s[h, pl.ds(r, rows, stride=PAD), :]


def gate_of(pair, gain, bias, gate_w):
    rows, cols, width = pair.shape
    half = cols // 2 // PAD
    vec = pl.BlockSpec((1, width), lambda b: (0, 0))
    mat = pl.BlockSpec((width, width), lambda b: (0, 0))
    return pl.pallas_call(
        gate_kernel,
        grid=(1,),
        in_specs=[
            pl.BlockSpec((rows, PAD, width), lambda b: (0, 0, 0)),
            pl.BlockSpec((rows, PAD, width), lambda b: (0, half, 0)),
            vec,
            vec,
            mat,
        ],
        out_specs=pl.BlockSpec((2 * JD, rows, width), lambda b: (0, 0, 0)),
        out_shape=jax.ShapeDtypeStruct((2 * JD, rows, width), jnp.float32),
        scratch_shapes=[pltpu.VMEM((2, rows * PAD, width), jnp.float32)],
        compiler_params=pltpu.CompilerParams(vmem_limit_bytes=32 << 20),
    )(pair, pair, gain, bias, gate_w)


def update_kernel(out_gain, out_bias, slab, gate, out_w, out, normed_s):
    hidden = slab.shape[0]
    rows = gate.shape[1]
    total = lax.fori_loop(
        0,
        hidden,
        lambda c, acc: acc + slab[c].astype(jnp.float32),
        jnp.zeros(slab.shape[1:], jnp.float32),
        unroll=16,
    )
    centre = total * (1.0 / hidden)

    def square(c, acc):
        centred = slab[c].astype(jnp.float32) - centre
        return acc + centred * centred

    squares = lax.fori_loop(0, hidden, square, jnp.zeros_like(centre), unroll=16)
    inv = lax.rsqrt(squares * (1.0 / hidden) + epsilon)

    def finish(c, carry):
        centred = slab[c].astype(jnp.float32) - centre
        normed_s[pl.ds(pl.multiple_of(c * PAD, PAD), PAD), :] = (
            centred * inv * out_gain[c] + out_bias[c]
        )
        return carry

    lax.fori_loop(0, hidden, finish, 0, unroll=16)
    for r in range(JD):
        normed = normed_s[pl.ds(r, hidden, stride=PAD), :].astype(jnp.bfloat16)
        update = dot(normed, out_w[...], (((0,), (0,)), ((), ())))
        for h in range(2):
            m = h * JD + r
            out[m] = (gate[m] * update[h * rows : (h + 1) * rows]).astype(jnp.bfloat16)


def update_of(slab, gate, out_gain, out_bias, out_w):
    hidden = slab.shape[0]
    smem = pl.BlockSpec(memory_space=pltpu.SMEM)
    vmem = pl.BlockSpec(memory_space=pltpu.VMEM)
    return pl.pallas_call(
        update_kernel,
        in_specs=[smem, smem, vmem, vmem, vmem],
        out_specs=vmem,
        out_shape=jax.ShapeDtypeStruct(gate.shape, jnp.bfloat16),
        scratch_shapes=[pltpu.VMEM((hidden * PAD, slab.shape[2]), jnp.float32)],
        compiler_params=pltpu.CompilerParams(vmem_limit_bytes=32 << 20),
    )(out_gain, out_bias, slab, gate, out_w)


def on_device(
    pair_repr,
    chain_lengths,
    norm_gain,
    norm_bias,
    left_gate,
    left_value,
    right_gate,
    right_value,
    out_gain,
    out_bias,
    out_weight,
    gate_weight,
):
    rows, cols, width = pair_repr.shape
    groups = lax.axis_size("x") * lax.axis_size("core")
    chans = lax.axis_size("z") * lax.axis_size("yl")
    residues = rows * groups * lax.axis_size("yh")
    slot_size = residues // chain_lengths.shape[0]
    gain = norm_gain.reshape(1, width)
    bias = norm_bias.reshape(1, width)
    right = project_right(
        pair_repr, chain_lengths, gain, bias, right_gate, right_value, slot_size
    )
    right = lax.all_to_all(right, SPREAD, 0, 0, tiled=True)
    left = project_left(
        pair_repr, chain_lengths, gain, bias, left_gate, left_value, slot_size
    )
    left = lax.all_to_all(left, SPREAD, 0, 0, tiled=True)
    ring = lax.axis_size("yh")
    rights = [right] + [
        lax.ppermute(right, "yh", [(n, (n + d) % ring) for n in range(ring)])
        for d in range(1, ring)
    ]
    gate = gate_of(pair_repr, gain, bias, gate_weight)
    product = product_of(
        left.reshape(groups, chans, rows, cols),
        [part.reshape(groups, chans, PAD, cols) for part in rights],
    )
    slab = lax.all_to_all(
        product.reshape(groups * chans, PAD, 2 * rows), SPREAD, 0, 0, tiled=True
    )
    update = update_of(slab, gate, out_gain, out_bias, out_weight)
    return jnp.transpose(update, (1, 0, 2))


def solution(mesh):
    names = tuple(name for name, _ in AXES)
    sizes = tuple(size for _, size in AXES)
    fine = Mesh(mesh.devices.reshape(sizes), names)
    split = P(names[:3], names[3:], None)
    return jax.shard_map(
        on_device,
        mesh=fine,
        in_specs=(split,) + (P(),) * 11,
        out_specs=split,
        check_vma=False,
    )
```

time: 183 us -> 155 us (0.85)
  blocking collectives: 66 us -> 0 us
  starting transfers between devices: 6.96 us -> 55.8 us
  waiting for transfers between devices: 61.3 us -> 81.4 us
  between operations: 13.5 us -> 0.21 us
  Pallas kernels: 26.2 us -> 16.2 us
  local copies, waits for them, and re-layouts: 8.96 us -> 0.87 us
    all_to_all x2 -> x0, blocking collectives: 66 us -> none  [the longest x1 35.3 us: on_device(): right = lax.all_to_all(right, SPREAD, 0, 0, tiled=True)]
    all_gather x1 -> x0, waiting for transfers between devices: 60.6 us -> none  [on_device(): right = lax.all_gather(right, 'yh', axis=0, tiled=True)]
    ppermute x0 -> x3, waiting for transfers between devices: none -> 50.2 us  [on_device(): lax.ppermute(right, 'yh', [(n, (n + d) % ring) for n in range(ring)])]
    all_to_all x0 -> x2, starting transfers between devices: none -> 35 us  [the longest x1 18.4 us: on_device(): lax.all_to_all(product.reshape(groups * chans, PAD, 2 * rows), SPREAD, 0,...]
    all_to_all x0 -> x2, waiting for transfers between devices: none -> 31.2 us  [the longest x1 17.8 us: on_device(): lax.all_to_all(product.reshape(groups * chans, PAD, 2 * rows), SPREAD, 0,...]
    ppermute x0 -> x3, starting transfers between devices: none -> 14 us  [on_device(): lax.ppermute(right, 'yh', [(n, (n + d) % ring) for n in range(ring)])]
    pallas_call x4 -> x5, Pallas kernels: 26.2 us -> 16.2 us  [the longest x1 5.36 us: project_left(): pl.pallas_call(functools.partial(left_kernel, rows, slot_size, where), gr...]
    unnamed x36 -> x26, local copies, waits for them, and re-layouts: 8.03 us -> 0.87 us
  transfers between devices with their start and end apart: 2 -> 6, of which waited for: 1 -> 4; matrix products, arithmetic and copies ran while one was open for 0% -> 0% of each run, Pallas kernels for 0% -> 4%
where the time goes in v2:
time: 155 us
  waiting for transfers between devices  81.4 us (53%)
  starting transfers between devices  55.8 us (36%)
  Pallas kernels  16.2 us (10%)
    ppermute x3, waiting for transfers between devices, on_device(): lax.ppermute(right, 'yh', [(n, (n + d) % ring) for n in range(ring)])  50.2 us
    all_to_all x1, starting transfers between devices, on_device(): lax.all_to_all(product.reshape(groups * chans, PAD, 2 * rows), SPREAD, 0,...  18.4 us
    all_to_all x1, waiting for transfers between devices, on_device(): lax.all_to_all(product.reshape(groups * chans, PAD, 2 * rows), SPREAD, 0,...  17.8 us
    all_to_all x1, starting transfers between devices, on_device(): right = lax.all_to_all(right, SPREAD, 0, 0, tiled=True)  16.6 us
    ppermute x3, starting transfers between devices, on_device(): lax.ppermute(right, 'yh', [(n, (n + d) % ring) for n in range(ring)])  14 us
    all_to_all x1, waiting for transfers between devices, on_device(): right = lax.all_to_all(right, SPREAD, 0, 0, tiled=True)  13.4 us
    all_to_all x1, starting transfers between devices, on_device(): left = lax.all_to_all(left, SPREAD, 0, 0, tiled=True)  6.87 us
    pallas_call x1, Pallas kernels, project_left(): pl.pallas_call(functools.partial(left_kernel, rows, slot_size, where), gr...  5.36 us
  transfers between devices with their start and end apart: 6, of which 4 were waited for; matrix products, arithmetic and copies ran while one was open for 0% of the time, Pallas kernels for 4%

profile of v2, /device:TPU:1, one launch (start us, length us, event | category | flops | bytes accessed | tf_op | source)
XLA Modules:
  0.0 154.6 jit_solution(12203488991454715469)
XLA Ops:
  0.0 0.0 copy-start.7
  0.0 0.0 copy-start
  0.0 0.0 copy-start.5
  0.0 0.0 copy-start.6
  0.0 0.0 copy-start.1
  0.0 0.0 copy-start.2
  0.0 3.1 %shard_map.119 = bf16[128,16,128]{2,1,0:T(8,128)(2,1)} custom-call(s32[8]{0:T(128)} %lengths_h.1, bf16[64,128,128]{2,1,0:T(8,128)(2,1)} %pair_b.1, f32[1,128]{1,0:T(1,128)} %bitcast.9, f32[1,128]{1,0:T(1,128)} %bitcast.12, bf16[128,128]{1,0:T(8,128)(2,1)} %gate_h.1, bf16[128,128]{1,0:T(8,128)(2,1)} %value_h.1), custom_call_target="tpu_custom_call" | custom-call | tf_op jit(solution)/shard_map/pallas_call | solution.py:134
  3.1 16.6 %all-to-all-start.1 = ((bf16[128,16,128]{2,1,0:T(8,128)(2,1)}), bf16[128,16,128]{2,1,0:T(8,128)(2,1)S(1)}, u32[]{:S(2)}, u32[]{:S(2)}) async-start(bf16[128,16,128]{2,1,0:T(8,128)(2,1)} %shard_map.119), calls=%async_computation.1 | async-start | bytes 1048576 | tf_op jit(solution)/shard_map/all_to_all | solution.py:366
  19.8 0.0 copy-done.7
  19.8 0.0 copy-done
  19.8 0.0 copy-done.5
  19.8 0.0 copy-done.6
  19.8 0.0 copy-done.1
  19.8 0.0 copy-done.2
  19.8 5.4 %shard_map.118 = bf16[128,64,128]{2,1,0:T(8,128)(2,1)} custom-call(s32[8]{0:T(128)S(1)} %copy-done.7, bf16[64,128,128]{2,1,0:T(8,128)(2,1)S(1)} %copy-done, f32[1,128]{1,0:T(1,128)S(1)} %bitcast.10, f32[1,128]{1,0:T(1,128)S(1)} %bitcast.13, bf16[128,128]{1,0:T(8,128)(2,1)S(1)} %copy-done.1, bf16[128,128]{1,0:T(8,128)(2,1)S(1)} %copy-done.2), custom_call_target="tpu_custom_call" | custom-call | flops 536870912 | bytes 4194304 | tf_op jit(solution)/shard_map/pallas_call | solution.py:173
  25.2 13.4 %all-to-all-done.1 = bf16[128,16,128]{2,1,0:T(8,128)(2,1)S(1)} async-done(((bf16[128,16,128]{2,1,0:T(8,128)(2,1)}), bf16[128,16,128]{2,1,0:T(8,128)(2,1)S(1)}, u32[]{:S(2)}, u32[]{:S(2)}) %all-to-all-start.1) | async-done | bytes 524320 | tf_op jit(solution)/shard_map/all_to_all | solution.py:366
  38.6 0.0 copy-start.10
  38.6 6.9 %all-to-all-start = ((bf16[128,64,128]{2,1,0:T(8,128)(2,1)}), bf16[128,64,128]{2,1,0:T(8,128)(2,1)}, u32[]{:S(2)}, u32[]{:S(2)}) async-start(bf16[128,64,128]{2,1,0:T(8,128)(2,1)} %shard_map.118), calls=%async_computation | async-start | bytes 4194304 | tf_op jit(solution)/shard_map/all_to_all | solution.py:370
  45.5 4.2 %collective-permute-start = (bf16[128,16,128]{2,1,0:T(8,128)(2,1)S(1)}, bf16[128,16,128]{2,1,0:T(8,128)(2,1)S(1)}, u32[]{:S(2)}, u32[]{:S(2)}) collective-permute-start(bf16[128,16,128]{2,1,0:T(8,128)(2,1)S(1)} %all-to-all-done.1), channel_id=1, source_target_pairs={{0,128},{128,256},{256,384},{384,0},{1,129},{129,257},{257,385},{3... | collective-permute-start | bytes 1572872 | tf_op jit(solution)/shard_map/ppermute | solution.py:373
  49.7 4.8 %collective-permute-start.1 = (bf16[128,16,128]{2,1,0:T(8,128)(2,1)S(1)}, bf16[128,16,128]{2,1,0:T(8,128)(2,1)S(1)}, u32[]{:S(2)}, u32[]{:S(2)}) collective-permute-start(bf16[128,16,128]{2,1,0:T(8,128)(2,1)S(1)} %all-to-all-done.1), channel_id=1, source_target_pairs={{0,256},{128,384},{256,0},{384,128},{1,257},{129,385},{257,1},{385... | collective-permute-start | bytes 1572872 | tf_op jit(solution)/shard_map/ppermute | solution.py:373
  54.5 5.0 %collective-permute-start.2 = (bf16[128,16,128]{2,1,0:T(8,128)(2,1)S(1)}, bf16[128,16,128]{2,1,0:T(8,128)(2,1)}, u32[]{:S(2)}, u32[]{:S(2)}) collective-permute-start(bf16[128,16,128]{2,1,0:T(8,128)(2,1)S(1)} %all-to-all-done.1), channel_id=1, source_target_pairs={{0,384},{128,0},{256,128},{384,256},{1,385},{129,1},{257,129},{385... | collective-permute-start | bytes 1572872 | tf_op jit(solution)/shard_map/ppermute | solution.py:373
  59.5 34.0 %collective-permute-done = bf16[128,16,128]{2,1,0:T(8,128)(2,1)S(1)} collective-permute-done((bf16[128,16,128]{2,1,0:T(8,128)(2,1)S(1)}, bf16[128,16,128]{2,1,0:T(8,128)(2,1)S(1)}, u32[]{:S(2)}, u32[]{:S(2)}) %collective-permute-start) | collective-permute-done | bytes 524320 | tf_op jit(solution)/shard_map/ppermute | solution.py:373
  93.4 0.0 copy-start.11
  93.4 16.2 %collective-permute-done.1 = bf16[128,16,128]{2,1,0:T(8,128)(2,1)S(1)} collective-permute-done((bf16[128,16,128]{2,1,0:T(8,128)(2,1)S(1)}, bf16[128,16,128]{2,1,0:T(8,128)(2,1)S(1)}, u32[]{:S(2)}, u32[]{:S(2)}) %collective-permute-start.1) | collective-permute-done | bytes 524320 | tf_op jit(solution)/shard_map/ppermute | solution.py:373
  109.6 0.0 copy-start.12
  109.7 0.8 copy-done.12
  110.5 0.0 collective-permute-done.2
  110.5 0.0 all-to-all-done
  110.5 0.0 copy-done.10
  110.5 0.0 copy-done.11
  110.5 0.0 copy-start.3
  110.5 4.5 %shard_map.120 = bf16[8,16,16,128]{3,2,1,0:T(8,128)(2,1)} custom-call(bf16[8,16,64,128]{3,2,1,0:T(8,128)(2,1)} %bitcast.2.refs_0_, bf16[8,16,16,128]{3,2,1,0:T(8,128)(2,1)} %bitcast.15, bf16[8,16,16,128]{3,2,1,0:T(8,128)(2,1)} %bitcast.16, bf16[8,16,16,128]{3,2,1,0:T(8,128)(2,1)} %bitcast.17, bf16[8,16,16,128]{3,2,1,0:T(8,128)(2,1)} %bitcast.6.refs_4_), custom_call_target="tpu_custom_call" | custom-call | tf_op jit(solution)/shard_map/pallas_call | solution.py:247
  115.0 18.4 %all-to-all-start.2 = ((bf16[128,16,128]{2,1,0:T(8,128)(2,1)}), bf16[128,16,128]{2,1,0:T(8,128)(2,1)S(1)}, u32[]{:S(2)}, u32[]{:S(2)}) async-start(bf16[128,16,128]{2,1,0:T(8,128)(2,1)} %bitcast.7), calls=%async_computation.2 | async-start | bytes 1048576 | tf_op jit(solution)/shard_map/all_to_all | solution.py:381
  133.4 0.0 copy-done.3
  133.4 0.0 copy-start.4
  133.4 0.0 copy-start.8
  133.4 0.0 copy-start.9
  133.4 1.0 shard_map.121.gate
  134.4 17.8 %all-to-all-done.2.slab = bf16[128,16,128]{2,1,0:T(8,128)(2,1)S(1)} async-done(((bf16[128,16,128]{2,1,0:T(8,128)(2,1)}), bf16[128,16,128]{2,1,0:T(8,128)(2,1)S(1)}, u32[]{:S(2)}, u32[]{:S(2)}) %all-to-all-start.2) | async-done | bytes 524320 | tf_op jit(solution)/shard_map/all_to_all | solution.py:381
  152.2 0.0 copy-done.4
  152.2 0.0 copy-done.8
  152.2 0.0 copy-done.9
  152.2 2.3 %shard_map.122 = bf16[26,64,128]{2,1,0:T(8,128)(2,1)} custom-call(f32[128]{0:T(128)S(1)} %copy-done.8, f32[128]{0:T(128)S(1)} %copy-done.9, bf16[128,16,128]{2,1,0:T(8,128)(2,1)S(1)} %all-to-all-done.2.slab, f32[26,64,128]{2,1,0:T(8,128)S(1)} %shard_map.121.gate, bf16[128,128]{1,0:T(8,128)(2,1)S(1)} %copy-done.4), custom_call_target="tpu_custom_call" | custom-call | tf_op jit(solution)/shard_map/pallas_call | solution.py:332
Async XLA Ops:
  0.0 19.8 %copy-start.7 = (s32[8]{0:T(128)S(1)}, s32[8]{0:T(128)}, u32[]{:S(2)}) copy-start(s32[8]{0:T(128)} %lengths_h.1) | copy-start | bytes 100
  0.0 19.8 %copy-start = (bf16[64,128,128]{2,1,0:T(8,128)(2,1)S(1)}, bf16[64,128,128]{2,1,0:T(8,128)(2,1)}, u32[]{:S(2)}) copy-start(bf16[64,128,128]{2,1,0:T(8,128)(2,1)} %pair_b.1) | copy-start | bytes 6291460
  0.0 19.8 %copy-start.5 = (f32[128]{0:T(128)S(1)}, f32[128]{0:T(128)}, u32[]{:S(2)}) copy-start(f32[128]{0:T(128)} %param.14) | copy-start | bytes 1540
  0.0 19.8 %copy-start.6 = (f32[128]{0:T(128)S(1)}, f32[128]{0:T(128)}, u32[]{:S(2)}) copy-start(f32[128]{0:T(128)} %param.15) | copy-start | bytes 1540
  0.0 19.8 %copy-start.1 = (bf16[128,128]{1,0:T(8,128)(2,1)S(1)}, bf16[128,128]{1,0:T(8,128)(2,1)}, u32[]{:S(2)}) copy-start(bf16[128,128]{1,0:T(8,128)(2,1)} %gate_w.2) | copy-start | bytes 98308
  0.0 19.8 %copy-start.2 = (bf16[128,128]{1,0:T(8,128)(2,1)S(1)}, bf16[128,128]{1,0:T(8,128)(2,1)}, u32[]{:S(2)}) copy-start(bf16[128,128]{1,0:T(8,128)(2,1)} %value_w.1) | copy-start | bytes 98308
  3.1 35.5 %all-to-all-start.1 = ((bf16[128,16,128]{2,1,0:T(8,128)(2,1)}), bf16[128,16,128]{2,1,0:T(8,128)(2,1)S(1)}, u32[]{:S(2)}, u32[]{:S(2)}) async-start(bf16[128,16,128]{2,1,0:T(8,128)(2,1)} %shard_map.119), calls=%async_computation.1 | async-start | bytes 1048576 | tf_op jit(solution)/shard_map/all_to_all | solution.py:366
  38.6 71.9 %copy-start.10 = (bf16[128,16,128]{2,1,0:T(8,128)(2,1)}, bf16[128,16,128]{2,1,0:T(8,128)(2,1)S(1)}, u32[]{:S(2)}) copy-start(bf16[128,16,128]{2,1,0:T(8,128)(2,1)S(1)} %all-to-all-done.1) | copy-start | bytes 1572868
  38.6 71.9 %all-to-all-start = ((bf16[128,64,128]{2,1,0:T(8,128)(2,1)}), bf16[128,64,128]{2,1,0:T(8,128)(2,1)}, u32[]{:S(2)}, u32[]{:S(2)}) async-start(bf16[128,64,128]{2,1,0:T(8,128)(2,1)} %shard_map.118), calls=%async_computation | async-start | bytes 4194304 | tf_op jit(solution)/shard_map/all_to_all | solution.py:370
  45.5 48.0 %collective-permute-start = (bf16[128,16,128]{2,1,0:T(8,128)(2,1)S(1)}, bf16[128,16,128]{2,1,0:T(8,128)(2,1)S(1)}, u32[]{:S(2)}, u32[]{:S(2)}) collective-permute-start(bf16[128,16,128]{2,1,0:T(8,128)(2,1)S(1)} %all-to-all-done.1), channel_id=1, source_target_pairs={{0,128},{128,256},{256,384},{384,0},{1,129},{129,257},{257,385},{3... | collective-permute-start | bytes 1572872 | tf_op jit(solution)/shard_map/ppermute | solution.py:373
  49.7 59.9 %collective-permute-start.1 = (bf16[128,16,128]{2,1,0:T(8,128)(2,1)S(1)}, bf16[128,16,128]{2,1,0:T(8,128)(2,1)S(1)}, u32[]{:S(2)}, u32[]{:S(2)}) collective-permute-start(bf16[128,16,128]{2,1,0:T(8,128)(2,1)S(1)} %all-to-all-done.1), channel_id=1, source_target_pairs={{0,256},{128,384},{256,0},{384,128},{1,257},{129,385},{257,1},{385... | collective-permute-start | bytes 1572872 | tf_op jit(solution)/shard_map/ppermute | solution.py:373
  54.5 56.0 %collective-permute-start.2 = (bf16[128,16,128]{2,1,0:T(8,128)(2,1)S(1)}, bf16[128,16,128]{2,1,0:T(8,128)(2,1)}, u32[]{:S(2)}, u32[]{:S(2)}) collective-permute-start(bf16[128,16,128]{2,1,0:T(8,128)(2,1)S(1)} %all-to-all-done.1), channel_id=1, source_target_pairs={{0,384},{128,0},{256,128},{384,256},{1,385},{129,1},{257,129},{385... | collective-permute-start | bytes 1572872 | tf_op jit(solution)/shard_map/ppermute | solution.py:373
  93.4 17.0 %copy-start.11 = (bf16[128,16,128]{2,1,0:T(8,128)(2,1)}, bf16[128,16,128]{2,1,0:T(8,128)(2,1)S(1)}, u32[]{:S(2)}) copy-start(bf16[128,16,128]{2,1,0:T(8,128)(2,1)S(1)} %collective-permute-done) | copy-start | bytes 1572868
  109.6 0.8 copy-start.12
  110.5 22.9 %copy-start.3 = (bf16[128,128]{1,0:T(8,128)(2,1)S(1)}, bf16[128,128]{1,0:T(8,128)(2,1)}, u32[]{:S(2)}) copy-start(bf16[128,128]{1,0:T(8,128)(2,1)} %gate_w.3) | copy-start | bytes 98308
  115.0 37.2 %all-to-all-start.2 = ((bf16[128,16,128]{2,1,0:T(8,128)(2,1)}), bf16[128,16,128]{2,1,0:T(8,128)(2,1)S(1)}, u32[]{:S(2)}, u32[]{:S(2)}) async-start(bf16[128,16,128]{2,1,0:T(8,128)(2,1)} %bitcast.7), calls=%async_computation.2 | async-start | bytes 1048576 | tf_op jit(solution)/shard_map/all_to_all | solution.py:381
  133.4 18.8 %copy-start.4 = (bf16[128,128]{1,0:T(8,128)(2,1)S(1)}, bf16[128,128]{1,0:T(8,128)(2,1)}, u32[]{:S(2)}) copy-start(bf16[128,128]{1,0:T(8,128)(2,1)} %out_w.1) | copy-start | bytes 98308
  133.4 18.8 %copy-start.8 = (f32[128]{0:T(128)S(1)}, f32[128]{0:T(128)}, u32[]{:S(2)}) copy-start(f32[128]{0:T(128)} %out_gain.1) | copy-start | bytes 1540
  133.4 18.8 %copy-start.9 = (f32[128]{0:T(128)S(1)}, f32[128]{0:T(128)}, u32[]{:S(2)}) copy-start(f32[128]{0:T(128)} %out_bias.1) | copy-start | bytes 1540

commit v3 on v2

--- a/solution.py
+++ b/solution.py
@@ -12,7 +12,8 @@
 PAD = 16
 BATCH = 4
 AXES = (("yh", 4), ("x", 4), ("core", 2), ("z", 8), ("yl", 2))
-SPREAD = ("x", "core", "z", "yl")
+SPREAD = ("yh", "core", "z", "yl")
+RING = "x"
 
 epsilon = 1e-05
 
@@ -225,22 +226,22 @@
     low = lax.broadcasted_iota(jnp.int32, (PAD, 2 * rows), 1) < rows
     half = groups // 2
     for d in range(ring):
-        base = lax.rem(me + ring - d, ring) * half
+        member = lax.rem(me + ring - d, ring)
         for q in range(half):
             top = (d * groups + 2 * q) * PAD
             for g in range(0, groups, 2):
                 span = slice(g * rows, (g + 2) * rows)
                 first = acc[top : top + PAD, span]
                 second = acc[top + PAD : top + 2 * PAD, span]
-                out[g, base + q] = jnp.where(low, first, pltpu.roll(second, rows, 1)).astype(
+                out[g, q * ring + member] = jnp.where(low, first, pltpu.roll(second, rows, 1)).astype(
                     jnp.bfloat16
                 )
-                out[g + 1, base + q] = jnp.where(
+                out[g + 1, q * ring + member] = jnp.where(
                     low, pltpu.roll(first, rows, 1), second
                 ).astype(jnp.bfloat16)
 
 
-def product_of(left, rights, where=lambda: lax.axis_index("yh")):
+def product_of(left, rights, where=lambda: lax.axis_index(RING)):
     groups, chans, rows, cols = left.shape
     ring = len(rights)
     hbm = pl.BlockSpec(memory_space=pltpu.HBM)
@@ -354,9 +355,10 @@
     gate_weight,
 ):
     rows, cols, width = pair_repr.shape
-    groups = lax.axis_size("x") * lax.axis_size("core")
+    groups = lax.axis_size("yh") * lax.axis_size("core")
     chans = lax.axis_size("z") * lax.axis_size("yl")
-    residues = rows * groups * lax.axis_size("yh")
+    ring = lax.axis_size(RING)
+    residues = rows * groups * ring
     slot_size = residues // chain_lengths.shape[0]
     gain = norm_gain.reshape(1, width)
     bias = norm_bias.reshape(1, width)
@@ -368,9 +370,8 @@
         pair_repr, chain_lengths, gain, bias, left_gate, left_value, slot_size
     )
     left = lax.all_to_all(left, SPREAD, 0, 0, tiled=True)
-    ring = lax.axis_size("yh")
     rights = [right] + [
-        lax.ppermute(right, "yh", [(n, (n + d) % ring) for n in range(ring)])
+        lax.ppermute(right, RING, [(n, (n + d) % ring) for n in range(ring)])
         for d in range(1, ring)
     ]
     gate = gate_of(pair_repr, gain, bias, gate_weight)

time: 155 us -> 137 us (0.88)
  starting transfers between devices: 55.8 us -> 45.5 us
  waiting for transfers between devices: 81.4 us -> 73.1 us
    ppermute x3, waiting for transfers between devices: 50.2 us -> 18.3 us  [on_device(): lax.ppermute(right, RING, [(n, (n + d) % ring) for n in range(ring)])]
    all_to_all x1, waiting for transfers between devices: 0.01 us -> 21.5 us  [on_device(): left = lax.all_to_all(left, SPREAD, 0, 0, tiled=True)]
    all_to_all x1, starting transfers between devices: 18.4 us -> 8.4 us  [on_device(): lax.all_to_all(product.reshape(groups * chans, PAD, 2 * rows), SPREAD, 0,...]
    ppermute x3, starting transfers between devices: 14 us -> 10.5 us  [on_device(): lax.ppermute(right, RING, [(n, (n + d) % ring) for n in range(ring)])]
    all_to_all x1, starting transfers between devices: 16.6 us -> 18.4 us  [on_device(): right = lax.all_to_all(right, SPREAD, 0, 0, tiled=True)]
  transfers between devices with their start and end apart: 6 -> 6, of which waited for: 4 -> 6; matrix products, arithmetic and copies ran while one was open for 0% -> 0% of each run, Pallas kernels for 4% -> 5%
where the time goes in v3:
time: 137 us; the launch traced here: 136 us
  waiting for transfers between devices  73.1 us (53%)
  starting transfers between devices  45.5 us (33%)
  Pallas kernels  16.2 us (12%)
    all_to_all x1, waiting for transfers between devices, on_device(): left = lax.all_to_all(left, SPREAD, 0, 0, tiled=True)  21.5 us
    all_to_all x1, waiting for transfers between devices, on_device(): lax.all_to_all(product.reshape(groups * chans, PAD, 2 * rows), SPREAD, 0,...  18.8 us
    all_to_all x1, starting transfers between devices, on_device(): right = lax.all_to_all(right, SPREAD, 0, 0, tiled=True)  18.4 us
    ppermute x3, waiting for transfers between devices, on_device(): lax.ppermute(right, RING, [(n, (n + d) % ring) for n in range(ring)])  18.3 us
    all_to_all x1, waiting for transfers between devices, on_device(): right = lax.all_to_all(right, SPREAD, 0, 0, tiled=True)  14.4 us
    ppermute x3, starting transfers between devices, on_device(): lax.ppermute(right, RING, [(n, (n + d) % ring) for n in range(ring)])  10.5 us
    all_to_all x1, starting transfers between devices, on_device(): lax.all_to_all(product.reshape(groups * chans, PAD, 2 * rows), SPREAD, 0,...  8.4 us
    all_to_all x1, starting transfers between devices, on_device(): left = lax.all_to_all(left, SPREAD, 0, 0, tiled=True)  8.13 us
  transfers between devices with their start and end apart: 6, of which 6 were waited for; matrix products, arithmetic and copies ran while one was open for 0% of the time, Pallas kernels for 5%

profile of v3, /device:TPU:1, one launch (start us, length us, event | category | flops | bytes accessed | tf_op | source)
XLA Modules:
  0.0 135.9 jit_solution(14643537026977235585)
XLA Ops:
  0.0 0.0 copy-start.7
  0.0 0.0 copy-start
  0.0 0.0 copy-start.5
  0.0 0.0 copy-start.6
  0.0 0.0 copy-start.1
  0.0 0.0 copy-start.2
  0.0 3.1 %shard_map.119 = bf16[128,16,128]{2,1,0:T(8,128)(2,1)} custom-call(s32[8]{0:T(128)} %lengths_h.1, bf16[64,128,128]{2,1,0:T(8,128)(2,1)} %pair_b.1, f32[1,128]{1,0:T(1,128)} %bitcast.9, f32[1,128]{1,0:T(1,128)} %bitcast.12, bf16[128,128]{1,0:T(8,128)(2,1)} %gate_h.1, bf16[128,128]{1,0:T(8,128)(2,1)} %value_h.1), custom_call_target="tpu_custom_call" | custom-call | tf_op jit(solution)/shard_map/pallas_call | solution.py:135
  3.1 18.4 %all-to-all-start.1 = ((bf16[128,16,128]{2,1,0:T(8,128)(2,1)}), bf16[128,16,128]{2,1,0:T(8,128)(2,1)S(1)}, u32[]{:S(2)}, u32[]{:S(2)}) async-start(bf16[128,16,128]{2,1,0:T(8,128)(2,1)} %shard_map.119), calls=%async_computation.1 | async-start | bytes 1048576 | tf_op jit(solution)/shard_map/all_to_all | solution.py:368
  21.6 0.0 copy-done.7
  21.6 0.0 copy-done
  21.6 0.0 copy-done.5
  21.6 0.0 copy-done.6
  21.6 0.0 copy-done.1
  21.6 0.0 copy-done.2
  21.6 5.4 %shard_map.118 = bf16[128,64,128]{2,1,0:T(8,128)(2,1)} custom-call(s32[8]{0:T(128)S(1)} %copy-done.7, bf16[64,128,128]{2,1,0:T(8,128)(2,1)S(1)} %copy-done, f32[1,128]{1,0:T(1,128)S(1)} %bitcast.10, f32[1,128]{1,0:T(1,128)S(1)} %bitcast.13, bf16[128,128]{1,0:T(8,128)(2,1)S(1)} %copy-done.1, bf16[128,128]{1,0:T(8,128)(2,1)S(1)} %copy-done.2), custom_call_target="tpu_custom_call" | custom-call | flops 536870912 | bytes 4194304 | tf_op jit(solution)/shard_map/pallas_call | solution.py:174
  27.0 14.4 %all-to-all-done.1 = bf16[128,16,128]{2,1,0:T(8,128)(2,1)S(1)} async-done(((bf16[128,16,128]{2,1,0:T(8,128)(2,1)}), bf16[128,16,128]{2,1,0:T(8,128)(2,1)S(1)}, u32[]{:S(2)}, u32[]{:S(2)}) %all-to-all-start.1) | async-done | bytes 524320 | tf_op jit(solution)/shard_map/all_to_all | solution.py:368
  41.4 0.0 copy-start.10
  41.4 8.1 %all-to-all-start = ((bf16[128,64,128]{2,1,0:T(8,128)(2,1)}), bf16[128,64,128]{2,1,0:T(8,128)(2,1)}, u32[]{:S(2)}, u32[]{:S(2)}) async-start(bf16[128,64,128]{2,1,0:T(8,128)(2,1)} %shard_map.118), calls=%async_computation | async-start | bytes 4194304 | tf_op jit(solution)/shard_map/all_to_all | solution.py:372
  49.6 3.1 %collective-permute-start = (bf16[128,16,128]{2,1,0:T(8,128)(2,1)S(1)}, bf16[128,16,128]{2,1,0:T(8,128)(2,1)S(1)}, u32[]{:S(2)}, u32[]{:S(2)}) collective-permute-start(bf16[128,16,128]{2,1,0:T(8,128)(2,1)S(1)} %all-to-all-done.1), channel_id=1, source_target_pairs={{0,32},{32,64},{64,96},{96,0},{1,33},{33,65},{65,97},{97,1},{2,34}... | collective-permute-start | bytes 1572872 | tf_op jit(solution)/shard_map/ppermute | solution.py:374
  52.7 4.4 %collective-permute-start.1 = (bf16[128,16,128]{2,1,0:T(8,128)(2,1)S(1)}, bf16[128,16,128]{2,1,0:T(8,128)(2,1)S(1)}, u32[]{:S(2)}, u32[]{:S(2)}) collective-permute-start(bf16[128,16,128]{2,1,0:T(8,128)(2,1)S(1)} %all-to-all-done.1), channel_id=1, source_target_pairs={{0,64},{32,96},{64,0},{96,32},{1,65},{33,97},{65,1},{97,33},{2,66}... | collective-permute-start | bytes 1572872 | tf_op jit(solution)/shard_map/ppermute | solution.py:374
  57.1 3.1 %collective-permute-start.2 = (bf16[128,16,128]{2,1,0:T(8,128)(2,1)S(1)}, bf16[128,16,128]{2,1,0:T(8,128)(2,1)}, u32[]{:S(2)}, u32[]{:S(2)}) collective-permute-start(bf16[128,16,128]{2,1,0:T(8,128)(2,1)S(1)} %all-to-all-done.1), channel_id=1, source_target_pairs={{0,96},{32,0},{64,32},{96,64},{1,97},{33,1},{65,33},{97,65},{2,98}... | collective-permute-start | bytes 1572872 | tf_op jit(solution)/shard_map/ppermute | solution.py:374
  60.1 5.1 %collective-permute-done = bf16[128,16,128]{2,1,0:T(8,128)(2,1)S(1)} collective-permute-done((bf16[128,16,128]{2,1,0:T(8,128)(2,1)S(1)}, bf16[128,16,128]{2,1,0:T(8,128)(2,1)S(1)}, u32[]{:S(2)}, u32[]{:S(2)}) %collective-permute-start) | collective-permute-done | bytes 524320 | tf_op jit(solution)/shard_map/ppermute | solution.py:374
  65.2 0.0 copy-start.11
  65.2 12.2 %collective-permute-done.1 = bf16[128,16,128]{2,1,0:T(8,128)(2,1)S(1)} collective-permute-done((bf16[128,16,128]{2,1,0:T(8,128)(2,1)S(1)}, bf16[128,16,128]{2,1,0:T(8,128)(2,1)S(1)}, u32[]{:S(2)}, u32[]{:S(2)}) %collective-permute-start.1) | collective-permute-done | bytes 524320 | tf_op jit(solution)/shard_map/ppermute | solution.py:374
  77.4 0.0 copy-start.12
  77.4 0.8 copy-done.12
  78.3 1.0 collective-permute-done.2
  79.2 21.5 %all-to-all-done = bf16[128,64,128]{2,1,0:T(8,128)(2,1)} async-done(((bf16[128,64,128]{2,1,0:T(8,128)(2,1)}), bf16[128,64,128]{2,1,0:T(8,128)(2,1)}, u32[]{:S(2)}, u32[]{:S(2)}) %all-to-all-start) | async-done | bytes 2097184 | tf_op jit(solution)/shard_map/all_to_all | solution.py:372
  100.8 0.0 copy-done.10
  100.8 0.0 copy-done.11
  100.8 0.0 copy-start.3
  100.8 4.5 %shard_map.120 = bf16[8,16,16,128]{3,2,1,0:T(8,128)(2,1)} custom-call(bf16[8,16,64,128]{3,2,1,0:T(8,128)(2,1)} %bitcast.2.refs_0_, bf16[8,16,16,128]{3,2,1,0:T(8,128)(2,1)} %bitcast.15, bf16[8,16,16,128]{3,2,1,0:T(8,128)(2,1)} %bitcast.16, bf16[8,16,16,128]{3,2,1,0:T(8,128)(2,1)} %bitcast.17, bf16[8,16,16,128]{3,2,1,0:T(8,128)(2,1)} %bitcast.6.refs_4_), custom_call_target="tpu_custom_call" | custom-call | tf_op jit(solution)/shard_map/pallas_call | solution.py:248
  105.3 8.4 %all-to-all-start.2 = ((bf16[128,16,128]{2,1,0:T(8,128)(2,1)}), bf16[128,16,128]{2,1,0:T(8,128)(2,1)S(1)}, u32[]{:S(2)}, u32[]{:S(2)}) async-start(bf16[128,16,128]{2,1,0:T(8,128)(2,1)} %bitcast.7), calls=%async_computation.2 | async-start | bytes 1048576 | tf_op jit(solution)/shard_map/all_to_all | solution.py:382
  113.7 0.0 copy-done.3
  113.7 0.0 copy-start.4
  113.7 0.0 copy-start.8
  113.7 0.0 copy-start.9
  113.8 1.0 shard_map.121.gate
  114.7 18.8 %all-to-all-done.2.slab = bf16[128,16,128]{2,1,0:T(8,128)(2,1)S(1)} async-done(((bf16[128,16,128]{2,1,0:T(8,128)(2,1)}), bf16[128,16,128]{2,1,0:T(8,128)(2,1)S(1)}, u32[]{:S(2)}, u32[]{:S(2)}) %all-to-all-start.2) | async-done | bytes 524320 | tf_op jit(solution)/shard_map/all_to_all | solution.py:382
  133.6 0.0 copy-done.4
  133.6 0.0 copy-done.8
  133.6 0.0 copy-done.9
  133.6 2.3 %shard_map.122 = bf16[26,64,128]{2,1,0:T(8,128)(2,1)} custom-call(f32[128]{0:T(128)S(1)} %copy-done.8, f32[128]{0:T(128)S(1)} %copy-done.9, bf16[128,16,128]{2,1,0:T(8,128)(2,1)S(1)} %all-to-all-done.2.slab, f32[26,64,128]{2,1,0:T(8,128)S(1)} %shard_map.121.gate, bf16[128,128]{1,0:T(8,128)(2,1)S(1)} %copy-done.4), custom_call_target="tpu_custom_call" | custom-call | tf_op jit(solution)/shard_map/pallas_call | solution.py:333
Async XLA Ops:
  0.0 21.6 %copy-start.7 = (s32[8]{0:T(128)S(1)}, s32[8]{0:T(128)}, u32[]{:S(2)}) copy-start(s32[8]{0:T(128)} %lengths_h.1) | copy-start | bytes 100
  0.0 21.6 %copy-start = (bf16[64,128,128]{2,1,0:T(8,128)(2,1)S(1)}, bf16[64,128,128]{2,1,0:T(8,128)(2,1)}, u32[]{:S(2)}) copy-start(bf16[64,128,128]{2,1,0:T(8,128)(2,1)} %pair_b.1) | copy-start | bytes 6291460
  0.0 21.6 %copy-start.5 = (f32[128]{0:T(128)S(1)}, f32[128]{0:T(128)}, u32[]{:S(2)}) copy-start(f32[128]{0:T(128)} %param.14) | copy-start | bytes 1540
  0.0 21.6 %copy-start.6 = (f32[128]{0:T(128)S(1)}, f32[128]{0:T(128)}, u32[]{:S(2)}) copy-start(f32[128]{0:T(128)} %param.15) | copy-start | bytes 1540
  0.0 21.6 %copy-start.1 = (bf16[128,128]{1,0:T(8,128)(2,1)S(1)}, bf16[128,128]{1,0:T(8,128)(2,1)}, u32[]{:S(2)}) copy-start(bf16[128,128]{1,0:T(8,128)(2,1)} %gate_w.2) | copy-start | bytes 98308
  0.0 21.6 %copy-start.2 = (bf16[128,128]{1,0:T(8,128)(2,1)S(1)}, bf16[128,128]{1,0:T(8,128)(2,1)}, u32[]{:S(2)}) copy-start(bf16[128,128]{1,0:T(8,128)(2,1)} %value_w.1) | copy-start | bytes 98308
  3.1 38.3 %all-to-all-start.1 = ((bf16[128,16,128]{2,1,0:T(8,128)(2,1)}), bf16[128,16,128]{2,1,0:T(8,128)(2,1)S(1)}, u32[]{:S(2)}, u32[]{:S(2)}) async-start(bf16[128,16,128]{2,1,0:T(8,128)(2,1)} %shard_map.119), calls=%async_computation.1 | async-start | bytes 1048576 | tf_op jit(solution)/shard_map/all_to_all | solution.py:368
  41.4 59.4 %copy-start.10 = (bf16[128,16,128]{2,1,0:T(8,128)(2,1)}, bf16[128,16,128]{2,1,0:T(8,128)(2,1)S(1)}, u32[]{:S(2)}) copy-start(bf16[128,16,128]{2,1,0:T(8,128)(2,1)S(1)} %all-to-all-done.1) | copy-start | bytes 1572868
  41.4 59.3 %all-to-all-start = ((bf16[128,64,128]{2,1,0:T(8,128)(2,1)}), bf16[128,64,128]{2,1,0:T(8,128)(2,1)}, u32[]{:S(2)}, u32[]{:S(2)}) async-start(bf16[128,64,128]{2,1,0:T(8,128)(2,1)} %shard_map.118), calls=%async_computation | async-start | bytes 4194304 | tf_op jit(solution)/shard_map/all_to_all | solution.py:372
  49.6 15.7 %collective-permute-start = (bf16[128,16,128]{2,1,0:T(8,128)(2,1)S(1)}, bf16[128,16,128]{2,1,0:T(8,128)(2,1)S(1)}, u32[]{:S(2)}, u32[]{:S(2)}) collective-permute-start(bf16[128,16,128]{2,1,0:T(8,128)(2,1)S(1)} %all-to-all-done.1), channel_id=1, source_target_pairs={{0,32},{32,64},{64,96},{96,0},{1,33},{33,65},{65,97},{97,1},{2,34}... | collective-permute-start | bytes 1572872 | tf_op jit(solution)/shard_map/ppermute | solution.py:374
  52.7 24.8 %collective-permute-start.1 = (bf16[128,16,128]{2,1,0:T(8,128)(2,1)S(1)}, bf16[128,16,128]{2,1,0:T(8,128)(2,1)S(1)}, u32[]{:S(2)}, u32[]{:S(2)}) collective-permute-start(bf16[128,16,128]{2,1,0:T(8,128)(2,1)S(1)} %all-to-all-done.1), channel_id=1, source_target_pairs={{0,64},{32,96},{64,0},{96,32},{1,65},{33,97},{65,1},{97,33},{2,66}... | collective-permute-start | bytes 1572872 | tf_op jit(solution)/shard_map/ppermute | solution.py:374
  57.1 22.2 %collective-permute-start.2 = (bf16[128,16,128]{2,1,0:T(8,128)(2,1)S(1)}, bf16[128,16,128]{2,1,0:T(8,128)(2,1)}, u32[]{:S(2)}, u32[]{:S(2)}) collective-permute-start(bf16[128,16,128]{2,1,0:T(8,128)(2,1)S(1)} %all-to-all-done.1), channel_id=1, source_target_pairs={{0,96},{32,0},{64,32},{96,64},{1,97},{33,1},{65,33},{97,65},{2,98}... | collective-permute-start | bytes 1572872 | tf_op jit(solution)/shard_map/ppermute | solution.py:374
  65.2 35.6 %copy-start.11 = (bf16[128,16,128]{2,1,0:T(8,128)(2,1)}, bf16[128,16,128]{2,1,0:T(8,128)(2,1)S(1)}, u32[]{:S(2)}) copy-start(bf16[128,16,128]{2,1,0:T(8,128)(2,1)S(1)} %collective-permute-done) | copy-start | bytes 1572868
  77.4 0.8 copy-start.12
  100.8 12.9 %copy-start.3 = (bf16[128,128]{1,0:T(8,128)(2,1)S(1)}, bf16[128,128]{1,0:T(8,128)(2,1)}, u32[]{:S(2)}) copy-start(bf16[128,128]{1,0:T(8,128)(2,1)} %gate_w.3) | copy-start | bytes 98308
  105.3 28.3 %all-to-all-start.2 = ((bf16[128,16,128]{2,1,0:T(8,128)(2,1)}), bf16[128,16,128]{2,1,0:T(8,128)(2,1)S(1)}, u32[]{:S(2)}, u32[]{:S(2)}) async-start(bf16[128,16,128]{2,1,0:T(8,128)(2,1)} %bitcast.7), calls=%async_computation.2 | async-start | bytes 1048576 | tf_op jit(solution)/shard_map/all_to_all | solution.py:382
  113.7 19.8 %copy-start.4 = (bf16[128,128]{1,0:T(8,128)(2,1)S(1)}, bf16[128,128]{1,0:T(8,128)(2,1)}, u32[]{:S(2)}) copy-start(bf16[128,128]{1,0:T(8,128)(2,1)} %out_w.1) | copy-start | bytes 98308
  113.7 19.8 %copy-start.8 = (f32[128]{0:T(128)S(1)}, f32[128]{0:T(128)}, u32[]{:S(2)}) copy-start(f32[128]{0:T(128)} %out_gain.1) | copy-start | bytes 1540
  113.7 19.8 %copy-start.9 = (f32[128]{0:T(128)S(1)}, f32[128]{0:T(128)}, u32[]{:S(2)}) copy-start(f32[128]{0:T(128)} %out_bias.1) | copy-start | bytes 1540

commit v4 on v3

--- a/solution.py
+++ b/solution.py
@@ -12,7 +12,7 @@
 PAD = 16
 BATCH = 4
 AXES = (("yh", 4), ("x", 4), ("core", 2), ("z", 8), ("yl", 2))
-SPREAD = ("yh", "core", "z", "yl")
+SPREAD = ("yh", "z", "yl")
 RING = "x"
 
 epsilon = 1e-05
@@ -195,68 +195,79 @@
 
 
 def product_kernel(ring, where, *refs):
-    left_h, rights_h = refs[0], refs[1 : 1 + ring]
-    out, left_mat, right_mat, acc, sems = refs[1 + ring :]
-    groups, chans, rows, cols = left_h.shape
-    me = where()
-    copies = []
-    for c in range(chans):
-        span = pl.ds(c * cols, cols)
-        pairs = [(left_h.at[:, c], left_mat.at[:, :, span])]
-        pairs += [
-            (right.at[:, c], right_mat.at[pl.ds(d * groups, groups), :, span])
-            for d, right in enumerate(rights_h)
-        ]
-        copies.append(fetch(sems.at[c], *pairs))
-    size = 4
-    for first in range(0, chans, size):
-        for c in range(first, first + size):
-            for copy in copies[c]:
-                copy.wait()
-        span = slice(first * cols, (first + size) * cols)
-        part = dot(
-            right_mat[:, :, span].reshape(ring * groups * PAD, size * cols),
-            left_mat[:, :, span].reshape(groups * rows, size * cols),
-            (((1,), (1,)), ((), ())),
+    count = 1 + 2 * ring
+    sources, out, acc, sems, held = refs[:count], *refs[count : count + 3], refs[count + 3 :]
+    left = held[0]
+    groups, chans, hidden, rows, cols = left.shape
+    paired = [held[1 + part * ring + d] for d in range(ring) for part in range(2)]
+    half = chans // 2
+    waves = [
+        fetch(
+            sems.at[h],
+            *[
+                (a.at[:, pl.ds(h * half, half)], b.at[:, pl.ds(h * half, half)])
+                for a, b in zip(sources, held)
+            ],
         )
-        if first == 0:
-            acc[...] = part
-        else:
-            acc[...] += part
+        for h in range(2)
+    ]
+    me, core = where()
     low = lax.broadcasted_iota(jnp.int32, (PAD, 2 * rows), 1) < rows
-    half = groups // 2
-    for d in range(ring):
-        member = lax.rem(me + ring - d, ring)
-        for q in range(half):
-            top = (d * groups + 2 * q) * PAD
-            for g in range(0, groups, 2):
-                span = slice(g * rows, (g + 2) * rows)
-                first = acc[top : top + PAD, span]
-                second = acc[top + PAD : top + 2 * PAD, span]
-                out[g, q * ring + member] = jnp.where(low, first, pltpu.roll(second, rows, 1)).astype(
-                    jnp.bfloat16
+    wide = 2
+
+    def side(parts, first, ch):
+        pieces = []
+        for c in range(first, first + wide):
+            tiles = [part[:, c, ch] for part in parts]
+            height = tiles[0].shape[0] * tiles[0].shape[1]
+            pieces.append(jnp.concatenate([t.reshape(height, cols) for t in tiles], axis=0))
+        return jnp.concatenate(pieces, axis=1)
+
+    for h, wave in enumerate(waves):
+        for copy in wave:
+            copy.wait()
+        for ch in range(hidden):
+            total = None if h == 0 else acc[ch].reshape(-1, groups * rows)
+            for first in range(h * half, (h + 1) * half, wide):
+                piece = dot(
+                    side(paired, first, ch), side([left], first, ch), (((1,), (1,)), ((), ()))
                 )
-                out[g + 1, q * ring + member] = jnp.where(
-                    low, pltpu.roll(first, rows, 1), second
-                ).astype(jnp.bfloat16)
-
-
-def product_of(left, rights, where=lambda: lax.axis_index(RING)):
-    groups, chans, rows, cols = left.shape
-    ring = len(rights)
-    hbm = pl.BlockSpec(memory_space=pltpu.HBM)
+                total = piece if total is None else total + piece
+            acc[ch] = total.reshape(acc.shape[1:])
+    for ch in range(hidden):
+        for d in range(ring):
+            member = lax.rem(me + ring - d, ring)
+            for q in range(groups):
+                upper = acc.at[ch, d, core, q]
+                lower = acc.at[ch, d, 1 - core, q]
+                for g in range(0, groups, 2):
+                    span = pl.ds(g * rows, 2 * rows)
+                    u, v = upper[:, span], lower[:, span]
+                    spot = q * ring + member
+                    out[g, spot, ch] = jnp.where(low, u, pltpu.roll(v, rows, 1)).astype(
+                        jnp.bfloat16
+                    )
+                    out[g + 1, spot, ch] = jnp.where(low, pltpu.roll(u, rows, 1), v).astype(
+                        jnp.bfloat16
+                    )
+
+
+def product_of(left, own, other, where=lambda: (lax.axis_index(RING), lax.axis_index("core"))):
+    groups, chans, hidden, rows, cols = left.shape
+    ring = len(own)
+    arrays = (left, *own, *other)
     return pl.pallas_call(
         functools.partial(product_kernel, ring, where),
-        in_specs=[hbm] * (1 + ring),
-        out_shape=jax.ShapeDtypeStruct((groups, chans, PAD, 2 * rows), jnp.bfloat16),
+        in_specs=[pl.BlockSpec(memory_space=pltpu.HBM)] * len(arrays),
+        out_specs=pl.BlockSpec(memory_space=pltpu.VMEM),
+        out_shape=jax.ShapeDtypeStruct((groups, chans, hidden, PAD, 2 * rows), jnp.bfloat16),
         scratch_shapes=[
-            pltpu.VMEM((groups, rows, chans * cols), jnp.bfloat16),
-            pltpu.VMEM((ring * groups, PAD, chans * cols), jnp.bfloat16),
-            pltpu.VMEM((ring * groups * PAD, groups * rows), jnp.float32),
-            pltpu.SemaphoreType.DMA((chans, 1 + ring)),
+            pltpu.VMEM((hidden, ring, 2, groups, PAD, groups * rows), jnp.float32),
+            pltpu.SemaphoreType.DMA((2, len(arrays))),
+            *[pltpu.VMEM(array.shape, jnp.bfloat16) for array in arrays],
         ],
         compiler_params=pltpu.CompilerParams(vmem_limit_bytes=48 << 20),
-    )(*in_hbm(left, *rights))
+    )(*in_hbm(*arrays))
 
 
 def gate_kernel(pair_a, pair_b, gain, bias, gate_w, out, gate_s):
@@ -355,10 +366,11 @@
     gate_weight,
 ):
     rows, cols, width = pair_repr.shape
-    groups = lax.axis_size("yh") * lax.axis_size("core")
+    hidden = left_gate.shape[1]
+    groups = lax.axis_size("yh")
     chans = lax.axis_size("z") * lax.axis_size("yl")
     ring = lax.axis_size(RING)
-    residues = rows * groups * ring
+    residues = rows * groups * ring * lax.axis_size("core")
     slot_size = residues // chain_lengths.shape[0]
     gain = norm_gain.reshape(1, width)
     bias = norm_bias.reshape(1, width)
@@ -370,17 +382,20 @@
         pair_repr, chain_lengths, gain, bias, left_gate, left_value, slot_size
     )
     left = lax.all_to_all(left, SPREAD, 0, 0, tiled=True)
-    rights = [right] + [
+    own = [right] + [
         lax.ppermute(right, RING, [(n, (n + d) % ring) for n in range(ring)])
         for d in range(1, ring)
     ]
+    other = [lax.ppermute(part, "core", [(0, 1), (1, 0)]) for part in own]
     gate = gate_of(pair_repr, gain, bias, gate_weight)
+    shape = (groups, chans, hidden // (groups * chans))
     product = product_of(
-        left.reshape(groups, chans, rows, cols),
-        [part.reshape(groups, chans, PAD, cols) for part in rights],
+        left.reshape(*shape, rows, cols),
+        [part.reshape(*shape, PAD, cols) for part in own],
+        [part.reshape(*shape, PAD, cols) for part in other],
     )
     slab = lax.all_to_all(
-        product.reshape(groups * chans, PAD, 2 * rows), SPREAD, 0, 0, tiled=True
+        product.reshape(hidden, PAD, 2 * rows), SPREAD, 0, 0, tiled=True
     )
     update = update_of(slab, gate, out_gain, out_bias, out_weight)
     return jnp.transpose(update, (1, 0, 2))

time: 137 us -> 130 us (0.949)
  waiting for transfers between devices: 73.1 us -> 45.7 us
  starting transfers between devices: 45.5 us -> 63.5 us
    ppermute x0 -> x4, starting transfers between devices: none -> 16 us  [on_device(): other = [lax.ppermute(part, 'core', [(0, 1), (1, 0)]) for part in own]]
    ppermute x3, waiting for transfers between devices: 18.3 us -> 6.93 us  [on_device(): lax.ppermute(right, RING, [(n, (n + d) % ring) for n in range(ring)])]
    all_to_all x1, waiting for transfers between devices: 21.5 us -> 12.4 us  [on_device(): left = lax.all_to_all(left, SPREAD, 0, 0, tiled=True)]
    all_to_all x1, waiting for transfers between devices: 18.8 us -> 15 us  [on_device(): lax.all_to_all(product.reshape(hidden, PAD, 2 * rows), SPREAD, 0, 0, tile...]
    all_to_all x1, starting transfers between devices: 8.4 us -> 12 us  [on_device(): lax.all_to_all(product.reshape(hidden, PAD, 2 * rows), SPREAD, 0, 0, tile...]
    all_to_all x1, waiting for transfers between devices: 14.4 us -> 11.1 us  [on_device(): right = lax.all_to_all(right, SPREAD, 0, 0, tiled=True)]
  transfers between devices with their start and end apart: 6 -> 10, of which waited for: 6 -> 6; matrix products, arithmetic and copies ran while one was open for 0% -> 0% of each run, Pallas kernels for 5% -> 5%
where the time goes in v4:
time: 130 us; the launch traced here: 128 us
  starting transfers between devices  63.5 us (49%)
  waiting for transfers between devices  45.7 us (35%)
  Pallas kernels  16.4 us (13%)
  local copies, waits for them, and re-layouts  1.76 us (1%)
    all_to_all x1, starting transfers between devices, on_device(): right = lax.all_to_all(right, SPREAD, 0, 0, tiled=True)  17.1 us
    ppermute x4, starting transfers between devices, on_device(): other = [lax.ppermute(part, 'core', [(0, 1), (1, 0)]) for part in own]  16 us
    all_to_all x1, waiting for transfers between devices, on_device(): lax.all_to_all(product.reshape(hidden, PAD, 2 * rows), SPREAD, 0, 0, tile...  15 us
    all_to_all x1, waiting for transfers between devices, on_device(): left = lax.all_to_all(left, SPREAD, 0, 0, tiled=True)  12.4 us
    all_to_all x1, starting transfers between devices, on_device(): lax.all_to_all(product.reshape(hidden, PAD, 2 * rows), SPREAD, 0, 0, tile...  12 us
    all_to_all x1, waiting for transfers between devices, on_device(): right = lax.all_to_all(right, SPREAD, 0, 0, tiled=True)  11.1 us
    ppermute x3, starting transfers between devices, on_device(): lax.ppermute(right, RING, [(n, (n + d) % ring) for n in range(ring)])  10.5 us
    all_to_all x1, starting transfers between devices, on_device(): left = lax.all_to_all(left, SPREAD, 0, 0, tiled=True)  7.84 us
  transfers between devices with their start and end apart: 10, of which 6 were waited for; matrix products, arithmetic and copies ran while one was open for 0% of the time, Pallas kernels for 5%

profile of v4, /device:TPU:1, one launch (start us, length us, event | category | flops | bytes accessed | tf_op | source)
XLA Modules:
  0.0 127.7 jit_solution(6309026275443382506)
XLA Ops:
  0.0 0.0 copy-start.7
  0.0 0.0 copy-start
  0.0 0.0 copy-start.5
  0.0 0.0 copy-start.6
  0.0 0.0 copy-start.1
  0.0 0.0 copy-start.2
  0.0 3.1 %shard_map.119 = bf16[128,16,128]{2,1,0:T(8,128)(2,1)} custom-call(s32[8]{0:T(128)} %lengths_h.1, bf16[64,128,128]{2,1,0:T(8,128)(2,1)} %pair_b.1, f32[1,128]{1,0:T(1,128)} %bitcast.13, f32[1,128]{1,0:T(1,128)} %bitcast.16, bf16[128,128]{1,0:T(8,128)(2,1)} %gate_h.1, bf16[128,128]{1,0:T(8,128)(2,1)} %value_h.1), custom_call_target="tpu_custom_call" | custom-call | tf_op jit(solution)/shard_map/pallas_call | solution.py:135
  3.1 17.1 %all-to-all-start.1 = ((bf16[128,16,128]{2,1,0:T(8,128)(2,1)}), bf16[128,16,128]{2,1,0:T(8,128)(2,1)S(1)}, u32[]{:S(2)}, u32[]{:S(2)}) async-start(bf16[128,16,128]{2,1,0:T(8,128)(2,1)} %shard_map.119), calls=%async_computation.1 | async-start | bytes 1048576 | tf_op jit(solution)/shard_map/all_to_all | solution.py:380
  20.3 0.0 copy-done.7
  20.3 0.0 copy-done
  20.3 0.0 copy-done.5
  20.3 0.0 copy-done.6
  20.3 0.0 copy-done.1
  20.3 0.0 copy-done.2
  20.3 5.3 %shard_map.118 = bf16[128,64,128]{2,1,0:T(8,128)(2,1)} custom-call(s32[8]{0:T(128)S(1)} %copy-done.7, bf16[64,128,128]{2,1,0:T(8,128)(2,1)S(1)} %copy-done, f32[1,128]{1,0:T(1,128)S(1)} %bitcast.14, f32[1,128]{1,0:T(1,128)S(1)} %bitcast.17, bf16[128,128]{1,0:T(8,128)(2,1)S(1)} %copy-done.1, bf16[128,128]{1,0:T(8,128)(2,1)S(1)} %copy-done.2), custom_call_target="tpu_custom_call" | custom-call | flops 536870912 | bytes 4194304 | tf_op jit(solution)/shard_map/pallas_call | solution.py:174
  25.7 11.1 %all-to-all-done.1 = bf16[128,16,128]{2,1,0:T(8,128)(2,1)S(1)} async-done(((bf16[128,16,128]{2,1,0:T(8,128)(2,1)}), bf16[128,16,128]{2,1,0:T(8,128)(2,1)S(1)}, u32[]{:S(2)}, u32[]{:S(2)}) %all-to-all-start.1) | async-done | bytes 524320 | tf_op jit(solution)/shard_map/all_to_all | solution.py:380
  36.8 0.0 copy-start.10
  36.8 7.8 %all-to-all-start = ((bf16[128,64,128]{2,1,0:T(8,128)(2,1)}), bf16[128,64,128]{2,1,0:T(8,128)(2,1)}, u32[]{:S(2)}, u32[]{:S(2)}) async-start(bf16[128,64,128]{2,1,0:T(8,128)(2,1)} %shard_map.118), calls=%async_computation | async-start | bytes 4194304 | tf_op jit(solution)/shard_map/all_to_all | solution.py:384
  44.7 3.1 %collective-permute-start = (bf16[128,16,128]{2,1,0:T(8,128)(2,1)S(1)}, bf16[128,16,128]{2,1,0:T(8,128)(2,1)S(1)}, u32[]{:S(2)}, u32[]{:S(2)}) collective-permute-start(bf16[128,16,128]{2,1,0:T(8,128)(2,1)S(1)} %all-to-all-done.1), channel_id=1, source_target_pairs={{0,32},{32,64},{64,96},{96,0},{1,33},{33,65},{65,97},{97,1},{2,34}... | collective-permute-start | bytes 1572872 | tf_op jit(solution)/shard_map/ppermute | solution.py:386
  47.8 4.4 %collective-permute-start.1 = (bf16[128,16,128]{2,1,0:T(8,128)(2,1)S(1)}, bf16[128,16,128]{2,1,0:T(8,128)(2,1)S(1)}, u32[]{:S(2)}, u32[]{:S(2)}) collective-permute-start(bf16[128,16,128]{2,1,0:T(8,128)(2,1)S(1)} %all-to-all-done.1), channel_id=1, source_target_pairs={{0,64},{32,96},{64,0},{96,32},{1,65},{33,97},{65,1},{97,33},{2,66}... | collective-permute-start | bytes 1572872 | tf_op jit(solution)/shard_map/ppermute | solution.py:386
  52.1 3.1 %collective-permute-start.2 = (bf16[128,16,128]{2,1,0:T(8,128)(2,1)S(1)}, bf16[128,16,128]{2,1,0:T(8,128)(2,1)S(1)}, u32[]{:S(2)}, u32[]{:S(2)}) collective-permute-start(bf16[128,16,128]{2,1,0:T(8,128)(2,1)S(1)} %all-to-all-done.1), channel_id=1, source_target_pairs={{0,96},{32,0},{64,32},{96,64},{1,97},{33,1},{65,33},{97,65},{2,98}... | collective-permute-start | bytes 1572872 | tf_op jit(solution)/shard_map/ppermute | solution.py:386
  55.2 4.3 %collective-permute-start.3 = (bf16[128,16,128]{2,1,0:T(8,128)(2,1)S(1)}, bf16[128,16,128]{2,1,0:T(8,128)(2,1)S(1)}, u32[]{:S(2)}, u32[]{:S(2)}) collective-permute-start(bf16[128,16,128]{2,1,0:T(8,128)(2,1)S(1)} %all-to-all-done.1), channel_id=1, source_target_pairs={{0,16},{16,0},{1,17},{17,1},{2,18},{18,2},{3,19},{19,3},{4,20},{20... | collective-permute-start | bytes 1572872 | tf_op jit(solution)/shard_map/ppermute | solution.py:389
  59.6 0.1 collective-permute-done
  59.7 0.0 copy-start.11
  59.7 5.4 %collective-permute-start.4 = (bf16[128,16,128]{2,1,0:T(8,128)(2,1)S(1)}, bf16[128,16,128]{2,1,0:T(8,128)(2,1)S(1)}, u32[]{:S(2)}, u32[]{:S(2)}) collective-permute-start(bf16[128,16,128]{2,1,0:T(8,128)(2,1)S(1)} %collective-permute-done), channel_id=1, source_target_pairs={{0,16},{16,0},{1,17},{17,1},{2,18},{18,2},{3,19},{19,3},{4,20},{20... | collective-permute-start | bytes 1572872 | tf_op jit(solution)/shard_map/ppermute | solution.py:389
  65.1 6.8 %collective-permute-done.1 = bf16[128,16,128]{2,1,0:T(8,128)(2,1)S(1)} collective-permute-done((bf16[128,16,128]{2,1,0:T(8,128)(2,1)S(1)}, bf16[128,16,128]{2,1,0:T(8,128)(2,1)S(1)}, u32[]{:S(2)}, u32[]{:S(2)}) %collective-permute-start.1) | collective-permute-done | bytes 524320 | tf_op jit(solution)/shard_map/ppermute | solution.py:386
  71.9 0.0 copy-start.12
  71.9 4.3 %collective-permute-start.5 = (bf16[128,16,128]{2,1,0:T(8,128)(2,1)S(1)}, bf16[128,16,128]{2,1,0:T(8,128)(2,1)S(1)}, u32[]{:S(2)}, u32[]{:S(2)}) collective-permute-start(bf16[128,16,128]{2,1,0:T(8,128)(2,1)S(1)} %collective-permute-done.1), channel_id=1, source_target_pairs={{0,16},{16,0},{1,17},{17,1},{2,18},{18,2},{3,19},{19,3},{4,20},{20... | collective-permute-start | bytes 1572872 | tf_op jit(solution)/shard_map/ppermute | solution.py:389
  76.2 0.0 collective-permute-done.2
  76.2 0.0 copy-start.13
  76.2 1.9 %collective-permute-start.6 = (bf16[128,16,128]{2,1,0:T(8,128)(2,1)S(1)}, bf16[128,16,128]{2,1,0:T(8,128)(2,1)}, u32[]{:S(2)}, u32[]{:S(2)}) collective-permute-start(bf16[128,16,128]{2,1,0:T(8,128)(2,1)S(1)} %collective-permute-done.2), channel_id=1, source_target_pairs={{0,16},{16,0},{1,17},{17,1},{2,18},{18,2},{3,19},{19,3},{4,20},{20... | collective-permute-start | bytes 1572872 | tf_op jit(solution)/shard_map/ppermute | solution.py:389
  78.2 0.0 collective-permute-done.3
  78.2 0.0 copy-start.14
  78.2 0.0 collective-permute-done.4
  78.2 0.0 copy-done.12
  78.2 0.0 copy-start.15
  78.2 0.0 collective-permute-done.5
  78.2 0.0 copy-done.13
  78.2 0.8 copy-done.14
  79.0 0.1 copy-done.15
  79.1 0.0 copy-start.16
  79.1 0.8 copy-done.16
  79.9 0.2 collective-permute-done.6
  80.2 12.4 %all-to-all-done = bf16[128,64,128]{2,1,0:T(8,128)(2,1)} async-done(((bf16[128,64,128]{2,1,0:T(8,128)(2,1)}), bf16[128,64,128]{2,1,0:T(8,128)(2,1)}, u32[]{:S(2)}, u32[]{:S(2)}) %all-to-all-start) | async-done | bytes 2097184 | tf_op jit(solution)/shard_map/all_to_all | solution.py:384
  92.6 0.0 copy-done.10
  92.6 0.0 copy-done.11
  92.6 0.0 copy-start.3
  92.6 4.7 %shard_map.120 = bf16[4,16,2,16,128]{4,3,2,1,0:T(8,128)(2,1)} custom-call(bf16[4,16,2,64,128]{4,3,2,1,0:T(8,128)(2,1)} %bitcast.2.refs_0_, bf16[4,16,2,16,128]{4,3,2,1,0:T(8,128)(2,1)} %bitcast.19, bf16[4,16,2,16,128]{4,3,2,1,0:T(8,128)(2,1)} %bitcast.20, bf16[4,16,2,16,128]{4,3,2,1,0:T(8,128)(2,1)} %bitcast.21, bf16[4,16,2,16,128]{4,3,2,1,0:T(8,128)(2,1)} %bitcast.22, ...), custom_call_target="tpu_custom_call" | custom-call | tf_op jit(solution)/shard_map/pallas_call | solution.py:259
  97.3 12.0 %all-to-all-start.2 = ((bf16[128,16,128]{2,1,0:T(8,128)(2,1)}), bf16[128,16,128]{2,1,0:T(8,128)(2,1)S(1)}, u32[]{:S(2)}, u32[]{:S(2)}) async-start(bf16[128,16,128]{2,1,0:T(8,128)(2,1)} %bitcast.11), calls=%async_computation.2 | async-start | bytes 1048576 | tf_op jit(solution)/shard_map/all_to_all | solution.py:397
  109.3 0.0 copy-done.3
  109.3 0.0 copy-start.4
  109.3 0.0 copy-start.8
  109.3 0.0 copy-start.9
  109.4 1.0 shard_map.121.gate
  110.3 15.0 %all-to-all-done.2.slab = bf16[128,16,128]{2,1,0:T(8,128)(2,1)S(1)} async-done(((bf16[128,16,128]{2,1,0:T(8,128)(2,1)}), bf16[128,16,128]{2,1,0:T(8,128)(2,1)S(1)}, u32[]{:S(2)}, u32[]{:S(2)}) %all-to-all-start.2) | async-done | bytes 524320 | tf_op jit(solution)/shard_map/all_to_all | solution.py:397
  125.4 0.0 copy-done.4
  125.4 0.0 copy-done.8
  125.4 0.0 copy-done.9
  125.4 2.3 %shard_map.122 = bf16[26,64,128]{2,1,0:T(8,128)(2,1)} custom-call(f32[128]{0:T(128)S(1)} %copy-done.8, f32[128]{0:T(128)S(1)} %copy-done.9, bf16[128,16,128]{2,1,0:T(8,128)(2,1)S(1)} %all-to-all-done.2.slab, f32[26,64,128]{2,1,0:T(8,128)S(1)} %shard_map.121.gate, bf16[128,128]{1,0:T(8,128)(2,1)S(1)} %copy-done.4), custom_call_target="tpu_custom_call" | custom-call | tf_op jit(solution)/shard_map/pallas_call | solution.py:344
Async XLA Ops:
  0.0 20.3 %copy-start.7 = (s32[8]{0:T(128)S(1)}, s32[8]{0:T(128)}, u32[]{:S(2)}) copy-start(s32[8]{0:T(128)} %lengths_h.1) | copy-start | bytes 100
  0.0 20.3 %copy-start = (bf16[64,128,128]{2,1,0:T(8,128)(2,1)S(1)}, bf16[64,128,128]{2,1,0:T(8,128)(2,1)}, u32[]{:S(2)}) copy-start(bf16[64,128,128]{2,1,0:T(8,128)(2,1)} %pair_b.1) | copy-start | bytes 6291460
  0.0 20.3 %copy-start.5 = (f32[128]{0:T(128)S(1)}, f32[128]{0:T(128)}, u32[]{:S(2)}) copy-start(f32[128]{0:T(128)} %param.14) | copy-start | bytes 1540
  0.0 20.3 %copy-start.6 = (f32[128]{0:T(128)S(1)}, f32[128]{0:T(128)}, u32[]{:S(2)}) copy-start(f32[128]{0:T(128)} %param.15) | copy-start | bytes 1540
  0.0 20.3 %copy-start.1 = (bf16[128,128]{1,0:T(8,128)(2,1)S(1)}, bf16[128,128]{1,0:T(8,128)(2,1)}, u32[]{:S(2)}) copy-start(bf16[128,128]{1,0:T(8,128)(2,1)} %gate_w.2) | copy-start | bytes 98308
  0.0 20.3 %copy-start.2 = (bf16[128,128]{1,0:T(8,128)(2,1)S(1)}, bf16[128,128]{1,0:T(8,128)(2,1)}, u32[]{:S(2)}) copy-start(bf16[128,128]{1,0:T(8,128)(2,1)} %value_w.1) | copy-start | bytes 98308
  3.1 33.7 %all-to-all-start.1 = ((bf16[128,16,128]{2,1,0:T(8,128)(2,1)}), bf16[128,16,128]{2,1,0:T(8,128)(2,1)S(1)}, u32[]{:S(2)}, u32[]{:S(2)}) async-start(bf16[128,16,128]{2,1,0:T(8,128)(2,1)} %shard_map.119), calls=%async_computation.1 | async-start | bytes 1048576 | tf_op jit(solution)/shard_map/all_to_all | solution.py:380
  36.8 55.8 %copy-start.10 = (bf16[128,16,128]{2,1,0:T(8,128)(2,1)}, bf16[128,16,128]{2,1,0:T(8,128)(2,1)S(1)}, u32[]{:S(2)}) copy-start(bf16[128,16,128]{2,1,0:T(8,128)(2,1)S(1)} %all-to-all-done.1) | copy-start | bytes 1572868
  36.8 55.8 %all-to-all-start = ((bf16[128,64,128]{2,1,0:T(8,128)(2,1)}), bf16[128,64,128]{2,1,0:T(8,128)(2,1)}, u32[]{:S(2)}, u32[]{:S(2)}) async-start(bf16[128,64,128]{2,1,0:T(8,128)(2,1)} %shard_map.118), calls=%async_computation | async-start | bytes 4194304 | tf_op jit(solution)/shard_map/all_to_all | solution.py:384
  44.7 15.0 %collective-permute-start = (bf16[128,16,128]{2,1,0:T(8,128)(2,1)S(1)}, bf16[128,16,128]{2,1,0:T(8,128)(2,1)S(1)}, u32[]{:S(2)}, u32[]{:S(2)}) collective-permute-start(bf16[128,16,128]{2,1,0:T(8,128)(2,1)S(1)} %all-to-all-done.1), channel_id=1, source_target_pairs={{0,32},{32,64},{64,96},{96,0},{1,33},{33,65},{65,97},{97,1},{2,34}... | collective-permute-start | bytes 1572872 | tf_op jit(solution)/shard_map/ppermute | solution.py:386
  47.8 24.1 %collective-permute-start.1 = (bf16[128,16,128]{2,1,0:T(8,128)(2,1)S(1)}, bf16[128,16,128]{2,1,0:T(8,128)(2,1)S(1)}, u32[]{:S(2)}, u32[]{:S(2)}) collective-permute-start(bf16[128,16,128]{2,1,0:T(8,128)(2,1)S(1)} %all-to-all-done.1), channel_id=1, source_target_pairs={{0,64},{32,96},{64,0},{96,32},{1,65},{33,97},{65,1},{97,33},{2,66}... | collective-permute-start | bytes 1572872 | tf_op jit(solution)/shard_map/ppermute | solution.py:386
  52.1 24.1 %collective-permute-start.2 = (bf16[128,16,128]{2,1,0:T(8,128)(2,1)S(1)}, bf16[128,16,128]{2,1,0:T(8,128)(2,1)S(1)}, u32[]{:S(2)}, u32[]{:S(2)}) collective-permute-start(bf16[128,16,128]{2,1,0:T(8,128)(2,1)S(1)} %all-to-all-done.1), channel_id=1, source_target_pairs={{0,96},{32,0},{64,32},{96,64},{1,97},{33,1},{65,33},{97,65},{2,98}... | collective-permute-start | bytes 1572872 | tf_op jit(solution)/shard_map/ppermute | solution.py:386
  55.2 23.0 %collective-permute-start.3 = (bf16[128,16,128]{2,1,0:T(8,128)(2,1)S(1)}, bf16[128,16,128]{2,1,0:T(8,128)(2,1)S(1)}, u32[]{:S(2)}, u32[]{:S(2)}) collective-permute-start(bf16[128,16,128]{2,1,0:T(8,128)(2,1)S(1)} %all-to-all-done.1), channel_id=1, source_target_pairs={{0,16},{16,0},{1,17},{17,1},{2,18},{18,2},{3,19},{19,3},{4,20},{20... | collective-permute-start | bytes 1572872 | tf_op jit(solution)/shard_map/ppermute | solution.py:389
  59.7 32.9 %copy-start.11 = (bf16[128,16,128]{2,1,0:T(8,128)(2,1)}, bf16[128,16,128]{2,1,0:T(8,128)(2,1)S(1)}, u32[]{:S(2)}) copy-start(bf16[128,16,128]{2,1,0:T(8,128)(2,1)S(1)} %collective-permute-done) | copy-start | bytes 1572868
  59.7 18.5 %collective-permute-start.4 = (bf16[128,16,128]{2,1,0:T(8,128)(2,1)S(1)}, bf16[128,16,128]{2,1,0:T(8,128)(2,1)S(1)}, u32[]{:S(2)}, u32[]{:S(2)}) collective-permute-start(bf16[128,16,128]{2,1,0:T(8,128)(2,1)S(1)} %collective-permute-done), channel_id=1, source_target_pairs={{0,16},{16,0},{1,17},{17,1},{2,18},{18,2},{3,19},{19,3},{4,20},{20... | collective-permute-start | bytes 1572872 | tf_op jit(solution)/shard_map/ppermute | solution.py:389
  71.9 6.3 %copy-start.12 = (bf16[128,16,128]{2,1,0:T(8,128)(2,1)}, bf16[128,16,128]{2,1,0:T(8,128)(2,1)S(1)}, u32[]{:S(2)}) copy-start(bf16[128,16,128]{2,1,0:T(8,128)(2,1)S(1)} %collective-permute-done.1) | copy-start | bytes 1572868
  71.9 6.3 %collective-permute-start.5 = (bf16[128,16,128]{2,1,0:T(8,128)(2,1)S(1)}, bf16[128,16,128]{2,1,0:T(8,128)(2,1)S(1)}, u32[]{:S(2)}, u32[]{:S(2)}) collective-permute-start(bf16[128,16,128]{2,1,0:T(8,128)(2,1)S(1)} %collective-permute-done.1), channel_id=1, source_target_pairs={{0,16},{16,0},{1,17},{17,1},{2,18},{18,2},{3,19},{19,3},{4,20},{20... | collective-permute-start | bytes 1572872 | tf_op jit(solution)/shard_map/ppermute | solution.py:389
  76.2 2.0 %copy-start.13 = (bf16[128,16,128]{2,1,0:T(8,128)(2,1)}, bf16[128,16,128]{2,1,0:T(8,128)(2,1)S(1)}, u32[]{:S(2)}) copy-start(bf16[128,16,128]{2,1,0:T(8,128)(2,1)S(1)} %collective-permute-done.2) | copy-start | bytes 1572868
  76.2 3.9 %collective-permute-start.6 = (bf16[128,16,128]{2,1,0:T(8,128)(2,1)S(1)}, bf16[128,16,128]{2,1,0:T(8,128)(2,1)}, u32[]{:S(2)}, u32[]{:S(2)}) collective-permute-start(bf16[128,16,128]{2,1,0:T(8,128)(2,1)S(1)} %collective-permute-done.2), channel_id=1, source_target_pairs={{0,16},{16,0},{1,17},{17,1},{2,18},{18,2},{3,19},{19,3},{4,20},{20... | collective-permute-start | bytes 1572872 | tf_op jit(solution)/shard_map/ppermute | solution.py:389
  78.2 0.8 copy-start.14
  78.2 0.9 copy-start.15
  79.1 0.8 copy-start.16
  92.6 16.7 %copy-start.3 = (bf16[128,128]{1,0:T(8,128)(2,1)S(1)}, bf16[128,128]{1,0:T(8,128)(2,1)}, u32[]{:S(2)}) copy-start(bf16[128,128]{1,0:T(8,128)(2,1)} %gate_w.3) | copy-start | bytes 98308
  97.3 28.1 %all-to-all-start.2 = ((bf16[128,16,128]{2,1,0:T(8,128)(2,1)}), bf16[128,16,128]{2,1,0:T(8,128)(2,1)S(1)}, u32[]{:S(2)}, u32[]{:S(2)}) async-start(bf16[128,16,128]{2,1,0:T(8,128)(2,1)} %bitcast.11), calls=%async_computation.2 | async-start | bytes 1048576 | tf_op jit(solution)/shard_map/all_to_all | solution.py:397
  109.3 16.0 %copy-start.4 = (bf16[128,128]{1,0:T(8,128)(2,1)S(1)}, bf16[128,128]{1,0:T(8,128)(2,1)}, u32[]{:S(2)}) copy-start(bf16[128,128]{1,0:T(8,128)(2,1)} %out_w.1) | copy-start | bytes 98308
  109.3 16.0 %copy-start.8 = (f32[128]{0:T(128)S(1)}, f32[128]{0:T(128)}, u32[]{:S(2)}) copy-start(f32[128]{0:T(128)} %out_gain.1) | copy-start | bytes 1540
  109.3 16.0 %copy-start.9 = (f32[128]{0:T(128)S(1)}, f32[128]{0:T(128)}, u32[]{:S(2)}) copy-start(f32[128]{0:T(128)} %out_bias.1) | copy-start | bytes 1540

commit v5 on v4

--- a/solution.py
+++ b/solution.py
@@ -12,7 +12,7 @@
 PAD = 16
 BATCH = 4
 AXES = (("yh", 4), ("x", 4), ("core", 2), ("z", 8), ("yl", 2))
-SPREAD = ("yh", "z", "yl")
+SPREAD = ("yl", "z", "yh")
 RING = "x"
 
 epsilon = 1e-05
@@ -198,27 +198,27 @@
     count = 1 + 2 * ring
     sources, out, acc, sems, held = refs[:count], *refs[count : count + 3], refs[count + 3 :]
     left = held[0]
-    groups, chans, hidden, rows, cols = left.shape
+    chans, groups, hidden, rows, cols = left.shape
     paired = [held[1 + part * ring + d] for d in range(ring) for part in range(2)]
     half = chans // 2
     waves = [
         fetch(
             sems.at[h],
             *[
-                (a.at[:, pl.ds(h * half, half)], b.at[:, pl.ds(h * half, half)])
+                (a.at[pl.ds(h * half, half)], b.at[pl.ds(h * half, half)])
                 for a, b in zip(sources, held)
             ],
         )
         for h in range(2)
     ]
-    me, core = where()
+    me, core, split = where()
     low = lax.broadcasted_iota(jnp.int32, (PAD, 2 * rows), 1) < rows
     wide = 2
 
     def side(parts, first, ch):
         pieces = []
         for c in range(first, first + wide):
-            tiles = [part[:, c, ch] for part in parts]
+            tiles = [part[c, :, ch] for part in parts]
             height = tiles[0].shape[0] * tiles[0].shape[1]
             pieces.append(jnp.concatenate([t.reshape(height, cols) for t in tiles], axis=0))
         return jnp.concatenate(pieces, axis=1)
@@ -238,29 +238,34 @@
         for d in range(ring):
             member = lax.rem(me + ring - d, ring)
             for q in range(groups):
+                piece = q * ring + member
+                spot = lax.rem(piece, split) * (chans // split) + piece // split
                 upper = acc.at[ch, d, core, q]
                 lower = acc.at[ch, d, 1 - core, q]
                 for g in range(0, groups, 2):
                     span = pl.ds(g * rows, 2 * rows)
                     u, v = upper[:, span], lower[:, span]
-                    spot = q * ring + member
-                    out[g, spot, ch] = jnp.where(low, u, pltpu.roll(v, rows, 1)).astype(
+                    out[spot, g, ch] = jnp.where(low, u, pltpu.roll(v, rows, 1)).astype(
                         jnp.bfloat16
                     )
-                    out[g + 1, spot, ch] = jnp.where(low, pltpu.roll(u, rows, 1), v).astype(
+                    out[spot, g + 1, ch] = jnp.where(low, pltpu.roll(u, rows, 1), v).astype(
                         jnp.bfloat16
                     )
 
 
-def product_of(left, own, other, where=lambda: (lax.axis_index(RING), lax.axis_index("core"))):
-    groups, chans, hidden, rows, cols = left.shape
+def product_place():
+    return lax.axis_index(RING), lax.axis_index("core"), lax.axis_size("yl")
+
+
+def product_of(left, own, other, where=product_place):
+    chans, groups, hidden, rows, cols = left.shape
     ring = len(own)
     arrays = (left, *own, *other)
     return pl.pallas_call(
         functools.partial(product_kernel, ring, where),
         in_specs=[pl.BlockSpec(memory_space=pltpu.HBM)] * len(arrays),
         out_specs=pl.BlockSpec(memory_space=pltpu.VMEM),
-        out_shape=jax.ShapeDtypeStruct((groups, chans, hidden, PAD, 2 * rows), jnp.bfloat16),
+        out_shape=jax.ShapeDtypeStruct((chans, groups, hidden, PAD, 2 * rows), jnp.bfloat16),
         scratch_shapes=[
             pltpu.VMEM((hidden, ring, 2, groups, PAD, groups * rows), jnp.float32),
             pltpu.SemaphoreType.DMA((2, len(arrays))),
@@ -388,7 +393,8 @@
     ]
     other = [lax.ppermute(part, "core", [(0, 1), (1, 0)]) for part in own]
     gate = gate_of(pair_repr, gain, bias, gate_weight)
-    shape = (groups, chans, hidden // (groups * chans))
+    gate, own[0] = lax.optimization_barrier((gate, own[0]))
+    shape = (chans, groups, hidden // (groups * chans))
     product = product_of(
         left.reshape(*shape, rows, cols),
         [part.reshape(*shape, PAD, cols) for part in own],

time: 130 us -> 129 us (level)
  the two profiles are of different devices: /device:TPU:1 before, /device:TPU:4 now
where the time goes in v5:
time: 129 us; the launch traced here: 128 us
  waiting for transfers between devices  45.6 us (35%)
  starting transfers between devices  38.7 us (30%)
  blocking collectives  26.1 us (20%)
  Pallas kernels  15.7 us (12%)
  local copies, waits for them, and re-layouts  1.78 us (1%)
    all_to_all x1, blocking collectives, on_device(): lax.all_to_all(product.reshape(hidden, PAD, 2 * rows), SPREAD, 0, 0, tile...  26.1 us
    all_to_all x1, waiting for transfers between devices, on_device(): left = lax.all_to_all(left, SPREAD, 0, 0, tiled=True)  16.6 us
    all_to_all x1, starting transfers between devices, on_device(): right = lax.all_to_all(right, SPREAD, 0, 0, tiled=True)  16.6 us
    ppermute x3, waiting for transfers between devices, on_device(): lax.ppermute(right, RING, [(n, (n + d) % ring) for n in range(ring)])  15.1 us
    all_to_all x1, waiting for transfers between devices, on_device(): right = lax.all_to_all(right, SPREAD, 0, 0, tiled=True)  14 us
    ppermute x3, starting transfers between devices, on_device(): lax.ppermute(right, RING, [(n, (n + d) % ring) for n in range(ring)])  8.86 us
    ppermute x4, starting transfers between devices, on_device(): other = [lax.ppermute(part, 'core', [(0, 1), (1, 0)]) for part in own]  7.65 us
    all_to_all x1, starting transfers between devices, on_device(): left = lax.all_to_all(left, SPREAD, 0, 0, tiled=True)  5.56 us
  transfers between devices with their start and end apart: 9, of which 5 were waited for; matrix products, arithmetic and copies ran while one was open for 0% of the time, Pallas kernels for 5%

profile of v5, /device:TPU:4, one launch (start us, length us, event | category | flops | bytes accessed | tf_op | source)
XLA Modules:
  0.0 128.1 jit_solution(9185605788737791848)
XLA Ops:
  0.0 0.0 copy-start.7
  0.0 0.0 copy-start
  0.0 0.0 copy-start.5
  0.0 0.0 copy-start.6
  0.0 0.0 copy-start.1
  0.0 0.0 copy-start.2
  0.0 3.1 %shard_map.120 = bf16[128,16,128]{2,1,0:T(8,128)(2,1)} custom-call(s32[8]{0:T(128)} %lengths_h.1, bf16[64,128,128]{2,1,0:T(8,128)(2,1)} %pair_h.1, f32[1,128]{1,0:T(1,128)} %bitcast.14, f32[1,128]{1,0:T(1,128)} %bitcast.17, bf16[128,128]{1,0:T(8,128)(2,1)} %gate_h.1, bf16[128,128]{1,0:T(8,128)(2,1)} %value_h.1), custom_call_target="tpu_custom_call" | custom-call | tf_op jit(solution)/shard_map/pallas_call | solution.py:135
  3.1 16.6 %all-to-all-start.1 = ((bf16[128,16,128]{2,1,0:T(8,128)(2,1)}), bf16[128,16,128]{2,1,0:T(8,128)(2,1)S(1)}, u32[]{:S(2)}, u32[]{:S(2)}) async-start(bf16[128,16,128]{2,1,0:T(8,128)(2,1)} %shard_map.120), calls=%async_computation.1 | async-start | bytes 1048576 | tf_op jit(solution)/shard_map/all_to_all | solution.py:385
  19.7 0.0 copy-done.7
  19.7 0.0 copy-done
  19.7 0.0 copy-done.5
  19.8 0.0 copy-done.6
  19.8 0.0 copy-done.1
  19.8 0.0 copy-done.2
  19.8 5.4 %shard_map.118 = bf16[128,64,128]{2,1,0:T(8,128)(2,1)} custom-call(s32[8]{0:T(128)S(1)} %copy-done.7, bf16[64,128,128]{2,1,0:T(8,128)(2,1)S(1)} %copy-done, f32[1,128]{1,0:T(1,128)S(1)} %bitcast.15, f32[1,128]{1,0:T(1,128)S(1)} %bitcast.18, bf16[128,128]{1,0:T(8,128)(2,1)S(1)} %copy-done.1, bf16[128,128]{1,0:T(8,128)(2,1)S(1)} %copy-done.2), custom_call_target="tpu_custom_call" | custom-call | flops 536870912 | bytes 4194304 | tf_op jit(solution)/shard_map/pallas_call | solution.py:174
  25.2 0.0 copy-start.3
  25.2 14.0 %all-to-all-done.1 = bf16[128,16,128]{2,1,0:T(8,128)(2,1)S(1)} async-done(((bf16[128,16,128]{2,1,0:T(8,128)(2,1)}), bf16[128,16,128]{2,1,0:T(8,128)(2,1)S(1)}, u32[]{:S(2)}, u32[]{:S(2)}) %all-to-all-start.1) | async-done | bytes 524320 | tf_op jit(solution)/shard_map/all_to_all | solution.py:385
  39.1 0.0 copy-start.10
  39.1 5.6 %all-to-all-start = ((bf16[128,64,128]{2,1,0:T(8,128)(2,1)}), bf16[128,64,128]{2,1,0:T(8,128)(2,1)}, u32[]{:S(2)}, u32[]{:S(2)}) async-start(bf16[128,64,128]{2,1,0:T(8,128)(2,1)} %shard_map.118), calls=%async_computation | async-start | bytes 4194304 | tf_op jit(solution)/shard_map/all_to_all | solution.py:389
  44.7 3.1 %collective-permute-start = (bf16[128,16,128]{2,1,0:T(8,128)(2,1)S(1)}, bf16[128,16,128]{2,1,0:T(8,128)(2,1)S(1)}, u32[]{:S(2)}, u32[]{:S(2)}) collective-permute-start(bf16[128,16,128]{2,1,0:T(8,128)(2,1)S(1)} %all-to-all-done.1), channel_id=1, source_target_pairs={{0,32},{32,64},{64,96},{96,0},{1,33},{33,65},{65,97},{97,1},{2,34}... | collective-permute-start | bytes 1572872 | tf_op jit(solution)/shard_map/ppermute | solution.py:391
  47.8 2.7 %collective-permute-start.1 = (bf16[128,16,128]{2,1,0:T(8,128)(2,1)S(1)}, bf16[128,16,128]{2,1,0:T(8,128)(2,1)S(1)}, u32[]{:S(2)}, u32[]{:S(2)}) collective-permute-start(bf16[128,16,128]{2,1,0:T(8,128)(2,1)S(1)} %all-to-all-done.1), channel_id=1, source_target_pairs={{0,64},{32,96},{64,0},{96,32},{1,65},{33,97},{65,1},{97,33},{2,66}... | collective-permute-start | bytes 1572872 | tf_op jit(solution)/shard_map/ppermute | solution.py:391
  50.5 3.1 %collective-permute-start.2 = (bf16[128,16,128]{2,1,0:T(8,128)(2,1)S(1)}, bf16[128,16,128]{2,1,0:T(8,128)(2,1)S(1)}, u32[]{:S(2)}, u32[]{:S(2)}) collective-permute-start(bf16[128,16,128]{2,1,0:T(8,128)(2,1)S(1)} %all-to-all-done.1), channel_id=1, source_target_pairs={{0,96},{32,0},{64,32},{96,64},{1,97},{33,1},{65,33},{97,65},{2,98}... | collective-permute-start | bytes 1572872 | tf_op jit(solution)/shard_map/ppermute | solution.py:391
  53.6 1.9 %collective-permute-start.3 = (bf16[128,16,128]{2,1,0:T(8,128)(2,1)S(1)}, bf16[128,16,128]{2,1,0:T(8,128)(2,1)S(1)}, u32[]{:S(2)}, u32[]{:S(2)}) collective-permute-start(bf16[128,16,128]{2,1,0:T(8,128)(2,1)S(1)} %all-to-all-done.1), channel_id=1, source_target_pairs={{0,16},{16,0},{1,17},{17,1},{2,18},{18,2},{3,19},{19,3},{4,20},{20... | collective-permute-start | bytes 1572872 | tf_op jit(solution)/shard_map/ppermute | solution.py:394
  55.5 6.0 %collective-permute-done = bf16[128,16,128]{2,1,0:T(8,128)(2,1)S(1)} collective-permute-done((bf16[128,16,128]{2,1,0:T(8,128)(2,1)S(1)}, bf16[128,16,128]{2,1,0:T(8,128)(2,1)S(1)}, u32[]{:S(2)}, u32[]{:S(2)}) %collective-permute-start) | collective-permute-done | bytes 524320 | tf_op jit(solution)/shard_map/ppermute | solution.py:391
  61.5 0.0 copy-start.11
  61.5 1.9 %collective-permute-start.4 = (bf16[128,16,128]{2,1,0:T(8,128)(2,1)S(1)}, bf16[128,16,128]{2,1,0:T(8,128)(2,1)S(1)}, u32[]{:S(2)}, u32[]{:S(2)}) collective-permute-start(bf16[128,16,128]{2,1,0:T(8,128)(2,1)S(1)} %collective-permute-done), channel_id=1, source_target_pairs={{0,16},{16,0},{1,17},{17,1},{2,18},{18,2},{3,19},{19,3},{4,20},{20... | collective-permute-start | bytes 1572872 | tf_op jit(solution)/shard_map/ppermute | solution.py:394
  63.4 7.3 %collective-permute-done.1 = bf16[128,16,128]{2,1,0:T(8,128)(2,1)S(1)} collective-permute-done((bf16[128,16,128]{2,1,0:T(8,128)(2,1)S(1)}, bf16[128,16,128]{2,1,0:T(8,128)(2,1)S(1)}, u32[]{:S(2)}, u32[]{:S(2)}) %collective-permute-start.1) | collective-permute-done | bytes 524320 | tf_op jit(solution)/shard_map/ppermute | solution.py:391
  70.7 0.0 copy-start.12
  70.7 1.9 %collective-permute-start.5 = (bf16[128,16,128]{2,1,0:T(8,128)(2,1)S(1)}, bf16[128,16,128]{2,1,0:T(8,128)(2,1)S(1)}, u32[]{:S(2)}, u32[]{:S(2)}) collective-permute-start(bf16[128,16,128]{2,1,0:T(8,128)(2,1)S(1)} %collective-permute-done.1), channel_id=1, source_target_pairs={{0,16},{16,0},{1,17},{17,1},{2,18},{18,2},{3,19},{19,3},{4,20},{20... | collective-permute-start | bytes 1572872 | tf_op jit(solution)/shard_map/ppermute | solution.py:394
  72.6 1.8 %collective-permute-done.2 = bf16[128,16,128]{2,1,0:T(8,128)(2,1)S(1)} collective-permute-done((bf16[128,16,128]{2,1,0:T(8,128)(2,1)S(1)}, bf16[128,16,128]{2,1,0:T(8,128)(2,1)S(1)}, u32[]{:S(2)}, u32[]{:S(2)}) %collective-permute-start.2) | collective-permute-done | bytes 524320 | tf_op jit(solution)/shard_map/ppermute | solution.py:391
  74.4 0.0 copy-start.13
  74.4 1.9 %collective-permute-start.6 = (bf16[128,16,128]{2,1,0:T(8,128)(2,1)S(1)}, bf16[128,16,128]{2,1,0:T(8,128)(2,1)}, u32[]{:S(2)}, u32[]{:S(2)}) collective-permute-start(bf16[128,16,128]{2,1,0:T(8,128)(2,1)S(1)} %collective-permute-done.2), channel_id=1, source_target_pairs={{0,16},{16,0},{1,17},{17,1},{2,18},{18,2},{3,19},{19,3},{4,20},{20... | collective-permute-start | bytes 1572872 | tf_op jit(solution)/shard_map/ppermute | solution.py:394
  76.3 0.0 copy-done.3
  76.3 1.0 shard_map.119.gate
  77.3 0.0 copy-done.10
  77.3 0.0 copy-done.11
  77.3 0.0 copy-done.12
  77.3 0.0 copy-done.13
  77.3 0.0 collective-permute-done.3
  77.4 0.0 copy-start.14
  77.4 0.0 collective-permute-done.4
  77.4 0.0 copy-start.15
  77.4 0.0 collective-permute-done.5
  77.4 0.8 copy-done.14
  78.2 0.2 copy-done.15
  78.3 0.0 copy-start.16
  78.3 0.8 copy-done.16
  79.1 0.0 collective-permute-done.6
  79.1 16.6 %all-to-all-done = bf16[128,64,128]{2,1,0:T(8,128)(2,1)} async-done(((bf16[128,64,128]{2,1,0:T(8,128)(2,1)}), bf16[128,64,128]{2,1,0:T(8,128)(2,1)}, u32[]{:S(2)}, u32[]{:S(2)}) %all-to-all-start) | async-done | bytes 2097184 | tf_op jit(solution)/shard_map/all_to_all | solution.py:389
  95.7 0.0 copy-start.4
  95.7 0.0 copy-start.8
  95.7 0.0 copy-start.9
  95.7 3.9 %shard_map.121 = bf16[16,4,2,16,128]{4,3,2,1,0:T(8,128)(2,1)S(1)} custom-call(bf16[16,4,2,64,128]{4,3,2,1,0:T(8,128)(2,1)} %bitcast.2.refs_0_, bf16[16,4,2,16,128]{4,3,2,1,0:T(8,128)(2,1)} %bitcast.20, bf16[16,4,2,16,128]{4,3,2,1,0:T(8,128)(2,1)} %bitcast.21, bf16[16,4,2,16,128]{4,3,2,1,0:T(8,128)(2,1)} %bitcast.22, bf16[16,4,2,16,128]{4,3,2,1,0:T(8,128)(2,1)} %bitcast.23, ...), custom_call_target="tpu_custom_call" | custom-call | tf_op jit(solution)/shard_map/pallas_call | solution.py:264
  99.7 26.1 %all_to_all.15.slab = bf16[128,16,128]{2,1,0:T(8,128)(2,1)S(1)} all-to-all(bf16[128,16,128]{2,1,0:T(8,128)(2,1)S(1)} %bitcast.13), channel_id=1, replica_groups=mesh['yh'=4,'x'=4,'core'=2,'z'=8,'yl'=2] {'yl','z','yh'}, dimensions={0} | all-to-all | bytes 1048576 | tf_op jit(solution)/shard_map/all_to_all | solution.py:403
  125.8 0.0 copy-done.4
  125.8 0.0 copy-done.8
  125.8 0.0 copy-done.9
  125.8 2.3 %shard_map.122 = bf16[26,64,128]{2,1,0:T(8,128)(2,1)} custom-call(f32[128]{0:T(128)S(1)} %copy-done.8, f32[128]{0:T(128)S(1)} %copy-done.9, bf16[128,16,128]{2,1,0:T(8,128)(2,1)S(1)} %all_to_all.15.slab, f32[26,64,128]{2,1,0:T(8,128)S(1)} %shard_map.119.gate, bf16[128,128]{1,0:T(8,128)(2,1)S(1)} %copy-done.4), custom_call_target="tpu_custom_call" | custom-call | tf_op jit(solution)/shard_map/pallas_call | solution.py:349
Async XLA Ops:
  0.0 19.7 %copy-start.7 = (s32[8]{0:T(128)S(1)}, s32[8]{0:T(128)}, u32[]{:S(2)}) copy-start(s32[8]{0:T(128)} %lengths_h.1) | copy-start | bytes 100
  0.0 19.7 %copy-start = (bf16[64,128,128]{2,1,0:T(8,128)(2,1)S(1)}, bf16[64,128,128]{2,1,0:T(8,128)(2,1)}, u32[]{:S(2)}) copy-start(bf16[64,128,128]{2,1,0:T(8,128)(2,1)} %pair_h.1) | copy-start | bytes 6291460
  0.0 19.7 %copy-start.5 = (f32[128]{0:T(128)S(1)}, f32[128]{0:T(128)}, u32[]{:S(2)}) copy-start(f32[128]{0:T(128)} %param.14) | copy-start | bytes 1540
  0.0 19.8 %copy-start.6 = (f32[128]{0:T(128)S(1)}, f32[128]{0:T(128)}, u32[]{:S(2)}) copy-start(f32[128]{0:T(128)} %param.15) | copy-start | bytes 1540
  0.0 19.8 %copy-start.1 = (bf16[128,128]{1,0:T(8,128)(2,1)S(1)}, bf16[128,128]{1,0:T(8,128)(2,1)}, u32[]{:S(2)}) copy-start(bf16[128,128]{1,0:T(8,128)(2,1)} %gate_w.2) | copy-start | bytes 98308
  0.0 19.8 %copy-start.2 = (bf16[128,128]{1,0:T(8,128)(2,1)S(1)}, bf16[128,128]{1,0:T(8,128)(2,1)}, u32[]{:S(2)}) copy-start(bf16[128,128]{1,0:T(8,128)(2,1)} %value_w.1) | copy-start | bytes 98308
  3.1 36.0 %all-to-all-start.1 = ((bf16[128,16,128]{2,1,0:T(8,128)(2,1)}), bf16[128,16,128]{2,1,0:T(8,128)(2,1)S(1)}, u32[]{:S(2)}, u32[]{:S(2)}) async-start(bf16[128,16,128]{2,1,0:T(8,128)(2,1)} %shard_map.120), calls=%async_computation.1 | async-start | bytes 1048576 | tf_op jit(solution)/shard_map/all_to_all | solution.py:385
  25.2 51.2 %copy-start.3 = (bf16[128,128]{1,0:T(8,128)(2,1)S(1)}, bf16[128,128]{1,0:T(8,128)(2,1)}, u32[]{:S(2)}) copy-start(bf16[128,128]{1,0:T(8,128)(2,1)} %gate_w.3) | copy-start | bytes 98308
  39.1 38.2 %copy-start.10 = (bf16[128,16,128]{2,1,0:T(8,128)(2,1)}, bf16[128,16,128]{2,1,0:T(8,128)(2,1)S(1)}, u32[]{:S(2)}) copy-start(bf16[128,16,128]{2,1,0:T(8,128)(2,1)S(1)} %all-to-all-done.1) | copy-start | bytes 1572868
  39.1 56.6 %all-to-all-start = ((bf16[128,64,128]{2,1,0:T(8,128)(2,1)}), bf16[128,64,128]{2,1,0:T(8,128)(2,1)}, u32[]{:S(2)}, u32[]{:S(2)}) async-start(bf16[128,64,128]{2,1,0:T(8,128)(2,1)} %shard_map.118), calls=%async_computation | async-start | bytes 4194304 | tf_op jit(solution)/shard_map/all_to_all | solution.py:389
  44.7 16.8 %collective-permute-start = (bf16[128,16,128]{2,1,0:T(8,128)(2,1)S(1)}, bf16[128,16,128]{2,1,0:T(8,128)(2,1)S(1)}, u32[]{:S(2)}, u32[]{:S(2)}) collective-permute-start(bf16[128,16,128]{2,1,0:T(8,128)(2,1)S(1)} %all-to-all-done.1), channel_id=1, source_target_pairs={{0,32},{32,64},{64,96},{96,0},{1,33},{33,65},{65,97},{97,1},{2,34}... | collective-permute-start | bytes 1572872 | tf_op jit(solution)/shard_map/ppermute | solution.py:391
  47.8 22.9 %collective-permute-start.1 = (bf16[128,16,128]{2,1,0:T(8,128)(2,1)S(1)}, bf16[128,16,128]{2,1,0:T(8,128)(2,1)S(1)}, u32[]{:S(2)}, u32[]{:S(2)}) collective-permute-start(bf16[128,16,128]{2,1,0:T(8,128)(2,1)S(1)} %all-to-all-done.1), channel_id=1, source_target_pairs={{0,64},{32,96},{64,0},{96,32},{1,65},{33,97},{65,1},{97,33},{2,66}... | collective-permute-start | bytes 1572872 | tf_op jit(solution)/shard_map/ppermute | solution.py:391
  50.5 23.9 %collective-permute-start.2 = (bf16[128,16,128]{2,1,0:T(8,128)(2,1)S(1)}, bf16[128,16,128]{2,1,0:T(8,128)(2,1)S(1)}, u32[]{:S(2)}, u32[]{:S(2)}) collective-permute-start(bf16[128,16,128]{2,1,0:T(8,128)(2,1)S(1)} %all-to-all-done.1), channel_id=1, source_target_pairs={{0,96},{32,0},{64,32},{96,64},{1,97},{33,1},{65,33},{97,65},{2,98}... | collective-permute-start | bytes 1572872 | tf_op jit(solution)/shard_map/ppermute | solution.py:391
  53.6 23.8 %collective-permute-start.3 = (bf16[128,16,128]{2,1,0:T(8,128)(2,1)S(1)}, bf16[128,16,128]{2,1,0:T(8,128)(2,1)S(1)}, u32[]{:S(2)}, u32[]{:S(2)}) collective-permute-start(bf16[128,16,128]{2,1,0:T(8,128)(2,1)S(1)} %all-to-all-done.1), channel_id=1, source_target_pairs={{0,16},{16,0},{1,17},{17,1},{2,18},{18,2},{3,19},{19,3},{4,20},{20... | collective-permute-start | bytes 1572872 | tf_op jit(solution)/shard_map/ppermute | solution.py:394
  61.5 15.9 %copy-start.11 = (bf16[128,16,128]{2,1,0:T(8,128)(2,1)}, bf16[128,16,128]{2,1,0:T(8,128)(2,1)S(1)}, u32[]{:S(2)}) copy-start(bf16[128,16,128]{2,1,0:T(8,128)(2,1)S(1)} %collective-permute-done) | copy-start | bytes 1572868
  61.5 15.9 %collective-permute-start.4 = (bf16[128,16,128]{2,1,0:T(8,128)(2,1)S(1)}, bf16[128,16,128]{2,1,0:T(8,128)(2,1)S(1)}, u32[]{:S(2)}, u32[]{:S(2)}) collective-permute-start(bf16[128,16,128]{2,1,0:T(8,128)(2,1)S(1)} %collective-permute-done), channel_id=1, source_target_pairs={{0,16},{16,0},{1,17},{17,1},{2,18},{18,2},{3,19},{19,3},{4,20},{20... | collective-permute-start | bytes 1572872 | tf_op jit(solution)/shard_map/ppermute | solution.py:394
  70.7 6.7 %copy-start.12 = (bf16[128,16,128]{2,1,0:T(8,128)(2,1)}, bf16[128,16,128]{2,1,0:T(8,128)(2,1)S(1)}, u32[]{:S(2)}) copy-start(bf16[128,16,128]{2,1,0:T(8,128)(2,1)S(1)} %collective-permute-done.1) | copy-start | bytes 1572868
  70.7 6.7 %collective-permute-start.5 = (bf16[128,16,128]{2,1,0:T(8,128)(2,1)S(1)}, bf16[128,16,128]{2,1,0:T(8,128)(2,1)S(1)}, u32[]{:S(2)}, u32[]{:S(2)}) collective-permute-start(bf16[128,16,128]{2,1,0:T(8,128)(2,1)S(1)} %collective-permute-done.1), channel_id=1, source_target_pairs={{0,16},{16,0},{1,17},{17,1},{2,18},{18,2},{3,19},{19,3},{4,20},{20... | collective-permute-start | bytes 1572872 | tf_op jit(solution)/shard_map/ppermute | solution.py:394
  74.4 2.9 %copy-start.13 = (bf16[128,16,128]{2,1,0:T(8,128)(2,1)}, bf16[128,16,128]{2,1,0:T(8,128)(2,1)S(1)}, u32[]{:S(2)}) copy-start(bf16[128,16,128]{2,1,0:T(8,128)(2,1)S(1)} %collective-permute-done.2) | copy-start | bytes 1572868
  74.4 4.7 %collective-permute-start.6 = (bf16[128,16,128]{2,1,0:T(8,128)(2,1)S(1)}, bf16[128,16,128]{2,1,0:T(8,128)(2,1)}, u32[]{:S(2)}, u32[]{:S(2)}) collective-permute-start(bf16[128,16,128]{2,1,0:T(8,128)(2,1)S(1)} %collective-permute-done.2), channel_id=1, source_target_pairs={{0,16},{16,0},{1,17},{17,1},{2,18},{18,2},{3,19},{19,3},{4,20},{20... | collective-permute-start | bytes 1572872 | tf_op jit(solution)/shard_map/ppermute | solution.py:394
  77.4 0.8 copy-start.14
  77.4 0.9 copy-start.15
  78.3 0.8 copy-start.16
  95.7 30.1 %copy-start.4 = (bf16[128,128]{1,0:T(8,128)(2,1)S(1)}, bf16[128,128]{1,0:T(8,128)(2,1)}, u32[]{:S(2)}) copy-start(bf16[128,128]{1,0:T(8,128)(2,1)} %out_w.1) | copy-start | bytes 98308
  95.7 30.1 %copy-start.8 = (f32[128]{0:T(128)S(1)}, f32[128]{0:T(128)}, u32[]{:S(2)}) copy-start(f32[128]{0:T(128)} %out_gain.1) | copy-start | bytes 1540
  95.7 30.1 %copy-start.9 = (f32[128]{0:T(128)S(1)}, f32[128]{0:T(128)}, u32[]{:S(2)}) copy-start(f32[128]{0:T(128)} %out_bias.1) | copy-start | bytes 1540

commit v6 on v5

v6 whole, which is shorter than its diff:
```python
import functools

import jax
import jax.numpy as jnp
from jax import lax
from jax.experimental import pallas as pl
from jax.experimental.pallas import tpu as pltpu
from jax.sharding import Mesh
from jax.sharding import PartitionSpec as P

JD = 13
PAD = 16
BATCH = 4
AXES = (("yh", 4), ("x", 4), ("core", 2), ("z", 8), ("yl", 2))
SPREAD = ("yl", "z", "yh")
RING = "x"

epsilon = 1e-05

dot = functools.partial(lax.dot_general, preferred_element_type=jnp.float32)


def normalize(values, gain_vec, bias_vec):
    centre = jnp.mean(values, axis=-1, keepdims=True)
    centred = values - centre
    spread_sq = jnp.mean(centred * centred, axis=-1, keepdims=True)
    return centred * lax.rsqrt(spread_sq + epsilon) * gain_vec + bias_vec


def place():
    blk = (lax.axis_index("yh") * 4 + lax.axis_index("x")) * 2 + lax.axis_index("core")
    chan = lax.axis_index("z") * 2 + lax.axis_index("yl")
    return blk, chan


def real_left(lengths, start, slot_size):
    return lengths[start // slot_size] - start % slot_size


def spread_rows(ref, per):
    count = ref.shape[0] // per
    return jnp.concatenate([ref[pl.ds(j, count, stride=per), :] for j in range(per)], axis=0)


def columns(vec, like):
    return jnp.broadcast_to(vec[...], like.shape).T


def prepare(gain, bias, gate_w, value_w, stack, scale, shift, per):
    hidden = gate_w.shape[1]
    scale[...] = (gate_w[...].astype(jnp.float32) * 0.5).T
    stack[:hidden] = spread_rows(scale, per).astype(jnp.bfloat16)
    scale[...] = value_w[...].astype(jnp.float32).T
    stack[hidden:] = spread_rows(scale, per).astype(jnp.bfloat16)
    scale[...] = columns(gain, scale)
    shift[...] = columns(bias, shift)


def project_rows(pair, row_count, col_count, stack, scale, shift, store):
    rows, cols, width = pair.shape
    hidden = stack.shape[0] // 2
    col_ids = lax.broadcasted_iota(jnp.int32, (1, cols), 1)
    for start in range(0, rows, BATCH):
        batch = min(BATCH, rows - start)
        flat = pair[start : start + batch].reshape(batch * cols, width)
        values = flat.T.astype(jnp.float32)
        centre = jnp.mean(values, axis=0, keepdims=True)
        centred = values - centre
        spread_sq = jnp.mean(centred * centred, axis=0, keepdims=True)
        scale_all = jnp.concatenate([scale[...]] * batch, axis=1)
        shift_all = jnp.concatenate([shift[...]] * batch, axis=1)
        normed = centred * lax.rsqrt(spread_sq + epsilon) * scale_all + shift_all
        mix = dot(stack[...], normed.astype(jnp.bfloat16), (((1,), (0,)), ((), ())))
        gated = (jnp.tanh(mix[:hidden]) + 1.0) * mix[hidden:]
        for j in range(batch):
            i = start + j
            kept = jnp.where(i < row_count, col_count, 0)
            mask = jnp.where(col_ids < kept, 0.5, 0.0)
            store(i, gated[:, j * cols : (j + 1) * cols] * mask)


def in_hbm(*arrays):
    return [pltpu.with_memory_space_constraint(array, pltpu.HBM) for array in arrays]


def fetch(sems, *copies):
    started = [pltpu.make_async_copy(a, b, sems.at[n]) for n, (a, b) in enumerate(copies)]
    for copy in started:
        copy.start()
    return started


def right_kernel(
    per,
    limit,
    slot_size,
    where,
    lengths_h,
    pair_h,
    gain_h,
    bias_h,
    gate_h,
    value_h,
    out,
    lengths,
    pair,
    gain,
    bias,
    gate_w,
    value_w,
    stack,
    scale,
    shift,
    planes,
    sems,
):
    copies = fetch(
        sems,
        (gate_h, gate_w),
        (value_h, value_w),
        (gain_h, gain),
        (bias_h, bias),
        (lengths_h, lengths),
        (pair_h.at[pl.ds(0, JD)], pair),
    )
    for copy in copies:
        copy.wait()
    blk, chan = where()
    prepare(gain, bias, gate_w, value_w, stack, scale, shift, per)
    row_count = real_left(lengths, blk * limit, slot_size)
    col_count = real_left(lengths, chan * pair.shape[1], slot_size)
    peers = stack.shape[0] // 2 // per

    def store(i, value):
        for j in range(per):
            planes[pl.ds(i * per + j, peers, stride=JD * per), :] = value[
                j * peers : (j + 1) * peers
            ]

    project_rows(pair, row_count, col_count, stack, scale, shift, store)
    out[...] = planes[...].astype(jnp.bfloat16)


def shared_scratch(width, hidden, cols, rows):
    return [
        pltpu.VMEM((2 * hidden, width), jnp.bfloat16),
        pltpu.VMEM((width, cols), jnp.float32),
        pltpu.VMEM((width, cols), jnp.float32),
        pltpu.VMEM((hidden * rows, cols), jnp.float32),
    ]


def project_right(pair, lengths, gain, bias, gate_w, value_w, slot_size, per, where=place):
    rows, cols, width = pair.shape
    hidden = gate_w.shape[1]
    return pl.pallas_call(
        functools.partial(right_kernel, per, rows, slot_size, where),
        in_specs=[pl.BlockSpec(memory_space=pltpu.HBM)] * 6,
        out_specs=pl.BlockSpec((hidden * JD, cols), lambda: (0, 0)),
        out_shape=jax.ShapeDtypeStruct((hidden * JD, cols), jnp.bfloat16),
        scratch_shapes=[
            pltpu.SMEM(lengths.shape, jnp.int32),
            pltpu.VMEM((JD, cols, width), jnp.bfloat16),
            pltpu.VMEM((1, width), jnp.float32),
            pltpu.VMEM((1, width), jnp.float32),
            pltpu.VMEM((width, hidden), jnp.bfloat16),
            pltpu.VMEM((width, hidden), jnp.bfloat16),
            *shared_scratch(width, hidden, cols, JD),
            pltpu.SemaphoreType.DMA((6,)),
        ],
        compiler_params=pltpu.CompilerParams(vmem_limit_bytes=32 << 20),
    )(*in_hbm(lengths, pair, gain, bias, gate_w, value_w))


def left_kernel(
    limit, slot_size, where, lengths, pair, gain, bias, gate_w, value_w, out, stack, scale, shift, planes
):
    step = pl.program_id(0)
    blk, chan = where()

    @pl.when(step == 0)
    def _():
        prepare(gain, bias, gate_w, value_w, stack, scale, shift, 1)

    row_count = real_left(lengths, blk * limit, slot_size) - step * PAD
    col_count = real_left(lengths, chan * pair.shape[1], slot_size)
    rows, cols, _ = pair.shape
    hidden = stack.shape[0] // 2

    def store(i, value):
        planes[pl.ds(i, hidden, stride=rows), :] = value

    project_rows(pair, row_count, col_count, stack, scale, shift, store)
    out[...] = planes[...].reshape(hidden, rows, cols).astype(jnp.bfloat16)


def project_left(pair, lengths, gain, bias, gate_w, value_w, slot_size, where=place):
    rows, cols, width = pair.shape
    hidden = gate_w.shape[1]
    whole = pl.BlockSpec((width, hidden), lambda b: (0, 0))
    vec = pl.BlockSpec((1, width), lambda b: (0, 0))
    return pl.pallas_call(
        functools.partial(left_kernel, rows, slot_size, where),
        grid=(rows // PAD,),
        in_specs=[
            pl.BlockSpec(memory_space=pltpu.SMEM),
            pl.BlockSpec((PAD, cols, width), lambda b: (b, 0, 0)),
            vec,
            vec,
            whole,
            whole,
        ],
        out_specs=pl.BlockSpec((hidden, PAD, cols), lambda b: (0, b, 0)),
        out_shape=pltpu.HBM((hidden, rows, cols), jnp.bfloat16),
        scratch_shapes=shared_scratch(width, hidden, cols, PAD),
        cost_estimate=pl.CostEstimate(
            flops=4 * rows * cols * width * hidden,
            bytes_accessed=4 * rows * cols * width,
            transcendentals=rows * cols * hidden,
        ),
        compiler_params=pltpu.CompilerParams(vmem_limit_bytes=32 << 20),
    )(lengths, pair, gain, bias, gate_w, value_w)


def product_kernel(ring, where, *refs):
    count = 1 + 2 * ring
    left_h, own, other = refs[0], refs[1 : 1 + ring], refs[1 + ring : count]
    out, left, right, acc, stage, sems = refs[count:]
    chans, groups, hidden, rows, cols = left.shape
    height = own[0].shape[1]
    seg = height // groups
    half = chans // 2
    paired = [part for two in zip(own, other) for part in two]
    waves = []
    for h in range(2):
        part = pl.ds(h * half, half)
        waves.append(
            fetch(
                sems.at[h],
                (left_h.at[part], left.at[part]),
                *[
                    (a.at[part], right.at[part, pl.ds(n * height, height)])
                    for n, a in enumerate(paired)
                ],
            )
        )
    me, core, split = where()
    wide = 4
    parity = lax.broadcasted_iota(jnp.int32, (right.shape[1], groups * rows), 0) % hidden
    for h, wave in enumerate(waves):
        for copy in wave:
            copy.wait()
        for first in range(h * half, (h + 1) * half, wide):
            block = range(first, first + wide)
            lhs = jnp.concatenate([right[c] for c in block], axis=1)
            piece = None
            for ch in range(hidden):
                rhs = jnp.concatenate(
                    [left[c, :, ch].reshape(groups * rows, cols) for c in block], axis=1
                )
                part = dot(lhs, rhs, (((1,), (1,)), ((), ())))
                piece = part if piece is None else jnp.where(parity == ch, part, piece)
            if first == 0:
                acc[...] = piece.reshape(acc.shape)
            else:
                acc[...] += piece.reshape(acc.shape)
    low = lax.broadcasted_iota(jnp.int32, (seg, 2 * rows), 1) < rows
    for d in range(ring):
        member = lax.rem(me + ring - d, ring)
        for q in range(groups):
            piece = q * ring + member
            spot = lax.rem(piece, split) * (chans // split) + piece // split
            band = pl.ds(q * seg, seg)
            for g in range(0, groups, 2):
                span = pl.ds(g * rows, 2 * rows)
                u = acc[2 * d + core, band, span]
                v = acc[2 * d + 1 - core, band, span]
                stage[spot, pl.ds(g * seg, seg), :] = jnp.where(low, u, pltpu.roll(v, rows, 1))
                stage[spot, pl.ds((g + 1) * seg, seg), :] = jnp.where(
                    low, pltpu.roll(u, rows, 1), v
                )
    out[...] = stage[...].astype(jnp.bfloat16)


def product_place():
    return lax.axis_index(RING), lax.axis_index("core"), lax.axis_size("yl")


def product_of(left, own, other, where=product_place):
    chans, groups, hidden, rows, cols = left.shape
    ring = len(own)
    height = own[0].shape[1]
    arrays = (left, *own, *other)
    return pl.pallas_call(
        functools.partial(product_kernel, ring, where),
        in_specs=[pl.BlockSpec(memory_space=pltpu.HBM)] * len(arrays),
        out_specs=pl.BlockSpec(memory_space=pltpu.VMEM),
        out_shape=jax.ShapeDtypeStruct((chans, height, 2 * rows), jnp.bfloat16),
        scratch_shapes=[
            pltpu.VMEM(left.shape, jnp.bfloat16),
            pltpu.VMEM((chans, 2 * ring * height, cols), jnp.bfloat16),
            pltpu.VMEM((2 * ring, height, groups * rows), jnp.float32),
            pltpu.VMEM((chans, height, 2 * rows), jnp.float32),
            pltpu.SemaphoreType.DMA((2, len(arrays))),
        ],
        compiler_params=pltpu.CompilerParams(vmem_limit_bytes=48 << 20),
    )(*in_hbm(*arrays))


def gate_kernel(
    per,
    pair_a,
    pair_b,
    gain,
    bias,
    gate_w,
    out_gain,
    out_bias,
    out_w,
    out,
    scale,
    shift,
    weight,
    gate_s,
    turn,
):
    rows, _, width = pair_a.shape
    for h, pair in enumerate((pair_a, pair_b)):
        flat = pair[...].reshape(rows * PAD, width).astype(jnp.float32)
        normed = normalize(flat, gain[...], bias[...]).astype(jnp.bfloat16)
        gate_s[h] = jax.nn.sigmoid(dot(normed, gate_w[...], (((1,), (0,)), ((), ()))))
        for r in range(JD):
            out[h * JD + r] = gate_s[h, pl.ds(r, rows, stride=PAD), :]
    turn[...] = columns(out_gain, turn)
    scale[...] = spread_rows(turn, per)
    turn[...] = columns(out_bias, turn)
    shift[...] = spread_rows(turn, per)
    turn[...] = out_w[...].astype(jnp.float32)
    weight[...] = spread_rows(turn, per).astype(jnp.bfloat16)


def gate_of(pair, gain, bias, gate_w, out_gain, out_bias, out_w, per):
    rows, cols, width = pair.shape
    half = cols // 2 // PAD
    vec = pl.BlockSpec((1, width), lambda b: (0, 0))
    mat = pl.BlockSpec((width, width), lambda b: (0, 0))
    return pl.pallas_call(
        functools.partial(gate_kernel, per),
        grid=(1,),
        in_specs=[
            pl.BlockSpec((rows, PAD, width), lambda b: (0, 0, 0)),
            pl.BlockSpec((rows, PAD, width), lambda b: (0, half, 0)),
            vec,
            vec,
            mat,
            vec,
            vec,
            mat,
        ],
        out_specs=[pl.BlockSpec((2 * JD, rows, width), lambda b: (0, 0, 0)), mat, mat, mat],
        out_shape=[
            jax.ShapeDtypeStruct((2 * JD, rows, width), jnp.float32),
            jax.ShapeDtypeStruct((width, width), jnp.float32),
            jax.ShapeDtypeStruct((width, width), jnp.float32),
            jax.ShapeDtypeStruct((width, width), jnp.bfloat16),
        ],
        scratch_shapes=[
            pltpu.VMEM((2, rows * PAD, width), jnp.float32),
            pltpu.VMEM((width, width), jnp.float32),
        ],
        compiler_params=pltpu.CompilerParams(vmem_limit_bytes=32 << 20),
    )(pair, pair, gain, bias, gate_w, out_gain, out_bias, out_w)


def update_kernel(per, slab, gate, scale, shift, weight, out, plain):
    hidden = weight.shape[0]
    rows = gate.shape[1]
    peers = hidden // per
    plain[...] = slab[...].astype(jnp.float32)
    for r in range(JD):
        values = jnp.concatenate(
            [plain[pl.ds(r * per + j, peers, stride=JD * per), :] for j in range(per)], axis=0
        )
        centre = jnp.mean(values, axis=0, keepdims=True)
        centred = values - centre
        spread_sq = jnp.mean(centred * centred, axis=0, keepdims=True)
        normed = centred * lax.rsqrt(spread_sq + epsilon) * scale[...] + shift[...]
        update = dot(normed.astype(jnp.bfloat16), weight[...], (((0,), (0,)), ((), ())))
        for h in range(2):
            m = h * JD + r
            out[m] = (gate[m] * update[h * rows : (h + 1) * rows]).astype(jnp.bfloat16)


def update_of(slab, gate, scale, shift, weight, per):
    vmem = pl.BlockSpec(memory_space=pltpu.VMEM)
    return pl.pallas_call(
        functools.partial(update_kernel, per),
        in_specs=[vmem] * 5,
        out_specs=vmem,
        out_shape=jax.ShapeDtypeStruct(gate.shape, jnp.bfloat16),
        scratch_shapes=[pltpu.VMEM(slab.shape, jnp.float32)],
        compiler_params=pltpu.CompilerParams(vmem_limit_bytes=32 << 20),
    )(slab, gate, scale, shift, weight)


def on_device(
    pair_repr,
    chain_lengths,
    norm_gain,
    norm_bias,
    left_gate,
    left_value,
    right_gate,
    right_value,
    out_gain,
    out_bias,
    out_weight,
    gate_weight,
):
    rows, cols, width = pair_repr.shape
    hidden = left_gate.shape[1]
    groups = lax.axis_size("yh")
    chans = lax.axis_size("z") * lax.axis_size("yl")
    ring = lax.axis_size(RING)
    residues = rows * groups * ring * lax.axis_size("core")
    slot_size = residues // chain_lengths.shape[0]
    gain = norm_gain.reshape(1, width)
    bias = norm_bias.reshape(1, width)
    peers = chans * groups
    per = hidden // peers
    message = (peers, JD, per, cols)
    right = project_right(
        pair_repr, chain_lengths, gain, bias, right_gate, right_value, slot_size, per
    )
    right = lax.all_to_all(right.reshape(message), SPREAD, 0, 0, tiled=True)
    left = project_left(
        pair_repr, chain_lengths, gain, bias, left_gate, left_value, slot_size
    )
    left = lax.all_to_all(left, SPREAD, 0, 0, tiled=True)
    own = [right] + [
        lax.ppermute(right, RING, [(n, (n + d) % ring) for n in range(ring)])
        for d in range(1, ring)
    ]
    other = [lax.ppermute(part, "core", [(0, 1), (1, 0)]) for part in own]
    gate, scale, shift, weight = gate_of(
        pair_repr,
        gain,
        bias,
        gate_weight,
        out_gain.reshape(1, hidden),
        out_bias.reshape(1, hidden),
        out_weight,
        per,
    )
    gate, own[0] = lax.optimization_barrier((gate, own[0]))
    band = (chans, groups * JD * per, cols)
    product = product_of(
        left.reshape(chans, groups, per, rows, cols),
        [part.reshape(band) for part in own],
        [part.reshape(band) for part in other],
    )
    slab = lax.all_to_all(
        product.reshape(peers, JD, per, 2 * rows), SPREAD, 0, 0, tiled=True
    )
    update = update_of(slab.reshape(hidden * JD, 2 * rows), gate, scale, shift, weight, per)
    return jnp.transpose(update, (1, 0, 2))


def solution(mesh):
    names = tuple(name for name, _ in AXES)
    sizes = tuple(size for _, size in AXES)
    fine = Mesh(mesh.devices.reshape(sizes), names)
    split = P(names[:3], names[3:], None)
    return jax.shard_map(
        on_device,
        mesh=fine,
        in_specs=(split,) + (P(),) * 11,
        out_specs=split,
        check_vma=False,
    )
```

time: 129 us -> 126 us (0.977)
  the two profiles are of different devices: /device:TPU:4 before, /device:TPU:1 now
where the time goes in v6:
time: 126 us; the launch traced here: 124 us
  starting transfers between devices  49.5 us (39%)
  waiting for transfers between devices  29.1 us (23%)
  blocking collectives  28.5 us (23%)
  Pallas kernels  14.7 us (12%)
  local copies, waits for them, and re-layouts  1.7 us (1%)
    all_to_all x1, blocking collectives, on_device(): lax.all_to_all(product.reshape(peers, JD, per, 2 * rows), SPREAD, 0, 0, t...  28.5 us
    all_to_all x1, starting transfers between devices, on_device(): right = lax.all_to_all(right.reshape(message), SPREAD, 0, 0, tiled=True)  17.4 us
    all_to_all x1, waiting for transfers between devices, on_device(): left = lax.all_to_all(left, SPREAD, 0, 0, tiled=True)  15.2 us
    ppermute x4, starting transfers between devices, on_device(): other = [lax.ppermute(part, 'core', [(0, 1), (1, 0)]) for part in own]  14.7 us
    ppermute x3, starting transfers between devices, on_device(): lax.ppermute(right, RING, [(n, (n + d) % ring) for n in range(ring)])  10.5 us
    all_to_all x1, waiting for transfers between devices, on_device(): right = lax.all_to_all(right.reshape(message), SPREAD, 0, 0, tiled=True)  9.71 us
    all_to_all x1, starting transfers between devices, on_device(): left = lax.all_to_all(left, SPREAD, 0, 0, tiled=True)  6.88 us
    pallas_call x1, Pallas kernels, project_left(): pl.pallas_call(functools.partial(left_kernel, rows, slot_size, where), gr...  5.34 us
  transfers between devices with their start and end apart: 9, of which 3 were waited for; matrix products, arithmetic and copies ran while one was open for 0% of the time, Pallas kernels for 5%

profile of v6, /device:TPU:1, one launch (start us, length us, event | category | flops | bytes accessed | tf_op | source)
XLA Modules:
  0.0 123.9 jit_solution(9288667457270914322)
XLA Ops:
  0.0 0.0 copy-start.7
  0.0 0.0 copy-start
  0.0 0.0 copy-start.5
  0.0 0.0 copy-start.6
  0.0 0.0 copy-start.1
  0.0 0.0 copy-start.2
  0.0 2.7 %shard_map.120 = bf16[1664,128]{1,0:T(8,128)(2,1)} custom-call(s32[8]{0:T(128)} %lengths_h.1, bf16[64,128,128]{2,1,0:T(8,128)(2,1)} %pair_h.1, f32[1,128]{1,0:T(1,128)} %bitcast.19, f32[1,128]{1,0:T(1,128)} %bitcast.22, bf16[128,128]{1,0:T(8,128)(2,1)} %gate_h.1, bf16[128,128]{1,0:T(8,128)(2,1)} %value_h.1), custom_call_target="tpu_custom_call" | custom-call | tf_op jit(solution)/shard_map/pallas_call | solution.py:156
  2.7 17.4 %all-to-all-start.1 = ((bf16[64,13,2,128]{3,2,1,0:T(2,128)(2,1)}), bf16[64,13,2,128]{3,2,1,0:T(2,128)(2,1)}, u32[]{:S(2)}, u32[]{:S(2)}) async-start(bf16[64,13,2,128]{3,2,1,0:T(2,128)(2,1)} %bitcast.5), calls=%async_computation.1 | async-start | bytes 851968 | tf_op jit(solution)/shard_map/all_to_all | solution.py:435
  20.1 0.0 copy-done.7
  20.1 0.0 copy-done
  20.1 0.0 copy-done.5
  20.2 0.0 copy-done.6
  20.2 0.0 copy-done.1
  20.2 0.0 copy-done.2
  20.2 5.3 %shard_map.118 = bf16[128,64,128]{2,1,0:T(8,128)(2,1)} custom-call(s32[8]{0:T(128)S(1)} %copy-done.7, bf16[64,128,128]{2,1,0:T(8,128)(2,1)S(1)} %copy-done, f32[1,128]{1,0:T(1,128)S(1)} %bitcast.20, f32[1,128]{1,0:T(1,128)S(1)} %bitcast.23, bf16[128,128]{1,0:T(8,128)(2,1)S(1)} %copy-done.1, bf16[128,128]{1,0:T(8,128)(2,1)S(1)} %copy-done.2), custom_call_target="tpu_custom_call" | custom-call | flops 536870912 | bytes 4194304 | tf_op jit(solution)/shard_map/pallas_call | solution.py:202
  25.5 0.0 copy-start.3
  25.5 0.0 copy-start.4
  25.5 0.0 copy-start.8
  25.5 0.0 copy-start.9
  25.5 9.7 %all-to-all-done.1 = bf16[64,13,2,128]{3,2,1,0:T(2,128)(2,1)} async-done(((bf16[64,13,2,128]{3,2,1,0:T(2,128)(2,1)}), bf16[64,13,2,128]{3,2,1,0:T(2,128)(2,1)}, u32[]{:S(2)}, u32[]{:S(2)}) %all-to-all-start.1) | async-done | bytes 426016 | tf_op jit(solution)/shard_map/all_to_all | solution.py:435
  35.2 6.9 %all-to-all-start = ((bf16[128,64,128]{2,1,0:T(8,128)(2,1)}), bf16[128,64,128]{2,1,0:T(8,128)(2,1)}, u32[]{:S(2)}, u32[]{:S(2)}) async-start(bf16[128,64,128]{2,1,0:T(8,128)(2,1)} %shard_map.118), calls=%async_computation | async-start | bytes 4194304 | tf_op jit(solution)/shard_map/all_to_all | solution.py:439
  42.1 3.1 %collective-permute-start = (bf16[64,13,2,128]{3,2,1,0:T(2,128)(2,1)}, bf16[64,13,2,128]{3,2,1,0:T(2,128)(2,1)S(1)}, u32[]{:S(2)}, u32[]{:S(2)}) collective-permute-start(bf16[64,13,2,128]{3,2,1,0:T(2,128)(2,1)} %all-to-all-done.1), channel_id=1, source_target_pairs={{0,32},{32,64},{64,96},{96,0},{1,33},{33,65},{65,97},{97,1},{2,34}... | collective-permute-start | bytes 1277960 | tf_op jit(solution)/shard_map/ppermute | solution.py:441
  45.3 4.4 %collective-permute-start.1 = (bf16[64,13,2,128]{3,2,1,0:T(2,128)(2,1)}, bf16[64,13,2,128]{3,2,1,0:T(2,128)(2,1)S(1)}, u32[]{:S(2)}, u32[]{:S(2)}) collective-permute-start(bf16[64,13,2,128]{3,2,1,0:T(2,128)(2,1)} %all-to-all-done.1), channel_id=1, source_target_pairs={{0,64},{32,96},{64,0},{96,32},{1,65},{33,97},{65,1},{97,33},{2,66}... | collective-permute-start | bytes 1277960 | tf_op jit(solution)/shard_map/ppermute | solution.py:441
  49.6 3.1 %collective-permute-start.2 = (bf16[64,13,2,128]{3,2,1,0:T(2,128)(2,1)}, bf16[64,13,2,128]{3,2,1,0:T(2,128)(2,1)S(1)}, u32[]{:S(2)}, u32[]{:S(2)}) collective-permute-start(bf16[64,13,2,128]{3,2,1,0:T(2,128)(2,1)} %all-to-all-done.1), channel_id=1, source_target_pairs={{0,96},{32,0},{64,32},{96,64},{1,97},{33,1},{65,33},{97,65},{2,98}... | collective-permute-start | bytes 1277960 | tf_op jit(solution)/shard_map/ppermute | solution.py:441
  52.7 4.6 %collective-permute-start.3 = (bf16[64,13,2,128]{3,2,1,0:T(2,128)(2,1)}, bf16[64,13,2,128]{3,2,1,0:T(2,128)(2,1)S(1)}, u32[]{:S(2)}, u32[]{:S(2)}) collective-permute-start(bf16[64,13,2,128]{3,2,1,0:T(2,128)(2,1)} %all-to-all-done.1), channel_id=1, source_target_pairs={{0,16},{16,0},{1,17},{17,1},{2,18},{18,2},{3,19},{19,3},{4,20},{20... | collective-permute-start | bytes 1277960 | tf_op jit(solution)/shard_map/ppermute | solution.py:444
  57.3 0.0 collective-permute-done
  57.3 0.0 copy-start.10
  57.3 3.6 %collective-permute-start.4 = (bf16[64,13,2,128]{3,2,1,0:T(2,128)(2,1)S(1)}, bf16[64,13,2,128]{3,2,1,0:T(2,128)(2,1)S(1)}, u32[]{:S(2)}, u32[]{:S(2)}) collective-permute-start(bf16[64,13,2,128]{3,2,1,0:T(2,128)(2,1)S(1)} %collective-permute-done), channel_id=1, source_target_pairs={{0,16},{16,0},{1,17},{17,1},{2,18},{18,2},{3,19},{19,3},{4,20},{20... | collective-permute-start | bytes 1277960 | tf_op jit(solution)/shard_map/ppermute | solution.py:444
  61.0 4.2 %collective-permute-done.1 = bf16[64,13,2,128]{3,2,1,0:T(2,128)(2,1)S(1)} collective-permute-done((bf16[64,13,2,128]{3,2,1,0:T(2,128)(2,1)}, bf16[64,13,2,128]{3,2,1,0:T(2,128)(2,1)S(1)}, u32[]{:S(2)}, u32[]{:S(2)}) %collective-permute-start.1) | collective-permute-done | bytes 426016 | tf_op jit(solution)/shard_map/ppermute | solution.py:441
  65.2 0.0 copy-start.11
  65.2 4.5 %collective-permute-start.5 = (bf16[64,13,2,128]{3,2,1,0:T(2,128)(2,1)S(1)}, bf16[64,13,2,128]{3,2,1,0:T(2,128)(2,1)S(1)}, u32[]{:S(2)}, u32[]{:S(2)}) collective-permute-start(bf16[64,13,2,128]{3,2,1,0:T(2,128)(2,1)S(1)} %collective-permute-done.1), channel_id=1, source_target_pairs={{0,16},{16,0},{1,17},{17,1},{2,18},{18,2},{3,19},{19,3},{4,20},{20... | collective-permute-start | bytes 1277960 | tf_op jit(solution)/shard_map/ppermute | solution.py:444
  69.7 0.0 collective-permute-done.2
  69.7 0.0 copy-start.12
  69.7 1.9 %collective-permute-start.6 = (bf16[64,13,2,128]{3,2,1,0:T(2,128)(2,1)S(1)}, bf16[64,13,2,128]{3,2,1,0:T(2,128)(2,1)}, u32[]{:S(2)}, u32[]{:S(2)}) collective-permute-start(bf16[64,13,2,128]{3,2,1,0:T(2,128)(2,1)S(1)} %collective-permute-done.2), channel_id=1, source_target_pairs={{0,16},{16,0},{1,17},{17,1},{2,18},{18,2},{3,19},{19,3},{4,20},{20... | collective-permute-start | bytes 1277960 | tf_op jit(solution)/shard_map/ppermute | solution.py:444
  71.7 0.0 copy-done.3
  71.7 0.0 copy-done.4
  71.7 0.0 copy-done.8
  71.7 0.0 copy-done.9
  71.7 1.0 shard_map.119
  72.7 0.0 copy-done.10
  72.7 0.0 copy-done.11
  72.7 0.0 copy-done.12
  72.7 0.0 collective-permute-done.3
  72.7 0.0 copy-start.13
  72.7 0.0 collective-permute-done.4
  72.7 0.0 copy-start.14
  72.8 0.0 collective-permute-done.5
  72.8 0.7 copy-done.13
  73.5 0.2 copy-done.14
  73.7 0.0 copy-start.15
  73.7 0.8 copy-done.15
  74.4 0.0 collective-permute-done.6
  74.4 15.2 %all-to-all-done = bf16[128,64,128]{2,1,0:T(8,128)(2,1)} async-done(((bf16[128,64,128]{2,1,0:T(8,128)(2,1)}), bf16[128,64,128]{2,1,0:T(8,128)(2,1)}, u32[]{:S(2)}, u32[]{:S(2)}) %all-to-all-start) | async-done | bytes 2097184 | tf_op jit(solution)/shard_map/all_to_all | solution.py:439
  89.6 4.4 %shard_map.121 = bf16[16,104,128]{2,1,0:T(8,128)(2,1)S(1)} custom-call(bf16[16,4,2,64,128]{4,3,2,1,0:T(8,128)(2,1)} %bitcast.2.refs_0_, bf16[16,104,128]{2,1,0:T(8,128)(2,1)} %bitcast.6.refs_1_, bf16[16,104,128]{2,1,0:T(8,128)(2,1)} %bitcast.27, bf16[16,104,128]{2,1,0:T(8,128)(2,1)} %bitcast.28, bf16[16,104,128]{2,1,0:T(8,128)(2,1)} %bitcast.29, ...), custom_call_target="tpu_custom_call" | custom-call | tf_op jit(solution)/shard_map/pallas_call | solution.py:294
  94.1 28.5 %all_to_all.15 = bf16[64,13,2,128]{3,2,1,0:T(2,128)(2,1)S(1)} all-to-all(bf16[64,13,2,128]{3,2,1,0:T(2,128)(2,1)S(1)} %bitcast.17), channel_id=1, replica_groups=mesh['yh'=4,'x'=4,'core'=2,'z'=8,'yl'=2] {'yl','z','yh'}, dimensions={0} | all-to-all | bytes 851968 | tf_op jit(solution)/shard_map/all_to_all | solution.py:462
  122.6 1.3 %shard_map.122 = bf16[26,64,128]{2,1,0:T(8,128)(2,1)} custom-call(bf16[1664,128]{1,0:T(8,128)(2,1)S(1)} %bitcast.18, f32[26,64,128]{2,1,0:T(8,128)S(1)} %get-tuple-element.13.gate, f32[128,128]{1,0:T(8,128)S(1)} %get-tuple-element.14.scale, f32[128,128]{1,0:T(8,128)S(1)} %get-tuple-element.15.shift, bf16[128,128]{1,0:T(8,128)(2,1)S(1)} %get-tuple-element.16.weight), custom_call_target="tpu_custom_call" | custom-call | tf_op jit(solution)/shard_map/pallas_call | solution.py:396
Async XLA Ops:
  0.0 20.1 %copy-start.7 = (s32[8]{0:T(128)S(1)}, s32[8]{0:T(128)}, u32[]{:S(2)}) copy-start(s32[8]{0:T(128)} %lengths_h.1) | copy-start | bytes 100
  0.0 20.1 %copy-start = (bf16[64,128,128]{2,1,0:T(8,128)(2,1)S(1)}, bf16[64,128,128]{2,1,0:T(8,128)(2,1)}, u32[]{:S(2)}) copy-start(bf16[64,128,128]{2,1,0:T(8,128)(2,1)} %pair_h.1) | copy-start | bytes 6291460
  0.0 20.1 %copy-start.5 = (f32[128]{0:T(128)S(1)}, f32[128]{0:T(128)}, u32[]{:S(2)}) copy-start(f32[128]{0:T(128)} %param.14) | copy-start | bytes 1540
  0.0 20.1 %copy-start.6 = (f32[128]{0:T(128)S(1)}, f32[128]{0:T(128)}, u32[]{:S(2)}) copy-start(f32[128]{0:T(128)} %param.15) | copy-start | bytes 1540
  0.0 20.1 %copy-start.1 = (bf16[128,128]{1,0:T(8,128)(2,1)S(1)}, bf16[128,128]{1,0:T(8,128)(2,1)}, u32[]{:S(2)}) copy-start(bf16[128,128]{1,0:T(8,128)(2,1)} %gate_w.2) | copy-start | bytes 98308
  0.0 20.1 %copy-start.2 = (bf16[128,128]{1,0:T(8,128)(2,1)S(1)}, bf16[128,128]{1,0:T(8,128)(2,1)}, u32[]{:S(2)}) copy-start(bf16[128,128]{1,0:T(8,128)(2,1)} %value_w.1) | copy-start | bytes 98308
  2.7 32.5 %all-to-all-start.1 = ((bf16[64,13,2,128]{3,2,1,0:T(2,128)(2,1)}), bf16[64,13,2,128]{3,2,1,0:T(2,128)(2,1)}, u32[]{:S(2)}, u32[]{:S(2)}) async-start(bf16[64,13,2,128]{3,2,1,0:T(2,128)(2,1)} %bitcast.5), calls=%async_computation.1 | async-start | bytes 851968 | tf_op jit(solution)/shard_map/all_to_all | solution.py:435
  25.5 46.1 %copy-start.3 = (bf16[128,128]{1,0:T(8,128)(2,1)S(1)}, bf16[128,128]{1,0:T(8,128)(2,1)}, u32[]{:S(2)}) copy-start(bf16[128,128]{1,0:T(8,128)(2,1)} %gate_w.3) | copy-start | bytes 98308
  25.5 46.1 %copy-start.4 = (bf16[128,128]{1,0:T(8,128)(2,1)S(1)}, bf16[128,128]{1,0:T(8,128)(2,1)}, u32[]{:S(2)}) copy-start(bf16[128,128]{1,0:T(8,128)(2,1)} %out_w.1) | copy-start | bytes 98308
  25.5 46.1 %copy-start.8 = (f32[128]{0:T(128)S(1)}, f32[128]{0:T(128)}, u32[]{:S(2)}) copy-start(f32[128]{0:T(128)} %param.20) | copy-start | bytes 1540
  25.5 46.2 %copy-start.9 = (f32[128]{0:T(128)S(1)}, f32[128]{0:T(128)}, u32[]{:S(2)}) copy-start(f32[128]{0:T(128)} %param.21) | copy-start | bytes 1540
  35.2 54.4 %all-to-all-start = ((bf16[128,64,128]{2,1,0:T(8,128)(2,1)}), bf16[128,64,128]{2,1,0:T(8,128)(2,1)}, u32[]{:S(2)}, u32[]{:S(2)}) async-start(bf16[128,64,128]{2,1,0:T(8,128)(2,1)} %shard_map.118), calls=%async_computation | async-start | bytes 4194304 | tf_op jit(solution)/shard_map/all_to_all | solution.py:439
  42.1 15.2 %collective-permute-start = (bf16[64,13,2,128]{3,2,1,0:T(2,128)(2,1)}, bf16[64,13,2,128]{3,2,1,0:T(2,128)(2,1)S(1)}, u32[]{:S(2)}, u32[]{:S(2)}) collective-permute-start(bf16[64,13,2,128]{3,2,1,0:T(2,128)(2,1)} %all-to-all-done.1), channel_id=1, source_target_pairs={{0,32},{32,64},{64,96},{96,0},{1,33},{33,65},{65,97},{97,1},{2,34}... | collective-permute-start | bytes 1277960 | tf_op jit(solution)/shard_map/ppermute | solution.py:441
  45.3 19.9 %collective-permute-start.1 = (bf16[64,13,2,128]{3,2,1,0:T(2,128)(2,1)}, bf16[64,13,2,128]{3,2,1,0:T(2,128)(2,1)S(1)}, u32[]{:S(2)}, u32[]{:S(2)}) collective-permute-start(bf16[64,13,2,128]{3,2,1,0:T(2,128)(2,1)} %all-to-all-done.1), channel_id=1, source_target_pairs={{0,64},{32,96},{64,0},{96,32},{1,65},{33,97},{65,1},{97,33},{2,66}... | collective-permute-start | bytes 1277960 | tf_op jit(solution)/shard_map/ppermute | solution.py:441
  49.6 20.1 %collective-permute-start.2 = (bf16[64,13,2,128]{3,2,1,0:T(2,128)(2,1)}, bf16[64,13,2,128]{3,2,1,0:T(2,128)(2,1)S(1)}, u32[]{:S(2)}, u32[]{:S(2)}) collective-permute-start(bf16[64,13,2,128]{3,2,1,0:T(2,128)(2,1)} %all-to-all-done.1), channel_id=1, source_target_pairs={{0,96},{32,0},{64,32},{96,64},{1,97},{33,1},{65,33},{97,65},{2,98}... | collective-permute-start | bytes 1277960 | tf_op jit(solution)/shard_map/ppermute | solution.py:441
  52.7 20.0 %collective-permute-start.3 = (bf16[64,13,2,128]{3,2,1,0:T(2,128)(2,1)}, bf16[64,13,2,128]{3,2,1,0:T(2,128)(2,1)S(1)}, u32[]{:S(2)}, u32[]{:S(2)}) collective-permute-start(bf16[64,13,2,128]{3,2,1,0:T(2,128)(2,1)} %all-to-all-done.1), channel_id=1, source_target_pairs={{0,16},{16,0},{1,17},{17,1},{2,18},{18,2},{3,19},{19,3},{4,20},{20... | collective-permute-start | bytes 1277960 | tf_op jit(solution)/shard_map/ppermute | solution.py:444
  57.3 15.4 %copy-start.10 = (bf16[64,13,2,128]{3,2,1,0:T(2,128)(2,1)}, bf16[64,13,2,128]{3,2,1,0:T(2,128)(2,1)S(1)}, u32[]{:S(2)}) copy-start(bf16[64,13,2,128]{3,2,1,0:T(2,128)(2,1)S(1)} %collective-permute-done) | copy-start | bytes 1277956
  57.3 15.4 %collective-permute-start.4 = (bf16[64,13,2,128]{3,2,1,0:T(2,128)(2,1)S(1)}, bf16[64,13,2,128]{3,2,1,0:T(2,128)(2,1)S(1)}, u32[]{:S(2)}, u32[]{:S(2)}) collective-permute-start(bf16[64,13,2,128]{3,2,1,0:T(2,128)(2,1)S(1)} %collective-permute-done), channel_id=1, source_target_pairs={{0,16},{16,0},{1,17},{17,1},{2,18},{18,2},{3,19},{19,3},{4,20},{20... | collective-permute-start | bytes 1277960 | tf_op jit(solution)/shard_map/ppermute | solution.py:444
  65.2 7.5 %copy-start.11 = (bf16[64,13,2,128]{3,2,1,0:T(2,128)(2,1)}, bf16[64,13,2,128]{3,2,1,0:T(2,128)(2,1)S(1)}, u32[]{:S(2)}) copy-start(bf16[64,13,2,128]{3,2,1,0:T(2,128)(2,1)S(1)} %collective-permute-done.1) | copy-start | bytes 1277956
  65.2 7.6 %collective-permute-start.5 = (bf16[64,13,2,128]{3,2,1,0:T(2,128)(2,1)S(1)}, bf16[64,13,2,128]{3,2,1,0:T(2,128)(2,1)S(1)}, u32[]{:S(2)}, u32[]{:S(2)}) collective-permute-start(bf16[64,13,2,128]{3,2,1,0:T(2,128)(2,1)S(1)} %collective-permute-done.1), channel_id=1, source_target_pairs={{0,16},{16,0},{1,17},{17,1},{2,18},{18,2},{3,19},{19,3},{4,20},{20... | collective-permute-start | bytes 1277960 | tf_op jit(solution)/shard_map/ppermute | solution.py:444
  69.7 3.0 %copy-start.12 = (bf16[64,13,2,128]{3,2,1,0:T(2,128)(2,1)}, bf16[64,13,2,128]{3,2,1,0:T(2,128)(2,1)S(1)}, u32[]{:S(2)}) copy-start(bf16[64,13,2,128]{3,2,1,0:T(2,128)(2,1)S(1)} %collective-permute-done.2) | copy-start | bytes 1277956
  69.7 4.7 %collective-permute-start.6 = (bf16[64,13,2,128]{3,2,1,0:T(2,128)(2,1)S(1)}, bf16[64,13,2,128]{3,2,1,0:T(2,128)(2,1)}, u32[]{:S(2)}, u32[]{:S(2)}) collective-permute-start(bf16[64,13,2,128]{3,2,1,0:T(2,128)(2,1)S(1)} %collective-permute-done.2), channel_id=1, source_target_pairs={{0,16},{16,0},{1,17},{17,1},{2,18},{18,2},{3,19},{19,3},{4,20},{20... | collective-permute-start | bytes 1277960 | tf_op jit(solution)/shard_map/ppermute | solution.py:444
  72.7 0.8 copy-start.13
  72.7 0.9 copy-start.14
  73.7 0.8 copy-start.15
